TPU v7x, 256 devices: a whole 4x4x8 slice. The times are simulated.
256 devices in a mesh: blk: 16 (over x_hi, y, core), rep: 16 (over x_lo, z).
Axes of the slice: x: 4 (x_hi: 2, x_lo: 2; x = x_hi * 2 + x_lo), y: 4, z: 8, core: 2. Of those that a mesh axis runs over, the one named last changes fastest.
Arguments:
- out_grad: bfloat16 [49152, 256], P(('blk', 'rep')), may hold values from -0.59765625 to 0.59765625
- pre_act: bfloat16 [49152, 256], P(('blk', 'rep')), may hold values from -6 to 6
- features: bfloat16 [49152, 256], P(('blk', 'rep')), may hold values from -0.02734375 to 0.02734375
- weight: bfloat16 [256, 256], replicated, may hold values from -0.375 to 0.375
- degrees: int32 [49152], P(('blk', 'rep')), may hold values from 1 to 255
- tiles: bfloat16 [4096, 24, 128, 128], P(('blk', 'rep')), may hold values from 0 to 1, as said below
- tile_rows: int32 [4096, 24], P(('blk', 'rep')), may hold values from 0 to 23, as said below
- tile_cols: int32 [4096, 24], P(('blk', 'rep')), may hold values from 0 to 23, as said below
Outputs:
- input_grad: bfloat16 [49152, 256], P(('blk', 'rep'))
- weight_grad: float32 [256, 256], replicated
Inputs may be any that keep to these rules, and one draw needn't show every extreme that they name: `tiles`: entries are 0 or 1. For each device and source row group the slots holding a nonzero tile come first, 1 to 24 of them; all 24 slots are nonzero in at least two source row groups of every device; the other slots are all zero. Within one row group b and one source row group h, the nonzero slots of all 16 devices of b hold distinct (tile_rows, tile_cols) positions; all-zero slots hold 0. `tile_cols`: All-zero slots hold 0.
All inputs are finite; a program needn't handle non-finite values.
Results may differ from a plain program's by a relative error of at most 0.0053.
Values may be sent and summed in bfloat16 or wider, within the bound.
No kernel may reach another device: no remote copies, remote signals or barrier semaphores. Data moves between devices by JAX's collectives and lax.ppermute only.
A program may use at most 128 MiB of HBM per device.

v0:
```python
import jax
import jax.numpy as jnp
from jax import lax
from jax.sharding import PartitionSpec as P


def shifted(value, axis, steps):
    count = lax.axis_size(axis)
    pairs = [(source, (source + steps) % count) for source in range(count)]
    return lax.ppermute(value, axis, pairs)


def body(out_grad, pre_act, features, weight, degrees, tiles, tile_rows, tile_cols):
    cycle = lax.axis_size("blk")
    own_group = lax.axis_index("blk")
    width = out_grad.shape[1]
    block = tiles.shape[2]
    inverse_root = lax.rsqrt(degrees.astype(jnp.float32))
    active = (pre_act > 0).astype(jnp.float32)
    scaled = (out_grad.astype(jnp.float32) * active * inverse_root[:, None]).astype(jnp.bfloat16)
    gathered_rows = lax.all_gather(scaled, "rep", axis=0, tiled=True)
    group_blocks = gathered_rows.shape[0] // block
    panel = gathered_rows.reshape(group_blocks, block, width)

    def add_batch(totals, part_rows, tile_set, row_set, col_set):
        picked = jnp.take(part_rows, row_set, axis=0)
        products = jnp.einsum("cji,cjf->cif", tile_set, picked, preferred_element_type=jnp.float32)
        return totals.at[col_set].add(products)

    def accumulate(totals, part_rows, source):
        tile_set = lax.dynamic_index_in_dim(tiles, source, 0, keepdims=False)
        row_set = lax.dynamic_index_in_dim(tile_rows, source, 0, keepdims=False)
        col_set = lax.dynamic_index_in_dim(tile_cols, source, 0, keepdims=False)
        result = add_batch(totals, part_rows, tile_set, row_set, col_set)
        return result

    def advance(current):
        return shifted(current, "blk", 1)

    empty_totals = jnp.zeros((group_blocks, block, width), jnp.float32)

    def turn_single(turn_number, carry):
        carry_totals, current = carry
        carry_totals = accumulate(carry_totals, current, (own_group - turn_number) % cycle)
        return (carry_totals, advance(current))

    totals, current = lax.fori_loop(0, cycle - 1, turn_single, (empty_totals, panel))
    totals = accumulate(totals, current, (own_group - (cycle - 1)) % cycle)
    summed = lax.psum_scatter(
        totals.reshape(group_blocks * block, width), "rep", scatter_dimension=0, tiled=True
    )
    propagated = (inverse_root[:, None] * summed).astype(jnp.bfloat16)
    input_grad = lax.dot_general(
        propagated, weight, (((1,), (1,)), ((), ())), preferred_element_type=jnp.float32
    ).astype(jnp.bfloat16)
    local_weight = lax.dot_general(
        features, propagated, (((0,), (0,)), ((), ())), preferred_element_type=jnp.float32
    )
    weight_grad = lax.psum(local_weight, ("blk", "rep"))
    return (input_grad, weight_grad)


def solution(mesh):
    placed = (
        P(("blk", "rep"), None),
        P(("blk", "rep"), None),
        P(("blk", "rep"), None),
        P(),
        P(("blk", "rep")),
        P(("blk", "rep"), None, None, None),
        P(("blk", "rep"), None),
        P(("blk", "rep"), None),
    )
    return jax.shard_map(
        body, mesh=mesh, in_specs=placed, out_specs=(P(("blk", "rep"), None), P()), check_vma=False
    )
```

profile of v0, /device:TPU:32, one launch (start us, length us, event | category | flops | bytes accessed | tf_op | source)
XLA Modules:
  0.0 828.7 jit_solution(11365679336427051718)
XLA Ops:
  11.1 71.3 %all-gather.2.cloned.1.call-done = bf16[3072,256]{1,0:T(8,128)(2,1)} async-done(((bf16[192,256]{1,0:T(8,128)(2,1)}), bf16[3072,256]{1,0:T(8,128)(2,1)}) %all-gather.2.cloned.1.call-update) | async-done | bytes 1572880 | tf_op jit(solution)/shard_map/all_gather | solution.py:21
  84.4 397.4 %while.17 = (s32[]{:T(128)}, f32[24,128,256]{2,1,0:T(8,128)}, bf16[24,128,256]{2,1,0:T(8,128)(2,1)}, s32[]{:T(128)}, s32[16,24]{1,0:T(8,128)}, /*index=5*/bf16[1...) while((s32[]{:T(128)}, f32[24,128,256]{2,1,0:T(8,128)}, ...), condition=%wide.region_2.4_spmd, body=%wide.region_0.3_spmd.sunk | while | flops 202900704 | bytes 27530252 | solution.py:47
  94.1 8.6 %scatter_fusion = f32[24,128,256]{2,1,0:T(8,128)} fusion(f32[24,128,256]{2,1,0:T(8,128)} %get-tuple-element.269, s32[24]{0:T(128)S(1)} %fusion.30, f32[24,128,256]{2,1,0:T(8,128)S(1)} %fusion.31), kind=kCustom, calls=%fused_computation.2.clone.1 | custom fusion | flops 786432 | bytes 9437280 | tf_op jit(solution)/shard_map/while/body/eval_jaxpr/scatter-add | solution.py:28
  102.7 8.2 collective-permute-done
  120.6 8.6 %scatter_fusion = f32[24,128,256]{2,1,0:T(8,128)} fusion(f32[24,128,256]{2,1,0:T(8,128)} %get-tuple-element.269, s32[24]{0:T(128)S(1)} %fusion.30, f32[24,128,256]{2,1,0:T(8,128)S(1)} %fusion.31), kind=kCustom, calls=%fused_computation.2.clone.1 | custom fusion | flops 786432 | bytes 9437280 | tf_op jit(solution)/shard_map/while/body/eval_jaxpr/scatter-add | solution.py:28
  129.2 8.2 collective-permute-done
  147.0 8.7 %scatter_fusion = f32[24,128,256]{2,1,0:T(8,128)} fusion(f32[24,128,256]{2,1,0:T(8,128)} %get-tuple-element.269, s32[24]{0:T(128)S(1)} %fusion.30, f32[24,128,256]{2,1,0:T(8,128)S(1)} %fusion.31), kind=kCustom, calls=%fused_computation.2.clone.1 | custom fusion | flops 786432 | bytes 9437280 | tf_op jit(solution)/shard_map/while/body/eval_jaxpr/scatter-add | solution.py:28
  155.7 8.1 collective-permute-done
  173.5 8.4 %scatter_fusion = f32[24,128,256]{2,1,0:T(8,128)} fusion(f32[24,128,256]{2,1,0:T(8,128)} %get-tuple-element.269, s32[24]{0:T(128)S(1)} %fusion.30, f32[24,128,256]{2,1,0:T(8,128)S(1)} %fusion.31), kind=kCustom, calls=%fused_computation.2.clone.1 | custom fusion | flops 786432 | bytes 9437280 | tf_op jit(solution)/shard_map/while/body/eval_jaxpr/scatter-add | solution.py:28
  182.0 8.4 %collective-permute-done = bf16[24,128,256]{2,1,0:T(8,128)(2,1)} collective-permute-done((bf16[24,128,256]{2,1,0:T(8,128)(2,1)}, bf16[24,128,256]{2,1,0:T(8,128)(2,1)}, u32[]{:S(2)}, u32[]{:S(2)}) %collective-permute-start) | collective-permute-done | bytes 1572896 | tf_op jit(solution)/shard_map/while/body/eval_jaxpr/ppermute | solution.py:10
  200.0 8.5 %scatter_fusion = f32[24,128,256]{2,1,0:T(8,128)} fusion(f32[24,128,256]{2,1,0:T(8,128)} %get-tuple-element.269, s32[24]{0:T(128)S(1)} %fusion.30, f32[24,128,256]{2,1,0:T(8,128)S(1)} %fusion.31), kind=kCustom, calls=%fused_computation.2.clone.1 | custom fusion | flops 786432 | bytes 9437280 | tf_op jit(solution)/shard_map/while/body/eval_jaxpr/scatter-add | solution.py:28
  208.5 8.3 %collective-permute-done = bf16[24,128,256]{2,1,0:T(8,128)(2,1)} collective-permute-done((bf16[24,128,256]{2,1,0:T(8,128)(2,1)}, bf16[24,128,256]{2,1,0:T(8,128)(2,1)}, u32[]{:S(2)}, u32[]{:S(2)}) %collective-permute-start) | collective-permute-done | bytes 1572896 | tf_op jit(solution)/shard_map/while/body/eval_jaxpr/ppermute | solution.py:10
  226.5 8.7 %scatter_fusion = f32[24,128,256]{2,1,0:T(8,128)} fusion(f32[24,128,256]{2,1,0:T(8,128)} %get-tuple-element.269, s32[24]{0:T(128)S(1)} %fusion.30, f32[24,128,256]{2,1,0:T(8,128)S(1)} %fusion.31), kind=kCustom, calls=%fused_computation.2.clone.1 | custom fusion | flops 786432 | bytes 9437280 | tf_op jit(solution)/shard_map/while/body/eval_jaxpr/scatter-add | solution.py:28
  235.3 8.1 collective-permute-done
  253.0 8.5 %scatter_fusion = f32[24,128,256]{2,1,0:T(8,128)} fusion(f32[24,128,256]{2,1,0:T(8,128)} %get-tuple-element.269, s32[24]{0:T(128)S(1)} %fusion.30, f32[24,128,256]{2,1,0:T(8,128)S(1)} %fusion.31), kind=kCustom, calls=%fused_computation.2.clone.1 | custom fusion | flops 786432 | bytes 9437280 | tf_op jit(solution)/shard_map/while/body/eval_jaxpr/scatter-add | solution.py:28
  261.5 8.3 collective-permute-done
  279.5 8.5 %scatter_fusion = f32[24,128,256]{2,1,0:T(8,128)} fusion(f32[24,128,256]{2,1,0:T(8,128)} %get-tuple-element.269, s32[24]{0:T(128)S(1)} %fusion.30, f32[24,128,256]{2,1,0:T(8,128)S(1)} %fusion.31), kind=kCustom, calls=%fused_computation.2.clone.1 | custom fusion | flops 786432 | bytes 9437280 | tf_op jit(solution)/shard_map/while/body/eval_jaxpr/scatter-add | solution.py:28
  288.0 8.4 %collective-permute-done = bf16[24,128,256]{2,1,0:T(8,128)(2,1)} collective-permute-done((bf16[24,128,256]{2,1,0:T(8,128)(2,1)}, bf16[24,128,256]{2,1,0:T(8,128)(2,1)}, u32[]{:S(2)}, u32[]{:S(2)}) %collective-permute-start) | collective-permute-done | bytes 1572896 | tf_op jit(solution)/shard_map/while/body/eval_jaxpr/ppermute | solution.py:10
  306.0 8.7 %scatter_fusion = f32[24,128,256]{2,1,0:T(8,128)} fusion(f32[24,128,256]{2,1,0:T(8,128)} %get-tuple-element.269, s32[24]{0:T(128)S(1)} %fusion.30, f32[24,128,256]{2,1,0:T(8,128)S(1)} %fusion.31), kind=kCustom, calls=%fused_computation.2.clone.1 | custom fusion | flops 786432 | bytes 9437280 | tf_op jit(solution)/shard_map/while/body/eval_jaxpr/scatter-add | solution.py:28
  314.7 8.1 collective-permute-done
  332.5 8.9 %scatter_fusion = f32[24,128,256]{2,1,0:T(8,128)} fusion(f32[24,128,256]{2,1,0:T(8,128)} %get-tuple-element.269, s32[24]{0:T(128)S(1)} %fusion.30, f32[24,128,256]{2,1,0:T(8,128)S(1)} %fusion.31), kind=kCustom, calls=%fused_computation.2.clone.1 | custom fusion | flops 786432 | bytes 9437280 | tf_op jit(solution)/shard_map/while/body/eval_jaxpr/scatter-add | solution.py:28
  359.0 8.8 %scatter_fusion = f32[24,128,256]{2,1,0:T(8,128)} fusion(f32[24,128,256]{2,1,0:T(8,128)} %get-tuple-element.269, s32[24]{0:T(128)S(1)} %fusion.30, f32[24,128,256]{2,1,0:T(8,128)S(1)} %fusion.31), kind=kCustom, calls=%fused_computation.2.clone.1 | custom fusion | flops 786432 | bytes 9437280 | tf_op jit(solution)/shard_map/while/body/eval_jaxpr/scatter-add | solution.py:28
  367.8 8.0 collective-permute-done
  385.5 8.6 %scatter_fusion = f32[24,128,256]{2,1,0:T(8,128)} fusion(f32[24,128,256]{2,1,0:T(8,128)} %get-tuple-element.269, s32[24]{0:T(128)S(1)} %fusion.30, f32[24,128,256]{2,1,0:T(8,128)S(1)} %fusion.31), kind=kCustom, calls=%fused_computation.2.clone.1 | custom fusion | flops 786432 | bytes 9437280 | tf_op jit(solution)/shard_map/while/body/eval_jaxpr/scatter-add | solution.py:28
  394.1 8.2 collective-permute-done
  412.0 8.5 %scatter_fusion = f32[24,128,256]{2,1,0:T(8,128)} fusion(f32[24,128,256]{2,1,0:T(8,128)} %get-tuple-element.269, s32[24]{0:T(128)S(1)} %fusion.30, f32[24,128,256]{2,1,0:T(8,128)S(1)} %fusion.31), kind=kCustom, calls=%fused_computation.2.clone.1 | custom fusion | flops 786432 | bytes 9437280 | tf_op jit(solution)/shard_map/while/body/eval_jaxpr/scatter-add | solution.py:28
  420.4 8.3 %collective-permute-done = bf16[24,128,256]{2,1,0:T(8,128)(2,1)} collective-permute-done((bf16[24,128,256]{2,1,0:T(8,128)(2,1)}, bf16[24,128,256]{2,1,0:T(8,128)(2,1)}, u32[]{:S(2)}, u32[]{:S(2)}) %collective-permute-start) | collective-permute-done | bytes 1572896 | tf_op jit(solution)/shard_map/while/body/eval_jaxpr/ppermute | solution.py:10
  438.4 8.9 %scatter_fusion = f32[24,128,256]{2,1,0:T(8,128)} fusion(f32[24,128,256]{2,1,0:T(8,128)} %get-tuple-element.269, s32[24]{0:T(128)S(1)} %fusion.30, f32[24,128,256]{2,1,0:T(8,128)S(1)} %fusion.31), kind=kCustom, calls=%fused_computation.2.clone.1 | custom fusion | flops 786432 | bytes 9437280 | tf_op jit(solution)/shard_map/while/body/eval_jaxpr/scatter-add | solution.py:28
  464.9 8.6 %scatter_fusion = f32[24,128,256]{2,1,0:T(8,128)} fusion(f32[24,128,256]{2,1,0:T(8,128)} %get-tuple-element.269, s32[24]{0:T(128)S(1)} %fusion.30, f32[24,128,256]{2,1,0:T(8,128)S(1)} %fusion.31), kind=kCustom, calls=%fused_computation.2.clone.1 | custom fusion | flops 786432 | bytes 9437280 | tf_op jit(solution)/shard_map/while/body/eval_jaxpr/scatter-add | solution.py:28
  473.5 8.2 collective-permute-done
  496.9 70.7 %reduce-scatter.2.cloned.1.call-done = f32[192,256]{1,0:T(8,128)} async-done(((f32[3072,256]{1,0:T(8,128)}), f32[192,256]{1,0:T(8,128)}) %reduce-scatter.2.cloned.1.call-update) | async-done | bytes 196624 | tf_op jit(solution)/shard_map/reduce_scatter | solution.py:49
  571.4 249.0 %all-reduce.2.cloned.1.call-done = f32[256,256]{0,1:T(8,128)} async-done(((f32[256,256]{0,1:T(8,128)}), f32[256,256]{0,1:T(8,128)}) %all-reduce.2.cloned.1.call-update) | async-done | bytes 262160 | tf_op jit(solution)/shard_map/psum | solution.py:59
  (133 shorter events, 187.4 us)
Async XLA Ops:
  7.2 562.4 %copy-start = (bf16[256,256]{1,0:T(8,128)(2,1)S(1)}, bf16[256,256]{1,0:T(8,128)(2,1)}, u32[]{:S(2)}) copy-start(bf16[256,256]{1,0:T(8,128)(2,1)} %param.15) | copy-start | bytes 393220
  7.2 75.2 %all-gather.2.cloned.1.call-start = ((), (), s32[]{:S(2)}) async-start(), calls=%async_computation.1 | async-start | bytes 1671168 | tf_op jit(solution)/shard_map/all_gather | solution.py:21
  9.6 558.0 %reduce-scatter.2.cloned.1.call-start = ((), (), s32[]{:S(2)}) async-start(), calls=%async_computation.2 | async-start | bytes 3342336 | tf_op jit(solution)/shard_map/reduce_scatter | solution.py:49
  87.1 23.8 %collective-permute-start = (bf16[24,128,256]{2,1,0:T(8,128)(2,1)}, bf16[24,128,256]{2,1,0:T(8,128)(2,1)}, u32[]{:S(2)}, u32[]{:S(2)}) collective-permute-start(bf16[24,128,256]{2,1,0:T(8,128)(2,1)} %copy.20), channel_id=1, source_target_pairs={{0,16},{16,32},{32,48},{48,64},{64,80},{80,96},{96,112},{112,128},... | collective-permute-start | bytes 4718600 | tf_op jit(solution)/shard_map/while/body/eval_jaxpr/ppermute | solution.py:10
  113.6 23.8 %collective-permute-start = (bf16[24,128,256]{2,1,0:T(8,128)(2,1)}, bf16[24,128,256]{2,1,0:T(8,128)(2,1)}, u32[]{:S(2)}, u32[]{:S(2)}) collective-permute-start(bf16[24,128,256]{2,1,0:T(8,128)(2,1)} %copy.20), channel_id=1, source_target_pairs={{0,16},{16,32},{32,48},{48,64},{64,80},{80,96},{96,112},{112,128},... | collective-permute-start | bytes 4718600 | tf_op jit(solution)/shard_map/while/body/eval_jaxpr/ppermute | solution.py:10
  140.1 23.8 %collective-permute-start = (bf16[24,128,256]{2,1,0:T(8,128)(2,1)}, bf16[24,128,256]{2,1,0:T(8,128)(2,1)}, u32[]{:S(2)}, u32[]{:S(2)}) collective-permute-start(bf16[24,128,256]{2,1,0:T(8,128)(2,1)} %copy.20), channel_id=1, source_target_pairs={{0,16},{16,32},{32,48},{48,64},{64,80},{80,96},{96,112},{112,128},... | collective-permute-start | bytes 4718600 | tf_op jit(solution)/shard_map/while/body/eval_jaxpr/ppermute | solution.py:10
  166.6 23.8 %collective-permute-start = (bf16[24,128,256]{2,1,0:T(8,128)(2,1)}, bf16[24,128,256]{2,1,0:T(8,128)(2,1)}, u32[]{:S(2)}, u32[]{:S(2)}) collective-permute-start(bf16[24,128,256]{2,1,0:T(8,128)(2,1)} %copy.20), channel_id=1, source_target_pairs={{0,16},{16,32},{32,48},{48,64},{64,80},{80,96},{96,112},{112,128},... | collective-permute-start | bytes 4718600 | tf_op jit(solution)/shard_map/while/body/eval_jaxpr/ppermute | solution.py:10
  193.1 23.8 %collective-permute-start = (bf16[24,128,256]{2,1,0:T(8,128)(2,1)}, bf16[24,128,256]{2,1,0:T(8,128)(2,1)}, u32[]{:S(2)}, u32[]{:S(2)}) collective-permute-start(bf16[24,128,256]{2,1,0:T(8,128)(2,1)} %copy.20), channel_id=1, source_target_pairs={{0,16},{16,32},{32,48},{48,64},{64,80},{80,96},{96,112},{112,128},... | collective-permute-start | bytes 4718600 | tf_op jit(solution)/shard_map/while/body/eval_jaxpr/ppermute | solution.py:10
  219.6 23.8 %collective-permute-start = (bf16[24,128,256]{2,1,0:T(8,128)(2,1)}, bf16[24,128,256]{2,1,0:T(8,128)(2,1)}, u32[]{:S(2)}, u32[]{:S(2)}) collective-permute-start(bf16[24,128,256]{2,1,0:T(8,128)(2,1)} %copy.20), channel_id=1, source_target_pairs={{0,16},{16,32},{32,48},{48,64},{64,80},{80,96},{96,112},{112,128},... | collective-permute-start | bytes 4718600 | tf_op jit(solution)/shard_map/while/body/eval_jaxpr/ppermute | solution.py:10
  246.0 23.8 %collective-permute-start = (bf16[24,128,256]{2,1,0:T(8,128)(2,1)}, bf16[24,128,256]{2,1,0:T(8,128)(2,1)}, u32[]{:S(2)}, u32[]{:S(2)}) collective-permute-start(bf16[24,128,256]{2,1,0:T(8,128)(2,1)} %copy.20), channel_id=1, source_target_pairs={{0,16},{16,32},{32,48},{48,64},{64,80},{80,96},{96,112},{112,128},... | collective-permute-start | bytes 4718600 | tf_op jit(solution)/shard_map/while/body/eval_jaxpr/ppermute | solution.py:10
  272.5 23.8 %collective-permute-start = (bf16[24,128,256]{2,1,0:T(8,128)(2,1)}, bf16[24,128,256]{2,1,0:T(8,128)(2,1)}, u32[]{:S(2)}, u32[]{:S(2)}) collective-permute-start(bf16[24,128,256]{2,1,0:T(8,128)(2,1)} %copy.20), channel_id=1, source_target_pairs={{0,16},{16,32},{32,48},{48,64},{64,80},{80,96},{96,112},{112,128},... | collective-permute-start | bytes 4718600 | tf_op jit(solution)/shard_map/while/body/eval_jaxpr/ppermute | solution.py:10
  299.0 23.8 %collective-permute-start = (bf16[24,128,256]{2,1,0:T(8,128)(2,1)}, bf16[24,128,256]{2,1,0:T(8,128)(2,1)}, u32[]{:S(2)}, u32[]{:S(2)}) collective-permute-start(bf16[24,128,256]{2,1,0:T(8,128)(2,1)} %copy.20), channel_id=1, source_target_pairs={{0,16},{16,32},{32,48},{48,64},{64,80},{80,96},{96,112},{112,128},... | collective-permute-start | bytes 4718600 | tf_op jit(solution)/shard_map/while/body/eval_jaxpr/ppermute | solution.py:10
  325.5 23.8 %collective-permute-start = (bf16[24,128,256]{2,1,0:T(8,128)(2,1)}, bf16[24,128,256]{2,1,0:T(8,128)(2,1)}, u32[]{:S(2)}, u32[]{:S(2)}) collective-permute-start(bf16[24,128,256]{2,1,0:T(8,128)(2,1)} %copy.20), channel_id=1, source_target_pairs={{0,16},{16,32},{32,48},{48,64},{64,80},{80,96},{96,112},{112,128},... | collective-permute-start | bytes 4718600 | tf_op jit(solution)/shard_map/while/body/eval_jaxpr/ppermute | solution.py:10
  352.0 23.8 %collective-permute-start = (bf16[24,128,256]{2,1,0:T(8,128)(2,1)}, bf16[24,128,256]{2,1,0:T(8,128)(2,1)}, u32[]{:S(2)}, u32[]{:S(2)}) collective-permute-start(bf16[24,128,256]{2,1,0:T(8,128)(2,1)} %copy.20), channel_id=1, source_target_pairs={{0,16},{16,32},{32,48},{48,64},{64,80},{80,96},{96,112},{112,128},... | collective-permute-start | bytes 4718600 | tf_op jit(solution)/shard_map/while/body/eval_jaxpr/ppermute | solution.py:10
  378.5 23.8 %collective-permute-start = (bf16[24,128,256]{2,1,0:T(8,128)(2,1)}, bf16[24,128,256]{2,1,0:T(8,128)(2,1)}, u32[]{:S(2)}, u32[]{:S(2)}) collective-permute-start(bf16[24,128,256]{2,1,0:T(8,128)(2,1)} %copy.20), channel_id=1, source_target_pairs={{0,16},{16,32},{32,48},{48,64},{64,80},{80,96},{96,112},{112,128},... | collective-permute-start | bytes 4718600 | tf_op jit(solution)/shard_map/while/body/eval_jaxpr/ppermute | solution.py:10
  405.0 23.8 %collective-permute-start = (bf16[24,128,256]{2,1,0:T(8,128)(2,1)}, bf16[24,128,256]{2,1,0:T(8,128)(2,1)}, u32[]{:S(2)}, u32[]{:S(2)}) collective-permute-start(bf16[24,128,256]{2,1,0:T(8,128)(2,1)} %copy.20), channel_id=1, source_target_pairs={{0,16},{16,32},{32,48},{48,64},{64,80},{80,96},{96,112},{112,128},... | collective-permute-start | bytes 4718600 | tf_op jit(solution)/shard_map/while/body/eval_jaxpr/ppermute | solution.py:10
  431.5 23.8 %collective-permute-start = (bf16[24,128,256]{2,1,0:T(8,128)(2,1)}, bf16[24,128,256]{2,1,0:T(8,128)(2,1)}, u32[]{:S(2)}, u32[]{:S(2)}) collective-permute-start(bf16[24,128,256]{2,1,0:T(8,128)(2,1)} %copy.20), channel_id=1, source_target_pairs={{0,16},{16,32},{32,48},{48,64},{64,80},{80,96},{96,112},{112,128},... | collective-permute-start | bytes 4718600 | tf_op jit(solution)/shard_map/while/body/eval_jaxpr/ppermute | solution.py:10
  458.0 23.8 %collective-permute-start = (bf16[24,128,256]{2,1,0:T(8,128)(2,1)}, bf16[24,128,256]{2,1,0:T(8,128)(2,1)}, u32[]{:S(2)}, u32[]{:S(2)}) collective-permute-start(bf16[24,128,256]{2,1,0:T(8,128)(2,1)} %copy.20), channel_id=1, source_target_pairs={{0,16},{16,32},{32,48},{48,64},{64,80},{80,96},{96,112},{112,128},... | collective-permute-start | bytes 4718600 | tf_op jit(solution)/shard_map/while/body/eval_jaxpr/ppermute | solution.py:10
  485.0 4.1 copy-start.1
  495.2 1.7 copy-start.2
  495.2 72.4 %copy-start.3 = (bf16[192,256]{1,0:T(8,128)(2,1)S(1)}, bf16[192,256]{1,0:T(8,128)(2,1)}, u32[]{:S(2)}) copy-start(bf16[192,256]{1,0:T(8,128)(2,1)} %param.14) | copy-start | bytes 294916
  496.9 323.5 %all-reduce.2.cloned.1.call-start = ((), (), s32[]{:S(2)}) async-start(), calls=%async_computation.3 | async-start | bytes 524288 | tf_op jit(solution)/shard_map/psum | solution.py:59
Sparse Core Ops, SparseCore 0:
  10.4 71.9 all-gather.1
  497.0 70.5 reduce-scatter.1
  573.6 246.7 all-reduce.1
where the time goes:
time: 835 us; the launch traced here: 829 us
  waiting for transfers between devices  514 us (62%)
  other arithmetic  160 us (19%)
  local copies, waits for them, and re-layouts  98.3 us (12%)
  matrix products  42.3 us (5%)
  between operations  13.8 us (2%)
    psum x1, waiting for transfers between devices, body(): weight_grad = lax.psum(local_weight, ('blk', 'rep'))  249 us
    scatter-add x16, other arithmetic, add_batch(): return totals.at[col_set].add(products)  136 us
    ppermute x15, waiting for transfers between devices, shifted(): return lax.ppermute(value, axis, pairs)  123 us
    all_gather x1, waiting for transfers between devices, body(): gathered_rows = lax.all_gather(scaled, 'rep', axis=0, tiled=True)  71.3 us
    reduce_scatter x1, waiting for transfers between devices, body(): lax.psum_scatter(totals.reshape(group_blocks * block, width), 'rep', scat...  70.7 us
    gather x16, local copies, waits for them, and re-layouts, add_batch(): picked = jnp.take(part_rows, row_set, axis=0)  52.1 us
    another operation x15, local copies, waits for them, and re-layouts  40.8 us
    dot_general x16, matrix products, add_batch(): jnp.einsum('cji,cjf->cif', tile_set, picked, preferred_element_type=jnp.f...  38.5 us
  transfers between devices with their start and end apart: 18, of which 18 were waited for; matrix products, arithmetic and copies ran while one was open for 29% of the time, Pallas kernels for 0%

commit v1 on v0

v1 whole, which is shorter than its diff:
```python
import jax
import jax.numpy as jnp
from jax import lax
from jax.experimental import pallas as pl
from jax.experimental.pallas import tpu as pltpu
from jax.sharding import PartitionSpec as P

NX, NY, NZ, NC = 4, 4, 8, 2
BOTH = ("blk", "rep")
UNROLL = 8


def flat_index(x, y, z, core):
    return (((x // 2) * NY + y) * NC + core) * (2 * NZ) + (x % 2) * NZ + z


def pairs(move):
    result = []
    for x in range(NX):
        for y in range(NY):
            for z in range(NZ):
                for core in range(NC):
                    tx, ty, tz, tc = move(x, y, z, core)
                    result.append((flat_index(x, y, z, core), flat_index(tx % NX, ty % NY, tz % NZ, tc)))
    return result


def along_z(step):
    return pairs(lambda x, y, z, core: (x, y, z + step, core))


def along_q(step):
    return pairs(lambda x, y, z, core: (x + step * core, y + step * (1 - core), z, core))


def along_s(step):
    return pairs(lambda x, y, z, core: (x + step * (1 - core), y + step * core, z, core))


def other_core():
    return pairs(lambda x, y, z, core: (x, y, z, 1 - core))


def send(value, moves):
    return lax.ppermute(value, BOTH, moves)


def ring(value, along, count):
    ahead, behind = along(1), along(-1)
    parts = {0: [value]}
    from_behind, from_ahead = value, value
    for step in range(1, count // 2):
        from_behind = send(from_behind, ahead)
        from_ahead = send(from_ahead, behind)
        parts[count - step] = [from_behind]
        parts[step] = [from_ahead]
    half = value.shape[0] // 2
    parts[count // 2] = [send(from_behind[:half], ahead), send(from_ahead[half:], behind)]
    return [parts[d] for d in range(count)]


def stacked(found):
    return jnp.stack([part[0] if len(part) == 1 else jnp.concatenate(part, axis=0) for part in found])


def products_kernel(chunk_starts, counts, unit0, unit1, columns, core, kept, received, *rest):
    chunks = rest[: len(chunk_starts)]
    own_out, other_out, units, totals, sem = rest[len(chunk_starts):]
    step = pl.program_id(0)

    @pl.when(step == 0)
    def _():
        copies = [
            pltpu.make_async_copy(chunk, units.at[pl.ds(start, chunk.shape[0])], sem.at[n])
            for n, (chunk, start) in enumerate(zip(chunks, chunk_starts))
        ]
        for copy in copies:
            copy.start()
        totals[...] = jnp.zeros_like(totals)
        for copy in copies:
            copy.wait()

    slots = kept.shape[2]
    for side, tiles in ((0, kept), (1, received)):
        base = (side * pl.num_programs(0) + step) * slots

        def batch(i, _):
            found = []
            for k in range(UNROLL):
                slot = i * UNROLL + k
                entry = base + slot
                tile = tiles[0, 0, slot] if side == 0 else tiles[0, slot]
                rows = jnp.concatenate([units[unit0[entry]], units[unit1[entry]]], axis=0)
                found.append((columns[entry], lax.dot_general(
                    tile, rows, (((0,), (0,)), ((), ())), preferred_element_type=jnp.float32)))
            for column, product in found:
                totals[column] += product
            return 0

        live = counts[side * pl.num_programs(0) + step]
        lax.fori_loop(0, (live + UNROLL - 1) // UNROLL, batch, 0)

    @pl.when(step == pl.num_programs(0) - 1)
    def _():
        half = own_out.shape[0]
        own_out[...] = totals[:half]
        other_out[...] = totals[half:].astype(other_out.dtype)


def products(tiles, received, chunks, chunk_starts, counts, unit0, unit1, columns, core):
    groups, _, slots, block, _ = tiles.shape
    width = chunks[0].shape[-1]
    return pl.pallas_call(
        lambda *refs: products_kernel(chunk_starts, *refs),
        out_shape=(
            jax.ShapeDtypeStruct((24, block, width), jnp.float32),
            jax.ShapeDtypeStruct((24, block, width), jnp.bfloat16),
        ),
        grid_spec=pltpu.PrefetchScalarGridSpec(
            num_scalar_prefetch=5,
            grid=(groups,),
            in_specs=[
                pl.BlockSpec((1, 1, slots, block, block), lambda g, n, u, v, k, core: (g, core[0], 0, 0, 0)),
                pl.BlockSpec((1, slots, block, block), lambda g, *_: (g, 0, 0, 0)),
            ] + [pl.BlockSpec(memory_space=pl.ANY)] * len(chunks),
            out_specs=(pl.BlockSpec((24, block, width), lambda g, *_: (0, 0, 0)),) * 2,
            scratch_shapes=[
                pltpu.VMEM((384, 64, width), jnp.bfloat16),
                pltpu.VMEM((48, block, width), jnp.float32),
                pltpu.SemaphoreType.DMA((len(chunks),)),
            ],
        ),
        compiler_params=pltpu.CompilerParams(vmem_limit_bytes=56 << 20),
        cost_estimate=pl.CostEstimate(flops=384 * 2 * block * block * width, bytes_accessed=30 << 20, transcendentals=0),
        name="tile_products",
    )(counts, unit0, unit1, columns, core, tiles, received, *chunks)


def body(out_grad, pre_act, features, weight, degrees, tiles, tile_rows, tile_cols):
    own_blk, own_rep = lax.axis_index("blk"), lax.axis_index("rep")
    core, y = own_blk % NC, (own_blk // NC) % NY
    x = (own_blk // (NC * NY)) * 2 + own_rep // NZ
    z = own_rep % NZ
    width = out_grad.shape[1]
    slots, block = tiles.shape[1], tiles.shape[2]
    groups = tiles.shape[0] // NC

    inverse_root = lax.rsqrt(degrees.astype(jnp.float32))
    active = (pre_act > 0).astype(jnp.float32)
    scaled = (out_grad.astype(jnp.float32) * active * inverse_root[:, None]).astype(jnp.bfloat16)

    odd = own_rep % 2
    full = lax.dynamic_slice_in_dim(scaled, odd * 64, 128, 0)
    half = lax.dynamic_slice_in_dim(scaled, (1 - odd) * 128, 64, 0)

    by_parity = tiles.reshape(groups, NC, slots, block, block)
    flip = other_core()
    passed = lax.dynamic_index_in_dim(by_parity, 1 - core, 1, keepdims=False)
    received = send(passed, flip)
    codes = (tile_rows * 32 + tile_cols).reshape(groups, NC, slots)
    kept_codes = lax.dynamic_index_in_dim(codes, core, 1, keepdims=False)
    received_codes = send(lax.dynamic_index_in_dim(codes, 1 - core, 1, keepdims=False), flip)
    codes = jnp.stack([kept_codes, received_codes])
    rows, cols = codes // 32, codes % 32

    group = jnp.arange(groups)[None, :, None] * NC
    pair, kind = rows // 3, rows % 3
    source_x = (group // (NC * NY)) * 2 + (2 * pair) // NZ
    source_y = (group // NC) % NY
    ahead_x, ahead_y = (source_x - x) % NX, (source_y - y) % NY
    ahead_s = jnp.where(core == 0, ahead_x, ahead_y)
    ahead_q = jnp.where(core == 0, ahead_y, ahead_x)
    first_z, second_z = (2 * pair - z) % NZ, (2 * pair + 1 - z) % NZ
    full_unit = ((ahead_s * 4 + ahead_q) * NZ + jnp.where(kind == 0, first_z, second_z)) * 2
    half_unit = 256 + ahead_q * 4 + ahead_s
    split = kind == 1
    unit0 = jnp.where(split, half_unit + first_z * 16, full_unit).reshape(-1).astype(jnp.int32)
    unit1 = jnp.where(split, half_unit + second_z * 16, full_unit + 1).reshape(-1).astype(jnp.int32)
    columns = (cols + jnp.arange(2)[:, None, None] * 24).reshape(-1).astype(jnp.int32)
    last = jnp.max(jnp.where(codes != 0, jnp.arange(slots) + 1, 0), axis=2)
    counts = jnp.minimum(last + 1, slots).reshape(-1).astype(jnp.int32)

    full_found = ring(stacked(ring(stacked(ring(full, along_z, NZ)), along_q, 4)), along_s, 4)
    half_found = ring(stacked(ring(stacked(ring(half, along_s, 4)), along_q, 4)), along_z, NZ)
    chunks, starts, at = [], [], 0
    for found in (full_found, half_found):
        for part in found:
            for piece in part:
                piece = piece.reshape(-1, 64, width)
                chunks.append(piece)
                starts.append(at)
                at += piece.shape[0]

    own, other = products(
        by_parity, received, chunks, starts, counts, unit0, unit1, columns, core.reshape(1).astype(jnp.int32)
    )
    partial = (own + send(other, flip).astype(jnp.float32)).astype(jnp.bfloat16)
    partial = partial.reshape(-1, width)
    exchanged = lax.all_to_all(partial, "rep", 0, 0, tiled=True)
    summed = exchanged.reshape(2 * NZ, -1, width).astype(jnp.float32).sum(axis=0)

    propagated = (inverse_root[:, None] * summed).astype(jnp.bfloat16)
    input_grad = lax.dot_general(
        propagated, weight, (((1,), (1,)), ((), ())), preferred_element_type=jnp.float32
    ).astype(jnp.bfloat16)
    local_weight = lax.dot_general(
        features, propagated, (((0,), (0,)), ((), ())), preferred_element_type=jnp.float32
    )
    own_rows = lax.all_to_all(local_weight, "rep", 0, 0, tiled=True).reshape(16, 16, width).sum(axis=0)
    spread = jnp.broadcast_to(own_rows[None], (16, 16, width)).reshape(256, width)
    own_rows = lax.all_to_all(spread, "blk", 0, 0, tiled=True).reshape(16, 16, width).sum(axis=0)
    spread = jnp.broadcast_to(own_rows[None], (16, 16, width)).reshape(256, width)
    weight_grad = lax.all_to_all(spread, "rep", 0, 0, tiled=True)
    return (input_grad, weight_grad)


def solution(mesh):
    placed = (
        P(("blk", "rep"), None),
        P(("blk", "rep"), None),
        P(("blk", "rep"), None),
        P(),
        P(("blk", "rep")),
        P(("blk", "rep"), None, None, None),
        P(("blk", "rep"), None),
        P(("blk", "rep"), None),
    )
    return jax.shard_map(
        body, mesh=mesh, in_specs=placed, out_specs=(P(("blk", "rep"), None), P()), check_vma=False
    )
```

time: 835 us -> 276 us (0.33)
  waiting for transfers between devices: 514 us -> 99.3 us
  other arithmetic: 160 us -> 5.24 us
  local copies, waits for them, and re-layouts: 98.3 us -> 20.7 us
  blocking collectives: 0 us -> 73.2 us
  starting transfers between devices: 0.16 us -> 51.8 us
  matrix products: 42.3 us -> 1.13 us
  Pallas kernels: 0 us -> 22.7 us
  between operations: 13.8 us -> 1.05 us
    psum x1 -> x0, waiting for transfers between devices: 249 us -> none  [body(): weight_grad = lax.psum(local_weight, ('blk', 'rep'))]
    scatter-add x16 -> x0, other arithmetic: 136 us -> none  [add_batch(): return totals.at[col_set].add(products)]
    all_to_all x0 -> x3, blocking collectives: none -> 73.2 us  [the longest x1 44.6 us: body(): exchanged = lax.all_to_all(partial, 'rep', 0, 0, tiled=True)]
    all_gather x1 -> x0, waiting for transfers between devices: 71.3 us -> none  [body(): gathered_rows = lax.all_gather(scaled, 'rep', axis=0, tiled=True)]
    reduce_scatter x1 -> x0, waiting for transfers between devices: 70.7 us -> none  [body(): lax.psum_scatter(totals.reshape(group_blocks * block, width), 'rep', scat...]
    gather x16 -> x0, local copies, waits for them, and re-layouts: 52.1 us -> none  [add_batch(): picked = jnp.take(part_rows, row_set, axis=0)]
    ppermute x15 -> x35, starting transfers between devices: 0.04 us -> 47.4 us  [send(): return lax.ppermute(value, BOTH, moves)]
    another operation x15 -> x3, local copies, waits for them, and re-layouts: 40.8 us -> 0.64 us  [the longest x1 0.63 us: body(): codes = jnp.stack([kept_codes, received_codes])]
  transfers between devices with their start and end apart: 18 -> 36, of which waited for: 18 -> 24; matrix products, arithmetic and copies ran while one was open for 29% -> 5% of each run, Pallas kernels for 0% -> 0%
where the time goes in v1:
time: 276 us; the launch traced here: 275 us
  waiting for transfers between devices  99.3 us (36%)
  blocking collectives  73.2 us (27%)
  starting transfers between devices  51.8 us (19%)
  Pallas kernels  22.7 us (8%)
  local copies, waits for them, and re-layouts  20.7 us (8%)
  other arithmetic  5.24 us (2%)
    ppermute x35, waiting for transfers between devices, send(): return lax.ppermute(value, BOTH, moves)  90.2 us
    ppermute x35, starting transfers between devices, send(): return lax.ppermute(value, BOTH, moves)  47.4 us
    all_to_all x1, blocking collectives, body(): exchanged = lax.all_to_all(partial, 'rep', 0, 0, tiled=True)  44.6 us
    pallas_call x1, Pallas kernels, products(): pl.pallas_call(lambda *refs: products_kernel(chunk_starts, *refs), out_sh...  22.7 us
    all_to_all x1, blocking collectives, body(): lax.all_to_all(local_weight, 'rep', 0, 0, tiled=True).reshape(16, 16, width)  14.8 us
    all_to_all x1, blocking collectives, body(): lax.all_to_all(spread, 'blk', 0, 0, tiled=True).reshape(16, 16, width)  13.8 us
    all_to_all x1, waiting for transfers between devices, body(): weight_grad = lax.all_to_all(spread, 'rep', 0, 0, tiled=True)  9.07 us
    squeeze x1, local copies, waits for them, and re-layouts, body(): passed = lax.dynamic_index_in_dim(by_parity, 1 - core, 1, keepdims=False)  8.19 us
  transfers between devices with their start and end apart: 36, of which 24 were waited for; matrix products, arithmetic and copies ran while one was open for 5% of the time, Pallas kernels for 0%

profile of v1, /device:TPU:32, one launch (start us, length us, event | category | flops | bytes accessed | tf_op | source)
XLA Modules:
  0.0 275.2 jit_solution(9121170099834731235)
XLA Ops:
  0.7 8.2 %dynamic-slice_bitcast_fusion = bf16[8,24,128,128]{3,2,1,0:T(8,128)(2,1)} fusion(bf16[8,2,24,128,128]{4,3,2,1,0:T(8,128)(2,1)} %bitcast.64, s32[]{:T(128)S(6)} %select_n.167), kind=kLoop, calls=%fused_computation | loop fusion | bytes 12582916 | tf_op jit(solution)/shard_map/jit(dynamic_index_in_dim)/squeeze | solution.py:158
  11.1 2.6 collective-permute-done.2
  13.8 3.3 %collective-permute-start.3 = (bf16[128,256]{1,0:T(8,128)(2,1)S(1)}, bf16[128,256]{1,0:T(8,128)(2,1)S(1)}, u32[]{:S(2)}, u32[]{:S(2)}) collective-permute-start(bf16[128,256]{1,0:T(8,128)(2,1)S(1)} %collective-permute-done.2), channel_id=1, source_target_pairs={{0,7},{16,23},{1,0},{17,16},{2,1},{18,17},{3,2},{19,18},{4,3},{20,... | collective-permute-start | bytes 196616 | tf_op jit(solution)/shard_map/ppermute | solution.py:45
  19.0 3.7 %collective-permute-start.4 = (bf16[128,256]{1,0:T(8,128)(2,1)S(1)}, bf16[128,256]{1,0:T(8,128)(2,1)S(1)}, u32[]{:S(2)}, u32[]{:S(2)}) collective-permute-start(bf16[128,256]{1,0:T(8,128)(2,1)S(1)} %collective-permute-done.3), channel_id=1, source_target_pairs={{0,7},{16,23},{1,0},{17,16},{2,1},{18,17},{3,2},{19,18},{4,3},{20,... | collective-permute-start | bytes 196616 | tf_op jit(solution)/shard_map/ppermute | solution.py:45
  24.6 3.6 %collective-permute-start.9 = (bf16[64,256]{1,0:T(8,128)(2,1)S(1)}, bf16[64,256]{1,0:T(8,128)(2,1)S(1)}, u32[]{:S(2)}, u32[]{:S(2)}) collective-permute-start(bf16[64,256]{1,0:T(8,128)(2,1)S(1)} %slice.49), channel_id=1, source_target_pairs={{0,7},{16,23},{1,0},{17,16},{2,1},{18,17},{3,2},{19,18},{4,3},{20,... | collective-permute-start | bytes 98312 | tf_op jit(solution)/shard_map/ppermute | solution.py:45
  29.8 3.9 %collective-permute-done.8 = bf16[64,256]{1,0:T(8,128)(2,1)S(1)} collective-permute-done((bf16[64,256]{1,0:T(8,128)(2,1)S(1)}, bf16[64,256]{1,0:T(8,128)(2,1)S(1)}, u32[]{:S(2)}, u32[]{:S(2)}) %collective-permute-start.8) | collective-permute-done | bytes 32800 | tf_op jit(solution)/shard_map/ppermute | solution.py:45
  33.7 3.1 %collective-permute-start.10 = (bf16[8,128,256]{2,1,0:T(8,128)(2,1)S(1)}, bf16[8,128,256]{2,1,0:T(8,128)(2,1)S(1)}, u32[]{:S(2)}, u32[]{:S(2)}) collective-permute-start(bf16[8,128,256]{2,1,0:T(8,128)(2,1)S(1)} %bitcast_dynamic-update-slice_fusion), channel_id=1, source_target_pairs={{0,96},{16,152},{1,97},{17,153},{2,98},{18,154},{3,99},{19,155},{4... | collective-permute-start | bytes 1572872 | tf_op jit(solution)/shard_map/ppermute | solution.py:45
  36.8 6.7 %collective-permute-done.10 = bf16[8,128,256]{2,1,0:T(8,128)(2,1)S(1)} collective-permute-done((bf16[8,128,256]{2,1,0:T(8,128)(2,1)S(1)}, bf16[8,128,256]{2,1,0:T(8,128)(2,1)S(1)}, u32[]{:S(2)}, u32[]{:S(2)}) %collective-permute-start.10) | collective-permute-done | bytes 524320 | tf_op jit(solution)/shard_map/ppermute | solution.py:45
  43.5 3.8 %collective-permute-start.13 = (bf16[4,128,256]{2,1,0:T(8,128)(2,1)S(1)}, bf16[4,128,256]{2,1,0:T(8,128)(2,1)S(1)}, u32[]{:S(2)}, u32[]{:S(2)}) collective-permute-start(bf16[4,128,256]{2,1,0:T(8,128)(2,1)S(1)} %slice.51), channel_id=1, source_target_pairs={{0,96},{16,152},{1,97},{17,153},{2,98},{18,154},{3,99},{19,155},{4... | collective-permute-start | bytes 786440 | tf_op jit(solution)/shard_map/ppermute | solution.py:45
  47.4 3.8 %collective-permute-done.13 = bf16[4,128,256]{2,1,0:T(8,128)(2,1)S(1)} collective-permute-done((bf16[4,128,256]{2,1,0:T(8,128)(2,1)S(1)}, bf16[4,128,256]{2,1,0:T(8,128)(2,1)S(1)}, u32[]{:S(2)}, u32[]{:S(2)}) %collective-permute-start.13) | collective-permute-done | bytes 262176 | tf_op jit(solution)/shard_map/ppermute | solution.py:45
  51.2 5.6 %collective-permute-done.12 = bf16[4,128,256]{2,1,0:T(8,128)(2,1)S(1)} collective-permute-done((bf16[4,128,256]{2,1,0:T(8,128)(2,1)S(1)}, bf16[4,128,256]{2,1,0:T(8,128)(2,1)S(1)}, u32[]{:S(2)}, u32[]{:S(2)}) %collective-permute-start.12) | collective-permute-done | bytes 262176 | tf_op jit(solution)/shard_map/ppermute | solution.py:45
  57.1 2.8 %collective-permute-start.15 = (bf16[4,8,128,256]{3,2,1,0:T(8,128)(2,1)S(1)}, bf16[4,8,128,256]{3,2,1,0:T(8,128)(2,1)}, u32[]{:S(2)}, u32[]{:S(2)}) collective-permute-start(bf16[4,8,128,256]{3,2,1,0:T(8,128)(2,1)S(1)} %pad_maximum_fusion), channel_id=1, source_target_pairs={{0,8},{16,48},{1,9},{17,49},{2,10},{18,50},{3,11},{19,51},{4,12},{... | collective-permute-start | bytes 6291464 | tf_op jit(solution)/shard_map/ppermute | solution.py:45
  63.3 23.3 %collective-permute-done.18 = bf16[64,256]{1,0:T(8,128)(2,1)S(1)} collective-permute-done((bf16[64,256]{1,0:T(8,128)(2,1)S(1)}, bf16[64,256]{1,0:T(8,128)(2,1)S(1)}, u32[]{:S(2)}, u32[]{:S(2)}) %collective-permute-start.18) | collective-permute-done | bytes 32800 | tf_op jit(solution)/shard_map/ppermute | solution.py:45
  86.6 2.6 collective-permute-start.21
  91.0 3.4 %collective-permute-done.20 = bf16[32,256]{1,0:T(8,128)(2,1)S(1)} collective-permute-done((bf16[32,256]{1,0:T(8,128)(2,1)S(1)}, bf16[32,256]{1,0:T(8,128)(2,1)S(1)}, u32[]{:S(2)}, u32[]{:S(2)}) %collective-permute-start.20) | collective-permute-done | bytes 16416 | tf_op jit(solution)/shard_map/ppermute | solution.py:45
  96.5 2.9 %collective-permute-done.22 = bf16[4,64,256]{2,1,0:T(8,128)(2,1)S(1)} collective-permute-done((bf16[4,64,256]{2,1,0:T(8,128)(2,1)S(1)}, bf16[4,64,256]{2,1,0:T(8,128)(2,1)S(1)}, u32[]{:S(2)}, u32[]{:S(2)}) %collective-permute-start.22) | collective-permute-done | bytes 131104 | tf_op jit(solution)/shard_map/ppermute | solution.py:45
  103.7 2.5 collective-permute-done.24
  106.3 3.3 %collective-permute-start.26 = (bf16[4,4,64,256]{3,2,1,0:T(8,128)(2,1)S(1)}, bf16[4,4,64,256]{3,2,1,0:T(8,128)(2,1)}, u32[]{:S(2)}, u32[]{:S(2)}) collective-permute-start(bf16[4,4,64,256]{3,2,1,0:T(8,128)(2,1)S(1)} %pad_maximum_fusion.1), channel_id=1, source_target_pairs={{0,7},{16,23},{1,0},{17,16},{2,1},{18,17},{3,2},{19,18},{4,3},{20,... | collective-permute-start | bytes 1572872 | tf_op jit(solution)/shard_map/ppermute | solution.py:45
  109.7 8.2 %collective-permute-done.26 = bf16[4,4,64,256]{3,2,1,0:T(8,128)(2,1)} collective-permute-done((bf16[4,4,64,256]{3,2,1,0:T(8,128)(2,1)S(1)}, bf16[4,4,64,256]{3,2,1,0:T(8,128)(2,1)}, u32[]{:S(2)}, u32[]{:S(2)}) %collective-permute-start.26) | collective-permute-done | bytes 524320 | tf_op jit(solution)/shard_map/ppermute | solution.py:45
  122.8 2.3 slice.53
  125.1 3.2 %collective-permute-start.17 = (bf16[2,8,128,256]{3,2,1,0:T(8,128)(2,1)}, bf16[2,8,128,256]{3,2,1,0:T(8,128)(2,1)S(1)}, u32[]{:S(2)}, u32[]{:S(2)}) collective-permute-start(bf16[2,8,128,256]{3,2,1,0:T(8,128)(2,1)} %slice.53), channel_id=1, source_target_pairs={{0,136},{16,112},{1,137},{17,113},{2,138},{18,114},{3,139},{19,115... | collective-permute-start | bytes 3145736 | tf_op jit(solution)/shard_map/ppermute | solution.py:45
  128.4 2.5 collective-permute-start.28
  132.7 13.4 %collective-permute-done.31 = bf16[4,4,64,256]{3,2,1,0:T(8,128)(2,1)S(1)} collective-permute-done((bf16[4,4,64,256]{3,2,1,0:T(8,128)(2,1)}, bf16[4,4,64,256]{3,2,1,0:T(8,128)(2,1)S(1)}, u32[]{:S(2)}, u32[]{:S(2)}) %collective-permute-start.31) | collective-permute-done | bytes 524320 | tf_op jit(solution)/shard_map/ppermute | solution.py:45
  147.6 3.0 %collective-permute-start.33 = (bf16[2,4,64,256]{3,2,1,0:T(8,128)(2,1)}, bf16[2,4,64,256]{3,2,1,0:T(8,128)(2,1)}, u32[]{:S(2)}, u32[]{:S(2)}) collective-permute-start(bf16[2,4,64,256]{3,2,1,0:T(8,128)(2,1)} %slice.59), channel_id=1, source_target_pairs={{0,7},{16,23},{1,0},{17,16},{2,1},{18,17},{3,2},{19,18},{4,3},{20,... | collective-permute-start | bytes 786440 | tf_op jit(solution)/shard_map/ppermute | solution.py:45
  156.7 22.7 %tile_products.1 = (f32[24,128,256]{2,1,0:T(8,128)}, bf16[24,128,256]{2,1,0:T(8,128)(2,1)}) custom-call(s32[16]{0:T(128)} %min.8.refs_0_, s32[384]{0:T(512)} %get-tuple-element.15.refs_1_, s32[384]{0:T(512)} %get-tuple-element.14.refs_2_, s32[384]{0:T(512)} %get-tuple-element.16.refs_3_, s32[1]{0:T(128)} %bitcast.4.refs_4_, ...), custom_call_target="tpu_custom_call" | custom-call | flops 3221225472 | bytes 31457280 | tf_op jit(solution)/shard_map/tile_products/pallas_call | solution.py:113
  179.5 3.6 %collective-permute-done.34 = bf16[24,128,256]{2,1,0:T(8,128)(2,1)S(1)} collective-permute-done((bf16[24,128,256]{2,1,0:T(8,128)(2,1)}, bf16[24,128,256]{2,1,0:T(8,128)(2,1)S(1)}, u32[]{:S(2)}, u32[]{:S(2)}) %collective-permute-start.34) | collective-permute-done | bytes 1572896 | tf_op jit(solution)/shard_map/ppermute | solution.py:45
  183.2 2.4 add_convert_fusion
  185.6 44.6 %all_to_all.33 = bf16[16,192,256]{2,1,0:T(8,128)(2,1)S(1)} all-to-all(bf16[16,192,256]{2,1,0:T(8,128)(2,1)S(1)} %bitcast.67), channel_id=1, replica_groups=mesh['blk'=16,'rep'=16] {'rep'}, dimensions={0} | all-to-all | bytes 3145728 | tf_op jit(solution)/shard_map/all_to_all | solution.py:199
  230.7 14.8 %all_to_all.34 = f32[16,16,256]{2,1,0:T(8,128)S(1)} all-to-all(f32[16,16,256]{2,1,0:T(8,128)S(1)} %bitcast.76), channel_id=1, replica_groups=mesh['blk'=16,'rep'=16] {'rep'}, dimensions={0} | all-to-all | bytes 524288 | tf_op jit(solution)/shard_map/all_to_all | solution.py:209
  245.6 13.8 %all_to_all.35 = f32[16,16,256]{2,1,0:T(8,128)S(1)} all-to-all(f32[16,16,256]{2,1,0:T(8,128)S(1)} %broadcast_in_dim.41), channel_id=1, replica_groups=mesh['blk'=16,'rep'=16] {'blk'}, dimensions={0} | all-to-all | bytes 524288 | tf_op jit(solution)/shard_map/all_to_all | solution.py:211
  260.1 4.4 %all-to-all-start.3 = ((f32[16,16,256]{2,1,0:T(8,128)}), f32[16,16,256]{2,1,0:T(8,128)S(1)}, u32[]{:S(2)}, u32[]{:S(2)}) async-start(f32[16,16,256]{2,1,0:T(8,128)} %broadcast_in_dim.42), calls=%async_computation.3 | async-start | bytes 524288 | tf_op jit(solution)/shard_map/all_to_all | solution.py:213
  265.4 9.1 %all-to-all-done.3 = f32[16,16,256]{2,1,0:T(8,128)S(1)} async-done(((f32[16,16,256]{2,1,0:T(8,128)}), f32[16,16,256]{2,1,0:T(8,128)S(1)}, u32[]{:S(2)}, u32[]{:S(2)}) %all-to-all-start.3) | async-done | bytes 262176 | tf_op jit(solution)/shard_map/all_to_all | solution.py:213
  (128 shorter events, 37.1 us)
Async XLA Ops:
  8.9 146.5 %collective-permute-start.1 = (bf16[8,24,128,128]{3,2,1,0:T(8,128)(2,1)}, bf16[8,24,128,128]{3,2,1,0:T(8,128)(2,1)}, u32[]{:S(2)}, u32[]{:S(2)}) collective-permute-start(bf16[8,24,128,128]{3,2,1,0:T(8,128)(2,1)} %dynamic-slice_bitcast_fusion), channel_id=1, source_target_pairs={{0,16},{16,0},{1,17},{17,1},{2,18},{18,2},{3,19},{19,3},{4,20},{20... | collective-permute-start | bytes 18874376 | tf_op jit(solution)/shard_map/ppermute | solution.py:45
  9.0 4.8 %collective-permute-start.2 = (bf16[128,256]{1,0:T(8,128)(2,1)S(1)}, bf16[128,256]{1,0:T(8,128)(2,1)S(1)}, u32[]{:S(2)}, u32[]{:S(2)}) collective-permute-start(bf16[128,256]{1,0:T(8,128)(2,1)S(1)} %get-tuple-element.7), channel_id=1, source_target_pairs={{0,7},{16,23},{1,0},{17,16},{2,1},{18,17},{3,2},{19,18},{4,3},{20,... | collective-permute-start | bytes 196616 | tf_op jit(solution)/shard_map/ppermute | solution.py:45
  11.0 6.6 %collective-permute-start.5 = (bf16[128,256]{1,0:T(8,128)(2,1)S(1)}, bf16[128,256]{1,0:T(8,128)(2,1)S(1)}, u32[]{:S(2)}, u32[]{:S(2)}) collective-permute-start(bf16[128,256]{1,0:T(8,128)(2,1)S(1)} %get-tuple-element.7), channel_id=1, source_target_pairs={{0,1},{16,17},{1,2},{17,18},{2,3},{18,19},{3,4},{19,20},{4,5},{20,... | collective-permute-start | bytes 196616 | tf_op jit(solution)/shard_map/ppermute | solution.py:45
  13.8 5.2 %collective-permute-start.3 = (bf16[128,256]{1,0:T(8,128)(2,1)S(1)}, bf16[128,256]{1,0:T(8,128)(2,1)S(1)}, u32[]{:S(2)}, u32[]{:S(2)}) collective-permute-start(bf16[128,256]{1,0:T(8,128)(2,1)S(1)} %collective-permute-done.2), channel_id=1, source_target_pairs={{0,7},{16,23},{1,0},{17,16},{2,1},{18,17},{3,2},{19,18},{4,3},{20,... | collective-permute-start | bytes 196616 | tf_op jit(solution)/shard_map/ppermute | solution.py:45
  17.6 5.5 %collective-permute-start.6 = (bf16[128,256]{1,0:T(8,128)(2,1)S(1)}, bf16[128,256]{1,0:T(8,128)(2,1)S(1)}, u32[]{:S(2)}, u32[]{:S(2)}) collective-permute-start(bf16[128,256]{1,0:T(8,128)(2,1)S(1)} %collective-permute-done.5), channel_id=1, source_target_pairs={{0,1},{16,17},{1,2},{17,18},{2,3},{18,19},{3,4},{19,20},{4,5},{20,... | collective-permute-start | bytes 196616 | tf_op jit(solution)/shard_map/ppermute | solution.py:45
  19.0 5.6 %collective-permute-start.4 = (bf16[128,256]{1,0:T(8,128)(2,1)S(1)}, bf16[128,256]{1,0:T(8,128)(2,1)S(1)}, u32[]{:S(2)}, u32[]{:S(2)}) collective-permute-start(bf16[128,256]{1,0:T(8,128)(2,1)S(1)} %collective-permute-done.3), channel_id=1, source_target_pairs={{0,7},{16,23},{1,0},{17,16},{2,1},{18,17},{3,2},{19,18},{4,3},{20,... | collective-permute-start | bytes 196616 | tf_op jit(solution)/shard_map/ppermute | solution.py:45
  23.0 5.5 %collective-permute-start.7 = (bf16[128,256]{1,0:T(8,128)(2,1)S(1)}, bf16[128,256]{1,0:T(8,128)(2,1)S(1)}, u32[]{:S(2)}, u32[]{:S(2)}) collective-permute-start(bf16[128,256]{1,0:T(8,128)(2,1)S(1)} %collective-permute-done.6), channel_id=1, source_target_pairs={{0,1},{16,17},{1,2},{17,18},{2,3},{18,19},{3,4},{19,20},{4,5},{20,... | collective-permute-start | bytes 196616 | tf_op jit(solution)/shard_map/ppermute | solution.py:45
  24.6 5.2 %collective-permute-start.9 = (bf16[64,256]{1,0:T(8,128)(2,1)S(1)}, bf16[64,256]{1,0:T(8,128)(2,1)S(1)}, u32[]{:S(2)}, u32[]{:S(2)}) collective-permute-start(bf16[64,256]{1,0:T(8,128)(2,1)S(1)} %slice.49), channel_id=1, source_target_pairs={{0,7},{16,23},{1,0},{17,16},{2,1},{18,17},{3,2},{19,18},{4,3},{20,... | collective-permute-start | bytes 98312 | tf_op jit(solution)/shard_map/ppermute | solution.py:45
  28.5 5.1 %collective-permute-start.8 = (bf16[64,256]{1,0:T(8,128)(2,1)S(1)}, bf16[64,256]{1,0:T(8,128)(2,1)S(1)}, u32[]{:S(2)}, u32[]{:S(2)}) collective-permute-start(bf16[64,256]{1,0:T(8,128)(2,1)S(1)} %slice.48), channel_id=1, source_target_pairs={{0,1},{16,17},{1,2},{17,18},{2,3},{18,19},{3,4},{19,20},{4,5},{20,... | collective-permute-start | bytes 98312 | tf_op jit(solution)/shard_map/ppermute | solution.py:45
  33.7 9.8 %collective-permute-start.10 = (bf16[8,128,256]{2,1,0:T(8,128)(2,1)S(1)}, bf16[8,128,256]{2,1,0:T(8,128)(2,1)S(1)}, u32[]{:S(2)}, u32[]{:S(2)}) collective-permute-start(bf16[8,128,256]{2,1,0:T(8,128)(2,1)S(1)} %bitcast_dynamic-update-slice_fusion), channel_id=1, source_target_pairs={{0,96},{16,152},{1,97},{17,153},{2,98},{18,154},{3,99},{19,155},{4... | collective-permute-start | bytes 1572872 | tf_op jit(solution)/shard_map/ppermute | solution.py:45
  36.8 10.5 %collective-permute-start.11 = (bf16[8,128,256]{2,1,0:T(8,128)(2,1)S(1)}, bf16[8,128,256]{2,1,0:T(8,128)(2,1)S(1)}, u32[]{:S(2)}, u32[]{:S(2)}) collective-permute-start(bf16[8,128,256]{2,1,0:T(8,128)(2,1)S(1)} %bitcast_dynamic-update-slice_fusion), channel_id=1, source_target_pairs={{0,32},{16,24},{1,33},{17,25},{2,34},{18,26},{3,35},{19,27},{4,36}... | collective-permute-start | bytes 1572872 | tf_op jit(solution)/shard_map/ppermute | solution.py:45
  43.5 7.7 %collective-permute-start.13 = (bf16[4,128,256]{2,1,0:T(8,128)(2,1)S(1)}, bf16[4,128,256]{2,1,0:T(8,128)(2,1)S(1)}, u32[]{:S(2)}, u32[]{:S(2)}) collective-permute-start(bf16[4,128,256]{2,1,0:T(8,128)(2,1)S(1)} %slice.51), channel_id=1, source_target_pairs={{0,96},{16,152},{1,97},{17,153},{2,98},{18,154},{3,99},{19,155},{4... | collective-permute-start | bytes 786440 | tf_op jit(solution)/shard_map/ppermute | solution.py:45
  47.3 9.4 %collective-permute-start.12 = (bf16[4,128,256]{2,1,0:T(8,128)(2,1)S(1)}, bf16[4,128,256]{2,1,0:T(8,128)(2,1)S(1)}, u32[]{:S(2)}, u32[]{:S(2)}) collective-permute-start(bf16[4,128,256]{2,1,0:T(8,128)(2,1)S(1)} %slice.50), channel_id=1, source_target_pairs={{0,32},{16,24},{1,33},{17,25},{2,34},{18,26},{3,35},{19,27},{4,36}... | collective-permute-start | bytes 786440 | tf_op jit(solution)/shard_map/ppermute | solution.py:45
  57.1 63.3 %collective-permute-start.15 = (bf16[4,8,128,256]{3,2,1,0:T(8,128)(2,1)S(1)}, bf16[4,8,128,256]{3,2,1,0:T(8,128)(2,1)}, u32[]{:S(2)}, u32[]{:S(2)}) collective-permute-start(bf16[4,8,128,256]{3,2,1,0:T(8,128)(2,1)S(1)} %pad_maximum_fusion), channel_id=1, source_target_pairs={{0,8},{16,48},{1,9},{17,49},{2,10},{18,50},{3,11},{19,51},{4,12},{... | collective-permute-start | bytes 6291464 | tf_op jit(solution)/shard_map/ppermute | solution.py:45
  59.9 62.9 %collective-permute-start.14 = (bf16[4,8,128,256]{3,2,1,0:T(8,128)(2,1)S(1)}, bf16[4,8,128,256]{3,2,1,0:T(8,128)(2,1)}, u32[]{:S(2)}, u32[]{:S(2)}) collective-permute-start(bf16[4,8,128,256]{3,2,1,0:T(8,128)(2,1)S(1)} %pad_maximum_fusion), channel_id=1, source_target_pairs={{0,136},{16,112},{1,137},{17,113},{2,138},{18,114},{3,139},{19,115... | collective-permute-start | bytes 6291464 | tf_op jit(solution)/shard_map/ppermute | solution.py:45
  61.3 25.3 %collective-permute-start.18 = (bf16[64,256]{1,0:T(8,128)(2,1)S(1)}, bf16[64,256]{1,0:T(8,128)(2,1)S(1)}, u32[]{:S(2)}, u32[]{:S(2)}) collective-permute-start(bf16[64,256]{1,0:T(8,128)(2,1)S(1)} %constant_dynamic-slice_fusion), channel_id=1, source_target_pairs={{0,136},{16,112},{1,137},{17,113},{2,138},{18,114},{3,139},{19,115... | collective-permute-start | bytes 98312 | tf_op jit(solution)/shard_map/ppermute | solution.py:45
  63.2 26.0 %collective-permute-start.19 = (bf16[64,256]{1,0:T(8,128)(2,1)S(1)}, bf16[64,256]{1,0:T(8,128)(2,1)S(1)}, u32[]{:S(2)}, u32[]{:S(2)}) collective-permute-start(bf16[64,256]{1,0:T(8,128)(2,1)S(1)} %constant_dynamic-slice_fusion), channel_id=1, source_target_pairs={{0,8},{16,48},{1,9},{17,49},{2,10},{18,50},{3,11},{19,51},{4,12},{... | collective-permute-start | bytes 98312 | tf_op jit(solution)/shard_map/ppermute | solution.py:45
  89.2 5.1 %collective-permute-start.20 = (bf16[32,256]{1,0:T(8,128)(2,1)S(1)}, bf16[32,256]{1,0:T(8,128)(2,1)S(1)}, u32[]{:S(2)}, u32[]{:S(2)}) collective-permute-start(bf16[32,256]{1,0:T(8,128)(2,1)S(1)} %slice.54), channel_id=1, source_target_pairs={{0,8},{16,48},{1,9},{17,49},{2,10},{18,50},{3,11},{19,51},{4,12},{... | collective-permute-start | bytes 49160 | tf_op jit(solution)/shard_map/ppermute | solution.py:45
  94.4 5.0 %collective-permute-start.22 = (bf16[4,64,256]{2,1,0:T(8,128)(2,1)S(1)}, bf16[4,64,256]{2,1,0:T(8,128)(2,1)S(1)}, u32[]{:S(2)}, u32[]{:S(2)}) collective-permute-start(bf16[4,64,256]{2,1,0:T(8,128)(2,1)S(1)} %get-tuple-element.9), channel_id=1, source_target_pairs={{0,96},{16,152},{1,97},{17,153},{2,98},{18,154},{3,99},{19,155},{4... | collective-permute-start | bytes 393224 | tf_op jit(solution)/shard_map/ppermute | solution.py:45
  94.5 6.3 %collective-permute-start.23 = (bf16[4,64,256]{2,1,0:T(8,128)(2,1)S(1)}, bf16[4,64,256]{2,1,0:T(8,128)(2,1)S(1)}, u32[]{:S(2)}, u32[]{:S(2)}) collective-permute-start(bf16[4,64,256]{2,1,0:T(8,128)(2,1)S(1)} %get-tuple-element.9), channel_id=1, source_target_pairs={{0,32},{16,24},{1,33},{17,25},{2,34},{18,26},{3,35},{19,27},{4,36}... | collective-permute-start | bytes 393224 | tf_op jit(solution)/shard_map/ppermute | solution.py:45
  100.7 5.5 %collective-permute-start.24 = (bf16[2,64,256]{2,1,0:T(8,128)(2,1)S(1)}, bf16[2,64,256]{2,1,0:T(8,128)(2,1)S(1)}, u32[]{:S(2)}, u32[]{:S(2)}) collective-permute-start(bf16[2,64,256]{2,1,0:T(8,128)(2,1)S(1)} %slice.56), channel_id=1, source_target_pairs={{0,32},{16,24},{1,33},{17,25},{2,34},{18,26},{3,35},{19,27},{4,36}... | collective-permute-start | bytes 196616 | tf_op jit(solution)/shard_map/ppermute | solution.py:45
  106.3 11.5 %collective-permute-start.26 = (bf16[4,4,64,256]{3,2,1,0:T(8,128)(2,1)S(1)}, bf16[4,4,64,256]{3,2,1,0:T(8,128)(2,1)}, u32[]{:S(2)}, u32[]{:S(2)}) collective-permute-start(bf16[4,4,64,256]{3,2,1,0:T(8,128)(2,1)S(1)} %pad_maximum_fusion.1), channel_id=1, source_target_pairs={{0,7},{16,23},{1,0},{17,16},{2,1},{18,17},{3,2},{19,18},{4,3},{20,... | collective-permute-start | bytes 1572872 | tf_op jit(solution)/shard_map/ppermute | solution.py:45
  109.7 10.5 %collective-permute-start.29 = (bf16[4,4,64,256]{3,2,1,0:T(8,128)(2,1)S(1)}, bf16[4,4,64,256]{3,2,1,0:T(8,128)(2,1)}, u32[]{:S(2)}, u32[]{:S(2)}) collective-permute-start(bf16[4,4,64,256]{3,2,1,0:T(8,128)(2,1)S(1)} %pad_maximum_fusion.1), channel_id=1, source_target_pairs={{0,1},{16,17},{1,2},{17,18},{2,3},{18,19},{3,4},{19,20},{4,5},{20,... | collective-permute-start | bytes 1572872 | tf_op jit(solution)/shard_map/ppermute | solution.py:45
  117.9 10.5 %collective-permute-start.27 = (bf16[4,4,64,256]{3,2,1,0:T(8,128)(2,1)}, bf16[4,4,64,256]{3,2,1,0:T(8,128)(2,1)}, u32[]{:S(2)}, u32[]{:S(2)}) collective-permute-start(bf16[4,4,64,256]{3,2,1,0:T(8,128)(2,1)} %collective-permute-done.26), channel_id=1, source_target_pairs={{0,7},{16,23},{1,0},{17,16},{2,1},{18,17},{3,2},{19,18},{4,3},{20,... | collective-permute-start | bytes 1572872 | tf_op jit(solution)/shard_map/ppermute | solution.py:45
  120.2 10.7 %collective-permute-start.30 = (bf16[4,4,64,256]{3,2,1,0:T(8,128)(2,1)}, bf16[4,4,64,256]{3,2,1,0:T(8,128)(2,1)}, u32[]{:S(2)}, u32[]{:S(2)}) collective-permute-start(bf16[4,4,64,256]{3,2,1,0:T(8,128)(2,1)} %collective-permute-done.29), channel_id=1, source_target_pairs={{0,1},{16,17},{1,2},{17,18},{2,3},{18,19},{3,4},{19,20},{4,5},{20,... | collective-permute-start | bytes 1572872 | tf_op jit(solution)/shard_map/ppermute | solution.py:45
  122.8 32.6 %collective-permute-start.16 = (bf16[2,8,128,256]{3,2,1,0:T(8,128)(2,1)}, bf16[2,8,128,256]{3,2,1,0:T(8,128)(2,1)S(1)}, u32[]{:S(2)}, u32[]{:S(2)}) collective-permute-start(bf16[2,8,128,256]{3,2,1,0:T(8,128)(2,1)} %slice.52), channel_id=1, source_target_pairs={{0,8},{16,48},{1,9},{17,49},{2,10},{18,50},{3,11},{19,51},{4,12},{... | collective-permute-start | bytes 3145736 | tf_op jit(solution)/shard_map/ppermute | solution.py:45
  125.1 30.3 %collective-permute-start.17 = (bf16[2,8,128,256]{3,2,1,0:T(8,128)(2,1)}, bf16[2,8,128,256]{3,2,1,0:T(8,128)(2,1)S(1)}, u32[]{:S(2)}, u32[]{:S(2)}) collective-permute-start(bf16[2,8,128,256]{3,2,1,0:T(8,128)(2,1)} %slice.53), channel_id=1, source_target_pairs={{0,136},{16,112},{1,137},{17,113},{2,138},{18,114},{3,139},{19,115... | collective-permute-start | bytes 3145736 | tf_op jit(solution)/shard_map/ppermute | solution.py:45
  128.4 18.5 %collective-permute-start.28 = (bf16[4,4,64,256]{3,2,1,0:T(8,128)(2,1)}, bf16[4,4,64,256]{3,2,1,0:T(8,128)(2,1)S(1)}, u32[]{:S(2)}, u32[]{:S(2)}) collective-permute-start(bf16[4,4,64,256]{3,2,1,0:T(8,128)(2,1)} %collective-permute-done.27), channel_id=1, source_target_pairs={{0,7},{16,23},{1,0},{17,16},{2,1},{18,17},{3,2},{19,18},{4,3},{20,... | collective-permute-start | bytes 1572872 | tf_op jit(solution)/shard_map/ppermute | solution.py:45
  130.9 15.2 %collective-permute-start.31 = (bf16[4,4,64,256]{3,2,1,0:T(8,128)(2,1)}, bf16[4,4,64,256]{3,2,1,0:T(8,128)(2,1)S(1)}, u32[]{:S(2)}, u32[]{:S(2)}) collective-permute-start(bf16[4,4,64,256]{3,2,1,0:T(8,128)(2,1)} %collective-permute-done.30), channel_id=1, source_target_pairs={{0,1},{16,17},{1,2},{17,18},{2,3},{18,19},{3,4},{19,20},{4,5},{20,... | collective-permute-start | bytes 1572872 | tf_op jit(solution)/shard_map/ppermute | solution.py:45
  146.8 8.4 %collective-permute-start.32 = (bf16[2,4,64,256]{3,2,1,0:T(8,128)(2,1)}, bf16[2,4,64,256]{3,2,1,0:T(8,128)(2,1)S(1)}, u32[]{:S(2)}, u32[]{:S(2)}) collective-permute-start(bf16[2,4,64,256]{3,2,1,0:T(8,128)(2,1)} %slice.58), channel_id=1, source_target_pairs={{0,1},{16,17},{1,2},{17,18},{2,3},{18,19},{3,4},{19,20},{4,5},{20,... | collective-permute-start | bytes 786440 | tf_op jit(solution)/shard_map/ppermute | solution.py:45
  147.6 7.8 %collective-permute-start.33 = (bf16[2,4,64,256]{3,2,1,0:T(8,128)(2,1)}, bf16[2,4,64,256]{3,2,1,0:T(8,128)(2,1)}, u32[]{:S(2)}, u32[]{:S(2)}) collective-permute-start(bf16[2,4,64,256]{3,2,1,0:T(8,128)(2,1)} %slice.59), channel_id=1, source_target_pairs={{0,7},{16,23},{1,0},{17,16},{2,1},{18,17},{3,2},{19,18},{4,3},{20,... | collective-permute-start | bytes 786440 | tf_op jit(solution)/shard_map/ppermute | solution.py:45
  260.1 14.4 %all-to-all-start.3 = ((f32[16,16,256]{2,1,0:T(8,128)}), f32[16,16,256]{2,1,0:T(8,128)S(1)}, u32[]{:S(2)}, u32[]{:S(2)}) async-start(f32[16,16,256]{2,1,0:T(8,128)} %broadcast_in_dim.42), calls=%async_computation.3 | async-start | bytes 524288 | tf_op jit(solution)/shard_map/all_to_all | solution.py:213
  (18 other events, 582.4 us)

commit v2 on v1

v2 whole, which is shorter than its diff:
```python
import jax
import jax.numpy as jnp
from jax import lax
from jax.experimental import pallas as pl
from jax.experimental.pallas import tpu as pltpu
from jax.sharding import PartitionSpec as P

NX, NY, NZ, NC = 4, 4, 8, 2
BOTH = ("blk", "rep")
UNROLL = 8


def flat_index(x, y, z, core):
    return (((x // 2) * NY + y) * NC + core) * (2 * NZ) + (x % 2) * NZ + z


def pairs(move):
    result = []
    for x in range(NX):
        for y in range(NY):
            for z in range(NZ):
                for core in range(NC):
                    tx, ty, tz, tc = move(x, y, z, core)
                    result.append((flat_index(x, y, z, core), flat_index(tx % NX, ty % NY, tz % NZ, tc)))
    return result


def along_z(step):
    return pairs(lambda x, y, z, core: (x, y, z + step, core))


def along_q(step):
    return pairs(lambda x, y, z, core: (x + step * core, y + step * (1 - core), z, core))


def along_s(step):
    return pairs(lambda x, y, z, core: (x + step * (1 - core), y + step * core, z, core))


def across_x():
    return pairs(lambda x, y, z, core: (x + 1 - 2 * (x % 2), y, z, core))


def other_core():
    return pairs(lambda x, y, z, core: (x, y, z, 1 - core))


def send(value, moves):
    return lax.ppermute(value, BOTH, moves)


def ring_first(value, along):
    return send(value, along(1)), send(value, along(-1))


def ring_last(behind, ahead, along):
    half = behind.shape[0] // 2
    return [send(behind[:half], along(1)), send(ahead[half:], along(-1))]


def together(*values):
    return lax.optimization_barrier(values)


def stacked(found):
    return jnp.stack([part[0] if len(part) == 1 else jnp.concatenate(part, axis=0) for part in found])


def products_kernel(places, counts, unit0, unit1, columns, here, kept, received, *rest):
    chunks = rest[: len(places)]
    own_out, other_out, units, totals, sem = rest[len(places):]
    step = pl.program_id(0)

    @pl.when(step == 0)
    def _():
        copies = [
            pltpu.make_async_copy(chunk.at[pl.ds(0, size)], units.at[pl.ds(start, size)], sem.at[n])
            for n, (chunk, (start, size)) in enumerate(zip(chunks, places))
        ]
        for copy in copies:
            copy.start()
        totals[...] = jnp.zeros_like(totals)
        for copy in copies:
            copy.wait()

    slots = kept.shape[2]
    for side, tiles in ((0, kept), (1, received)):
        base = (side * pl.num_programs(0) + step) * slots

        def batch(i, _):
            found = []
            for k in range(UNROLL):
                slot = i * UNROLL + k
                entry = base + slot
                tile = tiles[0, 0, slot] if side == 0 else tiles[0, slot]
                rows = jnp.concatenate([units[unit0[entry]], units[unit1[entry]]], axis=0)
                found.append((columns[entry], lax.dot_general(
                    tile, rows, (((0,), (0,)), ((), ())), preferred_element_type=jnp.float32)))
            for column, product in found:
                totals[column] += product
            return 0

        live = counts[side * pl.num_programs(0) + step]
        lax.fori_loop(0, (live + UNROLL - 1) // UNROLL, batch, 0)

    @pl.when(step == pl.num_programs(0) - 1)
    def _():
        for rep in range(2 * NZ):
            place = lax.bitwise_xor(rep // NZ, here[1]) * NZ + lax.rem(rep % NZ - here[2] + NZ, NZ)
            for out, side in ((own_out, 0), (other_out, 24)):
                tile = side + 3 * rep // 2
                if rep % 2 == 0:
                    out[place, :128] = totals[tile].astype(out.dtype)
                    out[place, 128:] = totals[tile + 1, :64].astype(out.dtype)
                else:
                    out[place, :64] = totals[tile, 64:].astype(out.dtype)
                    out[place, 64:] = totals[tile + 1].astype(out.dtype)


def combine_kernel(places, own, other, *rest):
    pieces = rest[: len(places)]
    partial, gradient, features, sem = rest[len(places):]
    step = pl.program_id(0)

    @pl.when(step == 0)
    def _():
        copies = [
            pltpu.make_async_copy(piece.at[pl.ds(start, features.shape[1])], features.at[n], sem.at[n])
            for n, (piece, start) in enumerate(zip(pieces, places))
        ]
        for copy in copies:
            copy.start()
        gradient[...] = jnp.zeros_like(gradient)
        for copy in copies:
            copy.wait()

    total = gradient[...]
    for near in range(2):
        rows = (own[near, 0] + other[near, 0].astype(jnp.float32)).astype(partial.dtype)
        partial[near, 0] = rows
        lanes = jnp.concatenate([features[step, 3 * near + n] for n in range(3)], axis=0)
        total += lax.dot_general(lanes, rows, (((0,), (0,)), ((), ())), preferred_element_type=jnp.float32)
    gradient[...] = total


def combine(own, other, pieces, places):
    width = own.shape[-1]
    block = pl.BlockSpec((2, 1, 192, width), lambda d: (0, d, 0, 0))
    return pl.pallas_call(
        lambda *refs: combine_kernel(places, *refs),
        out_shape=(
            jax.ShapeDtypeStruct((2, NZ, 192, width), jnp.bfloat16),
            jax.ShapeDtypeStruct((width, width), jnp.float32),
        ),
        grid_spec=pltpu.PrefetchScalarGridSpec(
            num_scalar_prefetch=0,
            grid=(NZ,),
            in_specs=[block, block] + [pl.BlockSpec(memory_space=pl.ANY)] * NZ,
            out_specs=(block, pl.BlockSpec((width, width), lambda d: (0, 0))),
            scratch_shapes=[pltpu.VMEM((NZ, 6, 64, width), jnp.bfloat16), pltpu.SemaphoreType.DMA((NZ,))],
        ),
        compiler_params=pltpu.CompilerParams(vmem_limit_bytes=56 << 20),
        cost_estimate=pl.CostEstimate(flops=2 * 3072 * width * width, bytes_accessed=8 << 20, transcendentals=0),
        name="combine_cores",
    )(own.reshape(2, NZ, 192, width), other.reshape(2, NZ, 192, width), *pieces)


def pick_kernel(side, tiles, picked, sem):
    copies = [
        pltpu.make_async_copy(tiles.at[group, side[0]], picked.at[group], sem.at[group])
        for group in range(picked.shape[0])
    ]
    for copy in copies:
        copy.start()
    for copy in copies:
        copy.wait()


def pick(tiles, side):
    groups, _, slots, block, _ = tiles.shape
    return pl.pallas_call(
        pick_kernel,
        out_shape=jax.ShapeDtypeStruct((groups, slots, block, block), tiles.dtype),
        grid_spec=pltpu.PrefetchScalarGridSpec(
            num_scalar_prefetch=1,
            grid=(),
            in_specs=[pl.BlockSpec(memory_space=pl.ANY)],
            out_specs=pl.BlockSpec(memory_space=pl.ANY),
            scratch_shapes=[pltpu.SemaphoreType.DMA((groups,))],
        ),
        cost_estimate=pl.CostEstimate(flops=0, bytes_accessed=12 << 20, transcendentals=0),
        name="pick_tiles",
    )(side.reshape(1).astype(jnp.int32), tiles)


def products(tiles, received, chunks, places, counts, unit0, unit1, columns, here):
    groups, _, slots, block, _ = tiles.shape
    width = chunks[0].shape[-1]
    return pl.pallas_call(
        lambda *refs: products_kernel(places, *refs),
        out_shape=(
            jax.ShapeDtypeStruct((2 * NZ, 192, width), jnp.float32),
            jax.ShapeDtypeStruct((2 * NZ, 192, width), jnp.bfloat16),
        ),
        grid_spec=pltpu.PrefetchScalarGridSpec(
            num_scalar_prefetch=5,
            grid=(groups,),
            in_specs=[
                pl.BlockSpec((1, 1, slots, block, block), lambda g, n, u, v, k, here: (g, here[0], 0, 0, 0)),
                pl.BlockSpec((1, slots, block, block), lambda g, *_: (g, 0, 0, 0)),
            ] + [pl.BlockSpec(memory_space=pl.ANY)] * len(chunks),
            out_specs=(pl.BlockSpec((2 * NZ, 192, width), lambda g, *_: (0, 0, 0)),) * 2,
            scratch_shapes=[
                pltpu.VMEM((384, 64, width), jnp.bfloat16),
                pltpu.VMEM((48, block, width), jnp.float32),
                pltpu.SemaphoreType.DMA((len(chunks),)),
            ],
        ),
        compiler_params=pltpu.CompilerParams(vmem_limit_bytes=56 << 20),
        cost_estimate=pl.CostEstimate(flops=384 * 2 * block * block * width, bytes_accessed=30 << 20, transcendentals=0),
        name="tile_products",
    )(counts, unit0, unit1, columns, here, tiles, received, *chunks)


def body(out_grad, pre_act, features, weight, degrees, tiles, tile_rows, tile_cols):
    own_blk, own_rep = lax.axis_index("blk"), lax.axis_index("rep")
    core, y = own_blk % NC, (own_blk // NC) % NY
    x = (own_blk // (NC * NY)) * 2 + own_rep // NZ
    z = own_rep % NZ
    width = out_grad.shape[1]
    slots, block = tiles.shape[1], tiles.shape[2]
    groups = tiles.shape[0] // NC

    inverse_root = lax.rsqrt(degrees.astype(jnp.float32))
    active = (pre_act > 0).astype(jnp.float32)
    scaled = (out_grad.astype(jnp.float32) * active * inverse_root[:, None]).astype(jnp.bfloat16)

    rooted_features = (features.astype(jnp.float32) * inverse_root[:, None]).astype(jnp.bfloat16)

    odd = own_rep % 2
    full = lax.dynamic_slice_in_dim(scaled, odd * 64, 128, 0)
    half = lax.dynamic_slice_in_dim(scaled, (1 - odd) * 128, 64, 0)

    flip = other_core()
    by_parity = tiles.reshape(groups, NC, slots, block, block)
    codes = (tile_rows * 32 + tile_cols).reshape(groups, NC, slots)
    kept_codes = lax.dynamic_index_in_dim(codes, core, 1, keepdims=False)
    received_codes = send(lax.dynamic_index_in_dim(codes, 1 - core, 1, keepdims=False), flip)
    half_s = [half] + [send(half, along_s(-d)) for d in (1, 2, 3)]
    full_z = {1: send(full, along_z(-1)), 7: send(full, along_z(1))}
    far_features = send(rooted_features, across_x())
    *half_s, full, full_z[1], full_z[7], far_features, side = together(
        *half_s, full, full_z[1], full_z[7], far_features, 1 - core)
    picked = pick(by_parity, side)
    half_plane = jnp.stack(half_s)
    half_q = [half_plane] + [send(half_plane, along_q(-d)) for d in (1, 2, 3)]
    far_ahead = send(jnp.stack([full_z[7], full]), along_z(-3))
    far_behind = send(jnp.stack([full_z[7], full, full_z[1]]), along_z(3))
    full_line = jnp.concatenate(
        [jnp.stack([full, full_z[1]]), far_ahead, far_behind, full_z[7][None]])
    half_plane = jnp.concatenate(
        [part for part in half_q] + [rooted_features.reshape(-1, 64, width), far_features.reshape(-1, 64, width)])
    half_plane, full_line, picked = together(half_plane, full_line, picked)
    received = send(picked, flip)
    half_z = {0: [half_plane]}
    behind, ahead = ring_first(half_plane, along_z)
    half_z[7], half_z[1] = [behind], [ahead]
    full_q = {0: [full_line]}
    q_behind, q_ahead = ring_first(full_line, along_q)
    full_q[3], full_q[1], full_q[2] = [q_behind], [q_ahead], ring_last(q_behind, q_ahead, along_q)
    full_plane = stacked([full_q[d] for d in range(4)])
    full_plane, behind, ahead = together(full_plane, behind, ahead)
    full_s = {0: [full_plane]}
    s_behind, s_ahead = ring_first(full_plane, along_s)
    full_s[3], full_s[1], full_s[2] = [s_behind], [s_ahead], ring_last(s_behind, s_ahead, along_s)
    for d in (2, 3):
        behind, ahead = send(behind, along_z(1)), send(ahead, along_z(-1))
        half_z[NZ - d], half_z[d] = [behind], [ahead]
    half_z[4] = ring_last(behind, ahead, along_z)
    full_found = [full_s[d] for d in range(4)]
    half_found = [half_z[d] for d in range(NZ)]

    codes = jnp.stack([kept_codes, received_codes])
    rows, cols = codes // 32, codes % 32

    group = jnp.arange(groups)[None, :, None] * NC
    pair, kind = rows // 3, rows % 3
    source_x = (group // (NC * NY)) * 2 + (2 * pair) // NZ
    source_y = (group // NC) % NY
    ahead_x, ahead_y = (source_x - x) % NX, (source_y - y) % NY
    ahead_s = jnp.where(core == 0, ahead_x, ahead_y)
    ahead_q = jnp.where(core == 0, ahead_y, ahead_x)
    first_z, second_z = (2 * pair - z) % NZ, (2 * pair + 1 - z) % NZ
    full_unit = ((ahead_s * 4 + ahead_q) * NZ + jnp.where(kind == 0, first_z, second_z)) * 2
    half_unit = 256 + ahead_q * 4 + ahead_s
    split = kind == 1
    unit0 = jnp.where(split, half_unit + first_z * 16, full_unit).reshape(-1).astype(jnp.int32)
    unit1 = jnp.where(split, half_unit + second_z * 16, full_unit + 1).reshape(-1).astype(jnp.int32)
    columns = (cols + jnp.arange(2)[:, None, None] * 24).reshape(-1).astype(jnp.int32)
    last = jnp.max(jnp.where(codes != 0, jnp.arange(slots) + 1, 0), axis=2)
    counts = jnp.minimum(last + 1, slots).reshape(-1).astype(jnp.int32)

    chunks, places, at = [], [], 0
    for part in (piece for found in full_found for piece in found):
        chunks.append(part.reshape(-1, 64, width))
        places.append((at, chunks[-1].shape[0]))
        at += chunks[-1].shape[0]
    feature_pieces, feature_places = [], []
    for found in half_found:
        left = 16
        for piece in found:
            count = min(left, piece.shape[0])
            chunks.append(piece)
            places.append((at, count))
            at, left = at + count, left - count
            last_piece, last_count = piece, count
        feature_pieces.append(last_piece)
        feature_places.append(last_count)

    here = jnp.stack([core, own_rep // NZ, z]).astype(jnp.int32)
    own, other = products(by_parity, received, chunks, places, counts, unit0, unit1, columns, here)
    partial, local_weight = combine(own, send(other, flip), feature_pieces, feature_places)
    across = send(partial[1], across_x())
    own_rows = lax.all_to_all(local_weight, "rep", 0, 0, tiled=True).reshape(16, 16, width).sum(axis=0)
    line = (partial[0].astype(jnp.float32) + across.astype(jnp.float32)).astype(jnp.bfloat16)
    own_rows, line = together(own_rows, line)
    terms = [line[0]] + [send(line[d], along_z(d)) for d in range(1, NZ)]
    own_rows, terms[1] = together(own_rows, terms[1])
    spread = jnp.broadcast_to(own_rows[None], (16, 16, width)).reshape(256, width)
    own_rows = lax.all_to_all(spread, "blk", 0, 0, tiled=True).reshape(16, 16, width).sum(axis=0)
    spread = jnp.broadcast_to(own_rows[None], (16, 16, width)).reshape(256, width)
    weight_grad = lax.all_to_all(spread, "rep", 0, 0, tiled=True)

    summed = sum(term.astype(jnp.float32) for term in terms)
    propagated = (inverse_root[:, None] * summed).astype(jnp.bfloat16)
    input_grad = lax.dot_general(
        propagated, weight, (((1,), (1,)), ((), ())), preferred_element_type=jnp.float32
    ).astype(jnp.bfloat16)
    return (input_grad, weight_grad)


def solution(mesh):
    placed = (
        P(("blk", "rep"), None),
        P(("blk", "rep"), None),
        P(("blk", "rep"), None),
        P(),
        P(("blk", "rep")),
        P(("blk", "rep"), None, None, None),
        P(("blk", "rep"), None),
        P(("blk", "rep"), None),
    )
    return jax.shard_map(
        body, mesh=mesh, in_specs=placed, out_specs=(P(("blk", "rep"), None), P()), check_vma=False
    )
```

time: 276 us -> 413 us (1.50)
  Pallas kernels: 22.7 us -> 223 us
  blocking collectives: 73.2 us -> 37.1 us
  waiting for transfers between devices: 99.3 us -> 68 us
  starting transfers between devices: 51.8 us -> 65.6 us
  local copies, waits for them, and re-layouts: 20.7 us -> 12 us
    pallas_call x1 -> x3, Pallas kernels: 22.7 us -> 223 us  [the longest x1 192 us: pick(): pl.pallas_call(pick_kernel, out_shape=jax.ShapeDtypeStruct((groups, slots...]
    all_to_all x1 -> x0, blocking collectives: 44.6 us -> none  [body(): exchanged = lax.all_to_all(partial, 'rep', 0, 0, tiled=True)]
    ppermute x35 -> x38, waiting for transfers between devices: 90.2 us -> 68 us  [send(): return lax.ppermute(value, BOTH, moves)]
    ppermute x35 -> x38, starting transfers between devices: 47.4 us -> 58.2 us  [send(): return lax.ppermute(value, BOTH, moves)]
    all_to_all x1, waiting for transfers between devices: 9.07 us -> 0.01 us  [body(): weight_grad = lax.all_to_all(spread, 'rep', 0, 0, tiled=True)]
    squeeze x1 -> x2, local copies, waits for them, and re-layouts: 8.19 us -> 1.35 us  [the longest x1 1.3 us: body(): across = send(partial[1], across_x())]
    all_to_all x1, blocking collectives: 14.8 us -> 20.7 us  [body(): lax.all_to_all(local_weight, 'rep', 0, 0, tiled=True).reshape(16, 16, width)]
  transfers between devices with their start and end apart: 36 -> 39, of which waited for: 24 -> 18; matrix products, arithmetic and copies ran while one was open for 5% -> 2% of each run, Pallas kernels for 0% -> 46%
where the time goes in v2:
time: 413 us; the launch traced here: 412 us
  Pallas kernels  223 us (54%)
  waiting for transfers between devices  68 us (16%)
  starting transfers between devices  65.6 us (16%)
  blocking collectives  37.1 us (9%)
  local copies, waits for them, and re-layouts  12 us (3%)
  other arithmetic  4.95 us (1%)
    pallas_call x1, Pallas kernels, pick(): pl.pallas_call(pick_kernel, out_shape=jax.ShapeDtypeStruct((groups, slots...  192 us
    ppermute x38, waiting for transfers between devices, send(): return lax.ppermute(value, BOTH, moves)  68 us
    ppermute x38, starting transfers between devices, send(): return lax.ppermute(value, BOTH, moves)  58.2 us
    pallas_call x1, Pallas kernels, products(): pl.pallas_call(lambda *refs: products_kernel(places, *refs), out_shape=(j...  22.4 us
    all_to_all x1, blocking collectives, body(): lax.all_to_all(local_weight, 'rep', 0, 0, tiled=True).reshape(16, 16, width)  20.7 us
    all_to_all x1, blocking collectives, body(): lax.all_to_all(spread, 'blk', 0, 0, tiled=True).reshape(16, 16, width)  16.5 us
    pallas_call x1, Pallas kernels, combine(): pl.pallas_call(lambda *refs: combine_kernel(places, *refs), out_shape=(ja...  8.49 us
  transfers between devices with their start and end apart: 39, of which 18 were waited for; matrix products, arithmetic and copies ran while one was open for 2% of the time, Pallas kernels for 46%

profile of v2, /device:TPU:32, one launch (start us, length us, event | category | flops | bytes accessed | tf_op | source)
XLA Modules:
  0.0 412.4 jit_solution(1514099381141873552)
XLA Ops:
  2.5 2.8 collective-permute-start.1
  9.7 3.2 collective-permute-done.2
  14.8 3.1 collective-permute-start.7
  19.6 5.9 %collective-permute-start.10 = (bf16[2,128,256]{2,1,0:T(8,128)(2,1)S(1)}, bf16[2,128,256]{2,1,0:T(8,128)(2,1)S(1)}, u32[]{:S(2)}, u32[]{:S(2)}) collective-permute-start(bf16[2,128,256]{2,1,0:T(8,128)(2,1)S(1)} %pad_maximum_fusion.3), channel_id=1, source_target_pairs={{0,5},{16,21},{1,6},{17,22},{2,7},{18,23},{3,0},{19,16},{4,1},{20,... | collective-permute-start | bytes 393224 | tf_op jit(solution)/shard_map/ppermute | solution.py:49
  25.6 191.8 %pick_tiles.1 = bf16[8,24,128,128]{3,2,1,0:T(8,128)(2,1)} custom-call(s32[1]{0:T(128)} %bitcast.17.side, bf16[8,2,24,128,128]{4,3,2,1,0:T(8,128)(2,1)} %bitcast.65), custom_call_target="tpu_custom_call" | custom-call | bytes 12582912 | tf_op jit(solution)/shard_map/pick_tiles/pallas_call | solution.py:181
  222.3 4.7 %collective-permute-done.13 = bf16[8,128,256]{2,1,0:T(8,128)(2,1)S(1)} collective-permute-done((bf16[8,128,256]{2,1,0:T(8,128)(2,1)S(1)}, bf16[8,128,256]{2,1,0:T(8,128)(2,1)S(1)}, u32[]{:S(2)}, u32[]{:S(2)}) %collective-permute-start.13) | collective-permute-done | bytes 524320 | tf_op jit(solution)/shard_map/ppermute | solution.py:49
  227.0 3.7 collective-permute-start.16
  230.8 3.8 collective-permute-done.16
  234.6 3.8 collective-permute-done.15
  240.3 3.0 collective-permute-start.19
  243.2 2.4 collective-permute-start.23
  245.7 14.3 %collective-permute-done.23.refs_14_.refs_4_ = bf16[22,64,256]{2,1,0:T(8,128)(2,1)} collective-permute-done((bf16[22,64,256]{2,1,0:T(8,128)(2,1)}, bf16[22,64,256]{2,1,0:T(8,128)(2,1)}, u32[]{:S(2)}, u32[]{:S(2)}) %collective-permute-start.23) | collective-permute-done | bytes 720928 | tf_op jit(solution)/shard_map/ppermute | solution.py:49
  260.0 2.6 collective-permute-start.24
  263.1 4.2 %collective-permute-done.20 = bf16[4,8,128,256]{3,2,1,0:T(8,128)(2,1)} collective-permute-done((bf16[4,8,128,256]{3,2,1,0:T(8,128)(2,1)S(1)}, bf16[4,8,128,256]{3,2,1,0:T(8,128)(2,1)}, u32[]{:S(2)}, u32[]{:S(2)}) %collective-permute-start.20) | collective-permute-done | bytes 2097184 | tf_op jit(solution)/shard_map/ppermute | solution.py:49
  272.0 3.2 collective-permute-start.22
  276.5 3.4 collective-permute-done.26.refs_18_.refs_7_
  281.1 3.0 collective-permute-start.28
  285.4 4.1 collective-permute-done.27.refs_16_
  290.7 22.4 %tile_products.1 = (f32[16,192,256]{2,1,0:T(8,128)}, bf16[16,192,256]{2,1,0:T(8,128)(2,1)}) custom-call(s32[16]{0:T(128)} %min.8.refs_0_, s32[384]{0:T(512)} %get-tuple-element.60.refs_1_, s32[384]{0:T(512)} %get-tuple-element.59.refs_2_, s32[384]{0:T(512)} %get-tuple-element.61.refs_3_, s32[3]{0:T(128)} %pad_add_fusion.1.refs_4_, ...), custom_call_target="tpu_custom_call" | custom-call | flops 3221225472 | bytes 31457280 | tf_op jit(solution)/shard_map/tile_products/pallas_call | solution.py:199
  313.4 3.6 collective-permute-done.29
  318.2 8.5 %combine_cores.1 = (bf16[2,8,192,256]{3,2,1,0:T(8,128)(2,1)}, f32[256,256]{1,0:T(8,128)}) custom-call(f32[2,8,192,256]{3,2,1,0:T(8,128)} %bitcast.68, bf16[2,8,192,256]{3,2,1,0:T(8,128)(2,1)} %bitcast.69, bf16[22,64,256]{2,1,0:T(8,128)(2,1)} %copy-done.3, bf16[22,64,256]{2,1,0:T(8,128)(2,1)} %collective-permute-done.18.refs_13_.refs_3_, ...), custom_call_target="tpu_custom_call" | custom-call | flops 402653184 | bytes 8388608 | tf_op jit(solution)/shard_map/combine_cores/pallas_call | solution.py:149
  328.0 3.7 collective-permute-start.30
  331.7 20.7 %all_to_all.24 = f32[16,16,256]{2,1,0:T(8,128)S(1)} all-to-all(f32[16,16,256]{2,1,0:T(8,128)} %bitcast.81), channel_id=1, replica_groups=mesh['blk'=16,'rep'=16] {'rep'}, dimensions={0} | all-to-all | bytes 524288 | tf_op jit(solution)/shard_map/all_to_all | solution.py:324
  353.9 5.2 %collective-permute-done.31 = bf16[192,256]{1,0:T(8,128)(2,1)S(1)} collective-permute-done((bf16[192,256]{1,0:T(8,128)(2,1)S(1)}, bf16[192,256]{1,0:T(8,128)(2,1)S(1)}, u32[]{:S(2)}, u32[]{:S(2)}) %collective-permute-start.31) | collective-permute-done | bytes 98336 | tf_op jit(solution)/shard_map/ppermute | solution.py:49
  359.1 16.5 %all_to_all.25 = f32[16,16,256]{2,1,0:T(8,128)S(1)} all-to-all(f32[16,16,256]{2,1,0:T(8,128)S(1)} %broadcast_in_dim.29), channel_id=1, replica_groups=mesh['blk'=16,'rep'=16] {'blk'}, dimensions={0} | all-to-all | bytes 524288 | tf_op jit(solution)/shard_map/all_to_all | solution.py:330
  376.4 7.4 %all-to-all-start.2 = ((f32[16,16,256]{2,1,0:T(8,128)}), f32[16,16,256]{2,1,0:T(8,128)S(1)}, u32[]{:S(2)}, u32[]{:S(2)}) async-start(f32[16,16,256]{2,1,0:T(8,128)} %broadcast_in_dim.44), calls=%async_computation.2 | async-start | bytes 524288 | tf_op jit(solution)/shard_map/all_to_all | solution.py:332
  384.0 4.0 collective-permute-start.36
  387.9 2.4 collective-permute-start.35
  390.3 2.7 collective-permute-start.34
  398.1 2.4 collective-permute-done.36
  400.6 5.8 %collective-permute-done.35 = bf16[192,256]{1,0:T(8,128)(2,1)S(1)} collective-permute-done((bf16[192,256]{1,0:T(8,128)(2,1)S(1)}, bf16[192,256]{1,0:T(8,128)(2,1)S(1)}, u32[]{:S(2)}, u32[]{:S(2)}) %collective-permute-start.35) | collective-permute-done | bytes 98336 | tf_op jit(solution)/shard_map/ppermute | solution.py:49
  406.4 4.4 %collective-permute-done.34 = bf16[192,256]{1,0:T(8,128)(2,1)S(1)} collective-permute-done((bf16[192,256]{1,0:T(8,128)(2,1)S(1)}, bf16[192,256]{1,0:T(8,128)(2,1)S(1)}, u32[]{:S(2)}, u32[]{:S(2)}) %collective-permute-start.34) | collective-permute-done | bytes 98336 | tf_op jit(solution)/shard_map/ppermute | solution.py:49
  (126 shorter events, 38.6 us)
Async XLA Ops:
  5.3 9.5 %collective-permute-start.6 = (bf16[192,256]{1,0:T(8,128)(2,1)S(1)}, bf16[192,256]{1,0:T(8,128)(2,1)S(1)}, u32[]{:S(2)}, u32[]{:S(2)}) collective-permute-start(bf16[192,256]{1,0:T(8,128)(2,1)S(1)} %get-tuple-element.62), channel_id=1, source_target_pairs={{0,8},{16,24},{1,9},{17,25},{2,10},{18,26},{3,11},{19,27},{4,12},{... | collective-permute-start | bytes 294920 | tf_op jit(solution)/shard_map/ppermute | solution.py:49
  5.3 9.4 %collective-permute-start.4 = (bf16[128,256]{1,0:T(8,128)(2,1)S(1)}, bf16[128,256]{1,0:T(8,128)(2,1)S(1)}, u32[]{:S(2)}, u32[]{:S(2)}) collective-permute-start(bf16[128,256]{1,0:T(8,128)(2,1)S(1)} %constant_dynamic-slice_fusion), channel_id=1, source_target_pairs={{0,7},{16,23},{1,0},{17,16},{2,1},{18,17},{3,2},{19,18},{4,3},{20,... | collective-permute-start | bytes 196616 | tf_op jit(solution)/shard_map/ppermute | solution.py:49
  6.4 8.3 %collective-permute-start.5 = (bf16[128,256]{1,0:T(8,128)(2,1)S(1)}, bf16[128,256]{1,0:T(8,128)(2,1)S(1)}, u32[]{:S(2)}, u32[]{:S(2)}) collective-permute-start(bf16[128,256]{1,0:T(8,128)(2,1)S(1)} %constant_dynamic-slice_fusion), channel_id=1, source_target_pairs={{0,1},{16,17},{1,2},{17,18},{2,3},{18,19},{3,4},{19,20},{4,5},{20,... | collective-permute-start | bytes 196616 | tf_op jit(solution)/shard_map/ppermute | solution.py:49
  14.8 202.6 %collective-permute-start.7 = (bf16[4,64,256]{2,1,0:T(8,128)(2,1)S(1)}, bf16[4,64,256]{2,1,0:T(8,128)(2,1)S(1)}, u32[]{:S(2)}, u32[]{:S(2)}) collective-permute-start(bf16[4,64,256]{2,1,0:T(8,128)(2,1)S(1)} %pad_maximum_fusion.2), channel_id=1, source_target_pairs={{0,96},{16,152},{1,97},{17,153},{2,98},{18,154},{3,99},{19,155},{4... | collective-permute-start | bytes 393224 | tf_op jit(solution)/shard_map/ppermute | solution.py:49
  17.9 199.5 %collective-permute-start.8 = (bf16[4,64,256]{2,1,0:T(8,128)(2,1)S(1)}, bf16[4,64,256]{2,1,0:T(8,128)(2,1)S(1)}, u32[]{:S(2)}, u32[]{:S(2)}) collective-permute-start(bf16[4,64,256]{2,1,0:T(8,128)(2,1)S(1)} %pad_maximum_fusion.2), channel_id=1, source_target_pairs={{0,64},{16,144},{1,65},{17,145},{2,66},{18,146},{3,67},{19,147},{4... | collective-permute-start | bytes 393224 | tf_op jit(solution)/shard_map/ppermute | solution.py:49
  18.6 198.9 %collective-permute-start.9 = (bf16[4,64,256]{2,1,0:T(8,128)(2,1)S(1)}, bf16[4,64,256]{2,1,0:T(8,128)(2,1)S(1)}, u32[]{:S(2)}, u32[]{:S(2)}) collective-permute-start(bf16[4,64,256]{2,1,0:T(8,128)(2,1)S(1)} %pad_maximum_fusion.2), channel_id=1, source_target_pairs={{0,32},{16,24},{1,33},{17,25},{2,34},{18,26},{3,35},{19,27},{4,36}... | collective-permute-start | bytes 393224 | tf_op jit(solution)/shard_map/ppermute | solution.py:49
  19.6 198.0 %collective-permute-start.10 = (bf16[2,128,256]{2,1,0:T(8,128)(2,1)S(1)}, bf16[2,128,256]{2,1,0:T(8,128)(2,1)S(1)}, u32[]{:S(2)}, u32[]{:S(2)}) collective-permute-start(bf16[2,128,256]{2,1,0:T(8,128)(2,1)S(1)} %pad_maximum_fusion.3), channel_id=1, source_target_pairs={{0,5},{16,21},{1,6},{17,22},{2,7},{18,23},{3,0},{19,16},{4,1},{20,... | collective-permute-start | bytes 393224 | tf_op jit(solution)/shard_map/ppermute | solution.py:49
  25.5 192.0 %collective-permute-start.11 = (bf16[3,128,256]{2,1,0:T(8,128)(2,1)S(1)}, bf16[3,128,256]{2,1,0:T(8,128)(2,1)S(1)}, u32[]{:S(2)}, u32[]{:S(2)}) collective-permute-start(bf16[3,128,256]{2,1,0:T(8,128)(2,1)S(1)} %pad_maximum_fusion.1), channel_id=1, source_target_pairs={{0,3},{16,19},{1,4},{17,20},{2,5},{18,21},{3,6},{19,22},{4,7},{20,... | collective-permute-start | bytes 589832 | tf_op jit(solution)/shard_map/ppermute | solution.py:49
  217.6 72.1 %collective-permute-start.12 = (bf16[8,24,128,128]{3,2,1,0:T(8,128)(2,1)}, bf16[8,24,128,128]{3,2,1,0:T(8,128)(2,1)}, u32[]{:S(2)}, u32[]{:S(2)}) collective-permute-start(bf16[8,24,128,128]{3,2,1,0:T(8,128)(2,1)} %pick_tiles.1), channel_id=1, source_target_pairs={{0,16},{16,0},{1,17},{17,1},{2,18},{18,2},{3,19},{19,3},{4,20},{20... | collective-permute-start | bytes 18874376 | tf_op jit(solution)/shard_map/ppermute | solution.py:49
  217.7 9.3 %collective-permute-start.13 = (bf16[8,128,256]{2,1,0:T(8,128)(2,1)S(1)}, bf16[8,128,256]{2,1,0:T(8,128)(2,1)S(1)}, u32[]{:S(2)}, u32[]{:S(2)}) collective-permute-start(bf16[8,128,256]{2,1,0:T(8,128)(2,1)S(1)} %constant_dynamic-update-slice_fusion.9), channel_id=1, source_target_pairs={{0,96},{16,152},{1,97},{17,153},{2,98},{18,154},{3,99},{19,155},{4... | collective-permute-start | bytes 1572872 | tf_op jit(solution)/shard_map/ppermute | solution.py:49
  220.0 10.7 %collective-permute-start.14 = (bf16[8,128,256]{2,1,0:T(8,128)(2,1)S(1)}, bf16[8,128,256]{2,1,0:T(8,128)(2,1)S(1)}, u32[]{:S(2)}, u32[]{:S(2)}) collective-permute-start(bf16[8,128,256]{2,1,0:T(8,128)(2,1)S(1)} %constant_dynamic-update-slice_fusion.9), channel_id=1, source_target_pairs={{0,32},{16,24},{1,33},{17,25},{2,34},{18,26},{3,35},{19,27},{4,36}... | collective-permute-start | bytes 1572872 | tf_op jit(solution)/shard_map/ppermute | solution.py:49
  220.0 18.7 %collective-permute-start.17 = (bf16[22,64,256]{2,1,0:T(8,128)(2,1)S(1)}, bf16[22,64,256]{2,1,0:T(8,128)(2,1)}, u32[]{:S(2)}, u32[]{:S(2)}) collective-permute-start(bf16[22,64,256]{2,1,0:T(8,128)(2,1)S(1)} %constant_dynamic-update-slice_fusion.refs_12_.refs_2_), channel_id=1, source_target_pairs={{0,1},{16,17},{1,2},{17,18},{2,3},{18,19},{3,4},{19,20},{4,5},{20,... | collective-permute-start | bytes 2162696 | tf_op jit(solution)/shard_map/ppermute | solution.py:49
  222.3 17.7 %collective-permute-start.18 = (bf16[22,64,256]{2,1,0:T(8,128)(2,1)S(1)}, bf16[22,64,256]{2,1,0:T(8,128)(2,1)}, u32[]{:S(2)}, u32[]{:S(2)}) collective-permute-start(bf16[22,64,256]{2,1,0:T(8,128)(2,1)S(1)} %constant_dynamic-update-slice_fusion.refs_12_.refs_2_), channel_id=1, source_target_pairs={{0,7},{16,23},{1,0},{17,16},{2,1},{18,17},{3,2},{19,18},{4,3},{20,... | collective-permute-start | bytes 2162696 | tf_op jit(solution)/shard_map/ppermute | solution.py:49
  230.7 7.7 %collective-permute-start.15 = (bf16[4,128,256]{2,1,0:T(8,128)(2,1)S(1)}, bf16[4,128,256]{2,1,0:T(8,128)(2,1)S(1)}, u32[]{:S(2)}, u32[]{:S(2)}) collective-permute-start(bf16[4,128,256]{2,1,0:T(8,128)(2,1)S(1)} %slice.64), channel_id=1, source_target_pairs={{0,32},{16,24},{1,33},{17,25},{2,34},{18,26},{3,35},{19,27},{4,36}... | collective-permute-start | bytes 786440 | tf_op jit(solution)/shard_map/ppermute | solution.py:49
  240.0 27.4 %collective-permute-start.20 = (bf16[4,8,128,256]{3,2,1,0:T(8,128)(2,1)S(1)}, bf16[4,8,128,256]{3,2,1,0:T(8,128)(2,1)}, u32[]{:S(2)}, u32[]{:S(2)}) collective-permute-start(bf16[4,8,128,256]{3,2,1,0:T(8,128)(2,1)S(1)} %pad_maximum_fusion), channel_id=1, source_target_pairs={{0,8},{16,48},{1,9},{17,49},{2,10},{18,50},{3,11},{19,51},{4,12},{... | collective-permute-start | bytes 6291464 | tf_op jit(solution)/shard_map/ppermute | solution.py:49
  240.3 29.4 %collective-permute-start.19 = (bf16[4,8,128,256]{3,2,1,0:T(8,128)(2,1)S(1)}, bf16[4,8,128,256]{3,2,1,0:T(8,128)(2,1)}, u32[]{:S(2)}, u32[]{:S(2)}) collective-permute-start(bf16[4,8,128,256]{3,2,1,0:T(8,128)(2,1)S(1)} %pad_maximum_fusion), channel_id=1, source_target_pairs={{0,136},{16,112},{1,137},{17,113},{2,138},{18,114},{3,139},{19,115... | collective-permute-start | bytes 6291464 | tf_op jit(solution)/shard_map/ppermute | solution.py:49
  243.2 16.8 %collective-permute-start.23 = (bf16[22,64,256]{2,1,0:T(8,128)(2,1)}, bf16[22,64,256]{2,1,0:T(8,128)(2,1)}, u32[]{:S(2)}, u32[]{:S(2)}) collective-permute-start(bf16[22,64,256]{2,1,0:T(8,128)(2,1)} %collective-permute-done.18.refs_13_.refs_3_), channel_id=1, source_target_pairs={{0,7},{16,23},{1,0},{17,16},{2,1},{18,17},{3,2},{19,18},{4,3},{20,... | collective-permute-start | bytes 2162696 | tf_op jit(solution)/shard_map/ppermute | solution.py:49
  245.7 17.4 %collective-permute-start.25 = (bf16[22,64,256]{2,1,0:T(8,128)(2,1)}, bf16[22,64,256]{2,1,0:T(8,128)(2,1)}, u32[]{:S(2)}, u32[]{:S(2)}) collective-permute-start(bf16[22,64,256]{2,1,0:T(8,128)(2,1)} %collective-permute-done.17.refs_20_.refs_9_), channel_id=1, source_target_pairs={{0,1},{16,17},{1,2},{17,18},{2,3},{18,19},{3,4},{19,20},{4,5},{20,... | collective-permute-start | bytes 2162696 | tf_op jit(solution)/shard_map/ppermute | solution.py:49
  260.0 21.0 %collective-permute-start.24 = (bf16[22,64,256]{2,1,0:T(8,128)(2,1)}, bf16[22,64,256]{2,1,0:T(8,128)(2,1)S(1)}, u32[]{:S(2)}, u32[]{:S(2)}) collective-permute-start(bf16[22,64,256]{2,1,0:T(8,128)(2,1)} %collective-permute-done.23.refs_14_.refs_4_), channel_id=1, source_target_pairs={{0,7},{16,23},{1,0},{17,16},{2,1},{18,17},{3,2},{19,18},{4,3},{20,... | collective-permute-start | bytes 2162696 | tf_op jit(solution)/shard_map/ppermute | solution.py:49
  263.1 16.8 %collective-permute-start.26 = (bf16[22,64,256]{2,1,0:T(8,128)(2,1)}, bf16[22,64,256]{2,1,0:T(8,128)(2,1)}, u32[]{:S(2)}, u32[]{:S(2)}) collective-permute-start(bf16[22,64,256]{2,1,0:T(8,128)(2,1)} %collective-permute-done.25.refs_19_.refs_8_), channel_id=1, source_target_pairs={{0,1},{16,17},{1,2},{17,18},{2,3},{18,19},{3,4},{19,20},{4,5},{20,... | collective-permute-start | bytes 2162696 | tf_op jit(solution)/shard_map/ppermute | solution.py:49
  269.6 20.0 %collective-permute-start.21 = (bf16[2,8,128,256]{3,2,1,0:T(8,128)(2,1)}, bf16[2,8,128,256]{3,2,1,0:T(8,128)(2,1)}, u32[]{:S(2)}, u32[]{:S(2)}) collective-permute-start(bf16[2,8,128,256]{3,2,1,0:T(8,128)(2,1)} %slice.66), channel_id=1, source_target_pairs={{0,8},{16,48},{1,9},{17,49},{2,10},{18,50},{3,11},{19,51},{4,12},{... | collective-permute-start | bytes 3145736 | tf_op jit(solution)/shard_map/ppermute | solution.py:49
  272.0 17.7 %collective-permute-start.22 = (bf16[2,8,128,256]{3,2,1,0:T(8,128)(2,1)}, bf16[2,8,128,256]{3,2,1,0:T(8,128)(2,1)S(1)}, u32[]{:S(2)}, u32[]{:S(2)}) collective-permute-start(bf16[2,8,128,256]{3,2,1,0:T(8,128)(2,1)} %slice.67), channel_id=1, source_target_pairs={{0,136},{16,112},{1,137},{17,113},{2,138},{18,114},{3,139},{19,115... | collective-permute-start | bytes 3145736 | tf_op jit(solution)/shard_map/ppermute | solution.py:49
  280.9 8.5 %collective-permute-start.27 = (bf16[11,64,256]{2,1,0:T(8,128)(2,1)S(1)}, bf16[11,64,256]{2,1,0:T(8,128)(2,1)}, u32[]{:S(2)}, u32[]{:S(2)}) collective-permute-start(bf16[11,64,256]{2,1,0:T(8,128)(2,1)S(1)} %slice.68), channel_id=1, source_target_pairs={{0,1},{16,17},{1,2},{17,18},{2,3},{18,19},{3,4},{19,20},{4,5},{20,... | collective-permute-start | bytes 1081352 | tf_op jit(solution)/shard_map/ppermute | solution.py:49
  281.1 8.6 %collective-permute-start.28 = (bf16[11,64,256]{2,1,0:T(8,128)(2,1)S(1)}, bf16[11,64,256]{2,1,0:T(8,128)(2,1)S(1)}, u32[]{:S(2)}, u32[]{:S(2)}) collective-permute-start(bf16[11,64,256]{2,1,0:T(8,128)(2,1)S(1)} %slice.69), channel_id=1, source_target_pairs={{0,7},{16,23},{1,0},{17,16},{2,1},{18,17},{3,2},{19,18},{4,3},{20,... | collective-permute-start | bytes 1081352 | tf_op jit(solution)/shard_map/ppermute | solution.py:49
  328.0 24.4 %collective-permute-start.30 = (bf16[8,192,256]{2,1,0:T(8,128)(2,1)S(1)}, bf16[8,192,256]{2,1,0:T(8,128)(2,1)}, u32[]{:S(2)}, u32[]{:S(2)}) collective-permute-start(bf16[8,192,256]{2,1,0:T(8,128)(2,1)S(1)} %slice_bitcast_fusion), channel_id=1, source_target_pairs={{0,8},{16,24},{1,9},{17,25},{2,10},{18,26},{3,11},{19,27},{4,12},{... | collective-permute-start | bytes 2359304 | tf_op jit(solution)/shard_map/ppermute | solution.py:49
  376.4 35.3 %all-to-all-start.2 = ((f32[16,16,256]{2,1,0:T(8,128)}), f32[16,16,256]{2,1,0:T(8,128)S(1)}, u32[]{:S(2)}, u32[]{:S(2)}) async-start(f32[16,16,256]{2,1,0:T(8,128)} %broadcast_in_dim.44), calls=%async_computation.2 | async-start | bytes 524288 | tf_op jit(solution)/shard_map/all_to_all | solution.py:332
  383.8 12.8 %collective-permute-start.37 = (bf16[192,256]{1,0:T(8,128)(2,1)S(1)}, bf16[192,256]{1,0:T(8,128)(2,1)S(1)}, u32[]{:S(2)}, u32[]{:S(2)}) collective-permute-start(bf16[192,256]{1,0:T(8,128)(2,1)S(1)} %get-tuple-element.49), channel_id=1, source_target_pairs={{0,7},{16,23},{1,0},{17,16},{2,1},{18,17},{3,2},{19,18},{4,3},{20,... | collective-permute-start | bytes 294920 | tf_op jit(solution)/shard_map/ppermute | solution.py:49
  384.0 16.6 %collective-permute-start.36 = (bf16[192,256]{1,0:T(8,128)(2,1)S(1)}, bf16[192,256]{1,0:T(8,128)(2,1)S(1)}, u32[]{:S(2)}, u32[]{:S(2)}) collective-permute-start(bf16[192,256]{1,0:T(8,128)(2,1)S(1)} %get-tuple-element.50), channel_id=1, source_target_pairs={{0,6},{16,22},{1,7},{17,23},{2,0},{18,16},{3,1},{19,17},{4,2},{20,... | collective-permute-start | bytes 294920 | tf_op jit(solution)/shard_map/ppermute | solution.py:49
  387.9 18.5 %collective-permute-start.35 = (bf16[192,256]{1,0:T(8,128)(2,1)S(1)}, bf16[192,256]{1,0:T(8,128)(2,1)S(1)}, u32[]{:S(2)}, u32[]{:S(2)}) collective-permute-start(bf16[192,256]{1,0:T(8,128)(2,1)S(1)} %get-tuple-element.51), channel_id=1, source_target_pairs={{0,5},{16,21},{1,6},{17,22},{2,7},{18,23},{3,0},{19,16},{4,1},{20,... | collective-permute-start | bytes 294920 | tf_op jit(solution)/shard_map/ppermute | solution.py:49
  390.3 20.5 %collective-permute-start.34 = (bf16[192,256]{1,0:T(8,128)(2,1)S(1)}, bf16[192,256]{1,0:T(8,128)(2,1)S(1)}, u32[]{:S(2)}, u32[]{:S(2)}) collective-permute-start(bf16[192,256]{1,0:T(8,128)(2,1)S(1)} %get-tuple-element.52), channel_id=1, source_target_pairs={{0,4},{16,20},{1,5},{17,21},{2,6},{18,22},{3,7},{19,23},{4,0},{20,... | collective-permute-start | bytes 294920 | tf_op jit(solution)/shard_map/ppermute | solution.py:49
  393.0 17.8 %collective-permute-start.33 = (bf16[192,256]{1,0:T(8,128)(2,1)S(1)}, bf16[192,256]{1,0:T(8,128)(2,1)S(1)}, u32[]{:S(2)}, u32[]{:S(2)}) collective-permute-start(bf16[192,256]{1,0:T(8,128)(2,1)S(1)} %get-tuple-element.53), channel_id=1, source_target_pairs={{0,3},{16,19},{1,4},{17,20},{2,5},{18,21},{3,6},{19,22},{4,7},{20,... | collective-permute-start | bytes 294920 | tf_op jit(solution)/shard_map/ppermute | solution.py:49
  396.6 14.2 %collective-permute-start.32 = (bf16[192,256]{1,0:T(8,128)(2,1)S(1)}, bf16[192,256]{1,0:T(8,128)(2,1)S(1)}, u32[]{:S(2)}, u32[]{:S(2)}) collective-permute-start(bf16[192,256]{1,0:T(8,128)(2,1)S(1)} %get-tuple-element.54), channel_id=1, source_target_pairs={{0,2},{16,18},{1,3},{17,19},{2,4},{18,20},{3,5},{19,21},{4,6},{20,... | collective-permute-start | bytes 294920 | tf_op jit(solution)/shard_map/ppermute | solution.py:49
  (17 other events, 555.6 us)

commit v3 on v2

--- a/solution.py
+++ b/solution.py
@@ -35,6 +35,24 @@
 
 def along_s(step):
     return pairs(lambda x, y, z, core: (x + step * (1 - core), y + step * core, z, core))
+
+
+def spread_over(value, places):
+    count = len(places[0])
+    copies = jnp.broadcast_to(value[None], (count, *value.shape))
+    return lax.all_to_all(copies, BOTH, 0, 0, axis_index_groups=places, tiled=True)
+
+
+def z_lines():
+    return [[flat_index(x, y, z, c) for z in range(NZ)] for x in range(NX) for y in range(NY) for c in range(NC)]
+
+
+def opposite_x():
+    return pairs(lambda x, y, z, core: (x + 2, y, z, core))
+
+
+def paired_y(bit):
+    return pairs(lambda x, y, z, core: (x, y ^ bit, z, core))
 
 
 def across_x():
@@ -105,19 +123,12 @@
 
     @pl.when(step == pl.num_programs(0) - 1)
     def _():
-        for rep in range(2 * NZ):
-            place = lax.bitwise_xor(rep // NZ, here[1]) * NZ + lax.rem(rep % NZ - here[2] + NZ, NZ)
-            for out, side in ((own_out, 0), (other_out, 24)):
-                tile = side + 3 * rep // 2
-                if rep % 2 == 0:
-                    out[place, :128] = totals[tile].astype(out.dtype)
-                    out[place, 128:] = totals[tile + 1, :64].astype(out.dtype)
-                else:
-                    out[place, :64] = totals[tile, 64:].astype(out.dtype)
-                    out[place, 64:] = totals[tile + 1].astype(out.dtype)
-
-
-def combine_kernel(places, own, other, *rest):
+        half = own_out.shape[0]
+        own_out[...] = totals[:half]
+        other_out[...] = totals[half:].astype(other_out.dtype)
+
+
+def combine_kernel(places, here, own, other, *rest):
     pieces = rest[: len(places)]
     partial, gradient, features, sem = rest[len(places):]
     step = pl.program_id(0)
@@ -135,17 +146,19 @@
             copy.wait()
 
     total = gradient[...]
-    for near in range(2):
-        rows = (own[near, 0] + other[near, 0].astype(jnp.float32)).astype(partial.dtype)
-        partial[near, 0] = rows
-        lanes = jnp.concatenate([features[step, 3 * near + n] for n in range(3)], axis=0)
+    ahead = lax.rem(step - here[2] + NZ, NZ)
+    for low in range(2):
+        rows = (own[low, 0] + other[low, 0].astype(jnp.float32)).astype(partial.dtype)
+        partial[low, 0] = rows
+        near = lax.bitwise_xor(low, here[1])
+        lanes = jnp.concatenate([features[ahead, 3 * near + n] for n in range(3)], axis=0)
         total += lax.dot_general(lanes, rows, (((0,), (0,)), ((), ())), preferred_element_type=jnp.float32)
     gradient[...] = total
 
 
-def combine(own, other, pieces, places):
+def combine(own, other, pieces, places, here):
     width = own.shape[-1]
-    block = pl.BlockSpec((2, 1, 192, width), lambda d: (0, d, 0, 0))
+    block = pl.BlockSpec((2, 1, 192, width), lambda d, here: (0, d, 0, 0))
     return pl.pallas_call(
         lambda *refs: combine_kernel(places, *refs),
         out_shape=(
@@ -153,27 +166,20 @@
             jax.ShapeDtypeStruct((width, width), jnp.float32),
         ),
         grid_spec=pltpu.PrefetchScalarGridSpec(
-            num_scalar_prefetch=0,
+            num_scalar_prefetch=1,
             grid=(NZ,),
             in_specs=[block, block] + [pl.BlockSpec(memory_space=pl.ANY)] * NZ,
-            out_specs=(block, pl.BlockSpec((width, width), lambda d: (0, 0))),
+            out_specs=(block, pl.BlockSpec((width, width), lambda d, here: (0, 0))),
             scratch_shapes=[pltpu.VMEM((NZ, 6, 64, width), jnp.bfloat16), pltpu.SemaphoreType.DMA((NZ,))],
         ),
         compiler_params=pltpu.CompilerParams(vmem_limit_bytes=56 << 20),
         cost_estimate=pl.CostEstimate(flops=2 * 3072 * width * width, bytes_accessed=8 << 20, transcendentals=0),
         name="combine_cores",
-    )(own.reshape(2, NZ, 192, width), other.reshape(2, NZ, 192, width), *pieces)
-
-
-def pick_kernel(side, tiles, picked, sem):
-    copies = [
-        pltpu.make_async_copy(tiles.at[group, side[0]], picked.at[group], sem.at[group])
-        for group in range(picked.shape[0])
-    ]
-    for copy in copies:
-        copy.start()
-    for copy in copies:
-        copy.wait()
+    )(here, own.reshape(2, NZ, 192, width), other.reshape(2, NZ, 192, width), *pieces)
+
+
+def pick_kernel(side, tiles, picked):
+    picked[...] = tiles[:, 0]
 
 
 def pick(tiles, side):
@@ -183,10 +189,9 @@
         out_shape=jax.ShapeDtypeStruct((groups, slots, block, block), tiles.dtype),
         grid_spec=pltpu.PrefetchScalarGridSpec(
             num_scalar_prefetch=1,
-            grid=(),
-            in_specs=[pl.BlockSpec(memory_space=pl.ANY)],
-            out_specs=pl.BlockSpec(memory_space=pl.ANY),
-            scratch_shapes=[pltpu.SemaphoreType.DMA((groups,))],
+            grid=(groups,),
+            in_specs=[pl.BlockSpec((1, 1, slots, block, block), lambda g, side: (g, side[0], 0, 0, 0))],
+            out_specs=pl.BlockSpec((1, slots, block, block), lambda g, side: (g, 0, 0, 0)),
         ),
         cost_estimate=pl.CostEstimate(flops=0, bytes_accessed=12 << 20, transcendentals=0),
         name="pick_tiles",
@@ -199,8 +204,8 @@
     return pl.pallas_call(
         lambda *refs: products_kernel(places, *refs),
         out_shape=(
-            jax.ShapeDtypeStruct((2 * NZ, 192, width), jnp.float32),
-            jax.ShapeDtypeStruct((2 * NZ, 192, width), jnp.bfloat16),
+            jax.ShapeDtypeStruct((24, block, width), jnp.float32),
+            jax.ShapeDtypeStruct((24, block, width), jnp.bfloat16),
         ),
         grid_spec=pltpu.PrefetchScalarGridSpec(
             num_scalar_prefetch=5,
@@ -209,7 +214,7 @@
                 pl.BlockSpec((1, 1, slots, block, block), lambda g, n, u, v, k, here: (g, here[0], 0, 0, 0)),
                 pl.BlockSpec((1, slots, block, block), lambda g, *_: (g, 0, 0, 0)),
             ] + [pl.BlockSpec(memory_space=pl.ANY)] * len(chunks),
-            out_specs=(pl.BlockSpec((2 * NZ, 192, width), lambda g, *_: (0, 0, 0)),) * 2,
+            out_specs=(pl.BlockSpec((24, block, width), lambda g, *_: (0, 0, 0)),) * 2,
             scratch_shapes=[
                 pltpu.VMEM((384, 64, width), jnp.bfloat16),
                 pltpu.VMEM((48, block, width), jnp.float32),
@@ -246,20 +251,13 @@
     codes = (tile_rows * 32 + tile_cols).reshape(groups, NC, slots)
     kept_codes = lax.dynamic_index_in_dim(codes, core, 1, keepdims=False)
     received_codes = send(lax.dynamic_index_in_dim(codes, 1 - core, 1, keepdims=False), flip)
-    half_s = [half] + [send(half, along_s(-d)) for d in (1, 2, 3)]
-    full_z = {1: send(full, along_z(-1)), 7: send(full, along_z(1))}
     far_features = send(rooted_features, across_x())
-    *half_s, full, full_z[1], full_z[7], far_features, side = together(
-        *half_s, full, full_z[1], full_z[7], far_features, 1 - core)
-    picked = pick(by_parity, side)
-    half_plane = jnp.stack(half_s)
-    half_q = [half_plane] + [send(half_plane, along_q(-d)) for d in (1, 2, 3)]
-    far_ahead = send(jnp.stack([full_z[7], full]), along_z(-3))
-    far_behind = send(jnp.stack([full_z[7], full, full_z[1]]), along_z(3))
-    full_line = jnp.concatenate(
-        [jnp.stack([full, full_z[1]]), far_ahead, far_behind, full_z[7][None]])
+    full_line = spread_over(full, z_lines())
+    half_line = jnp.stack([half] + [send(half, along_s(-d)) for d in (1, 2, 3)])
+    half_q = [half_line] + [send(half_line, along_q(-d)) for d in (1, 2, 3)]
+    picked = pick(by_parity, 1 - core)
     half_plane = jnp.concatenate(
-        [part for part in half_q] + [rooted_features.reshape(-1, 64, width), far_features.reshape(-1, 64, width)])
+        half_q + [rooted_features.reshape(-1, 64, width), far_features.reshape(-1, 64, width)])
     half_plane, full_line, picked = together(half_plane, full_line, picked)
     received = send(picked, flip)
     half_z = {0: [half_plane]}
@@ -291,7 +289,7 @@
     ahead_s = jnp.where(core == 0, ahead_x, ahead_y)
     ahead_q = jnp.where(core == 0, ahead_y, ahead_x)
     first_z, second_z = (2 * pair - z) % NZ, (2 * pair + 1 - z) % NZ
-    full_unit = ((ahead_s * 4 + ahead_q) * NZ + jnp.where(kind == 0, first_z, second_z)) * 2
+    full_unit = ((ahead_s * 4 + ahead_q) * NZ + (2 * pair + kind // 2) % NZ) * 2
     half_unit = 256 + ahead_q * 4 + ahead_s
     split = kind == 1
     unit0 = jnp.where(split, half_unit + first_z * 16, full_unit).reshape(-1).astype(jnp.int32)
@@ -319,19 +317,20 @@
 
     here = jnp.stack([core, own_rep // NZ, z]).astype(jnp.int32)
     own, other = products(by_parity, received, chunks, places, counts, unit0, unit1, columns, here)
-    partial, local_weight = combine(own, send(other, flip), feature_pieces, feature_places)
-    across = send(partial[1], across_x())
+    partial, local_weight = combine(own, send(other, flip), feature_pieces, feature_places, here)
+    near = lax.dynamic_index_in_dim(partial, own_rep // NZ, 0, keepdims=False)
+    across = send(lax.dynamic_index_in_dim(partial, 1 - own_rep // NZ, 0, keepdims=False), across_x())
     own_rows = lax.all_to_all(local_weight, "rep", 0, 0, tiled=True).reshape(16, 16, width).sum(axis=0)
-    line = (partial[0].astype(jnp.float32) + across.astype(jnp.float32)).astype(jnp.bfloat16)
-    own_rows, line = together(own_rows, line)
-    terms = [line[0]] + [send(line[d], along_z(d)) for d in range(1, NZ)]
-    own_rows, terms[1] = together(own_rows, terms[1])
-    spread = jnp.broadcast_to(own_rows[None], (16, 16, width)).reshape(256, width)
-    own_rows = lax.all_to_all(spread, "blk", 0, 0, tiled=True).reshape(16, 16, width).sum(axis=0)
+    line = (near.astype(jnp.float32) + across.astype(jnp.float32)).astype(jnp.bfloat16)
+    line, own_rows = together(line, own_rows)
+    terms = lax.all_to_all(line, BOTH, 0, 0, axis_index_groups=z_lines(), tiled=True)
+    for partner in (other_core(), opposite_x(), paired_y(1), paired_y(2)):
+        own_rows = own_rows + send(own_rows, partner)
+    own_rows, terms = together(own_rows, terms)
     spread = jnp.broadcast_to(own_rows[None], (16, 16, width)).reshape(256, width)
     weight_grad = lax.all_to_all(spread, "rep", 0, 0, tiled=True)
-
-    summed = sum(term.astype(jnp.float32) for term in terms)
+    summed = terms.astype(jnp.float32).sum(axis=0)
+
     propagated = (inverse_root[:, None] * summed).astype(jnp.bfloat16)
     input_grad = lax.dot_general(
         propagated, weight, (((1,), (1,)), ((), ())), preferred_element_type=jnp.float32

time: 413 us -> 225 us (0.54)
  Pallas kernels: 223 us -> 38.9 us
  blocking collectives: 37.1 us -> 0 us
  waiting for transfers between devices: 68 us -> 91.6 us
  starting transfers between devices: 65.6 us -> 70.1 us
    pallas_call x1, Pallas kernels: 192 us -> 7.83 us  [pick(): pl.pallas_call(pick_kernel, out_shape=jax.ShapeDtypeStruct((groups, slots...]
    all_to_all x2 -> x0, blocking collectives: 37.1 us -> none  [the longest x1 20.7 us: body(): lax.all_to_all(local_weight, 'rep', 0, 0, tiled=True).reshape(16, 16, width)]
    all_to_all x0 -> x3, starting transfers between devices: none -> 24.6 us  [the longest x1 8.57 us: spread_over(): lax.all_to_all(copies, BOTH, 0, 0, axis_index_groups=places, tiled=True)]
    all_to_all x0 -> x3, waiting for transfers between devices: none -> 17.9 us  [the longest x1 13.3 us: body(): lax.all_to_all(local_weight, 'rep', 0, 0, tiled=True).reshape(16, 16, width)]
    ppermute x38 -> x31, starting transfers between devices: 58.2 us -> 40.7 us  [send(): return lax.ppermute(value, BOTH, moves)]
    all_to_all x1, waiting for transfers between devices: 0.01 us -> 9.59 us  [body(): weight_grad = lax.all_to_all(spread, 'rep', 0, 0, tiled=True)]
    ppermute x38 -> x31, waiting for transfers between devices: 68 us -> 64.1 us  [send(): return lax.ppermute(value, BOTH, moves)]
  transfers between devices with their start and end apart: 39 -> 35, of which waited for: 18 -> 21; matrix products, arithmetic and copies ran while one was open for 2% -> 5% of each run, Pallas kernels for 46% -> 4%
where the time goes in v3:
time: 225 us; the launch traced here: 222 us
  waiting for transfers between devices  91.6 us (41%)
  starting transfers between devices  70.1 us (31%)
  Pallas kernels  38.9 us (17%)
  local copies, waits for them, and re-layouts  13.7 us (6%)
  other arithmetic  5.42 us (2%)
    ppermute x31, waiting for transfers between devices, send(): return lax.ppermute(value, BOTH, moves)  64.1 us
    ppermute x31, starting transfers between devices, send(): return lax.ppermute(value, BOTH, moves)  40.7 us
    pallas_call x1, Pallas kernels, products(): pl.pallas_call(lambda *refs: products_kernel(places, *refs), out_shape=(j...  21.8 us
    all_to_all x1, waiting for transfers between devices, body(): lax.all_to_all(local_weight, 'rep', 0, 0, tiled=True).reshape(16, 16, width)  13.3 us
    all_to_all x1, waiting for transfers between devices, body(): weight_grad = lax.all_to_all(spread, 'rep', 0, 0, tiled=True)  9.59 us
    pallas_call x1, Pallas kernels, combine(): pl.pallas_call(lambda *refs: combine_kernel(places, *refs), out_shape=(ja...  9.23 us
    all_to_all x1, starting transfers between devices, spread_over(): lax.all_to_all(copies, BOTH, 0, 0, axis_index_groups=places, tiled=True)  8.57 us
    all_to_all x1, starting transfers between devices, body(): lax.all_to_all(local_weight, 'rep', 0, 0, tiled=True).reshape(16, 16, width)  8.34 us
  transfers between devices with their start and end apart: 35, of which 21 were waited for; matrix products, arithmetic and copies ran while one was open for 5% of the time, Pallas kernels for 4%

profile of v3, /device:TPU:32, one launch (start us, length us, event | category | flops | bytes accessed | tf_op | source)
XLA Modules:
  0.0 221.6 jit_solution(7264116525715255366)
XLA Ops:
  2.5 2.8 %collective-permute-start.1 = (bf16[64,256]{1,0:T(8,128)(2,1)S(1)}, bf16[64,256]{1,0:T(8,128)(2,1)S(1)}, u32[]{:S(2)}, u32[]{:S(2)}) collective-permute-start(bf16[64,256]{1,0:T(8,128)(2,1)S(1)} %get-tuple-element.31), channel_id=1, source_target_pairs={{0,136},{16,112},{1,137},{17,113},{2,138},{18,114},{3,139},{19,115... | collective-permute-start | bytes 98312 | tf_op jit(solution)/shard_map/ppermute | solution.py:67
  9.7 8.6 %all-to-all-start = ((bf16[8,128,256]{2,1,0:T(8,128)(2,1)}), bf16[8,128,256]{2,1,0:T(8,128)(2,1)S(1)}, u32[]{:S(2)}, u32[]{:S(2)}) async-start(bf16[8,128,256]{2,1,0:T(8,128)(2,1)} %broadcast_in_dim.42), calls=%async_computation | async-start | bytes 1048576 | tf_op jit(solution)/shard_map/all_to_all | solution.py:43
  18.2 7.8 %pick_tiles.1 = bf16[8,24,128,128]{3,2,1,0:T(8,128)(2,1)} custom-call(s32[1]{0:T(128)} %bitcast.14.side, bf16[8,2,24,128,128]{4,3,2,1,0:T(8,128)(2,1)} %bitcast.39), custom_call_target="tpu_custom_call" | custom-call | bytes 12582912 | tf_op jit(solution)/shard_map/pick_tiles/pallas_call | solution.py:187
  26.1 3.1 %collective-permute-start.4 = (bf16[4,64,256]{2,1,0:T(8,128)(2,1)S(1)}, bf16[4,64,256]{2,1,0:T(8,128)(2,1)S(1)}, u32[]{:S(2)}, u32[]{:S(2)}) collective-permute-start(bf16[4,64,256]{2,1,0:T(8,128)(2,1)S(1)} %pad_maximum_fusion.1), channel_id=1, source_target_pairs={{0,96},{16,152},{1,97},{17,153},{2,98},{18,154},{3,99},{19,155},{4... | collective-permute-start | bytes 393224 | tf_op jit(solution)/shard_map/ppermute | solution.py:67
  30.8 2.3 %collective-permute-done.4 = bf16[4,64,256]{2,1,0:T(8,128)(2,1)S(1)} collective-permute-done((bf16[4,64,256]{2,1,0:T(8,128)(2,1)S(1)}, bf16[4,64,256]{2,1,0:T(8,128)(2,1)S(1)}, u32[]{:S(2)}, u32[]{:S(2)}) %collective-permute-start.4) | collective-permute-done | bytes 131104 | tf_op jit(solution)/shard_map/ppermute | solution.py:67
  33.1 2.6 %collective-permute-done.5 = bf16[4,64,256]{2,1,0:T(8,128)(2,1)S(1)} collective-permute-done((bf16[4,64,256]{2,1,0:T(8,128)(2,1)S(1)}, bf16[4,64,256]{2,1,0:T(8,128)(2,1)S(1)}, u32[]{:S(2)}, u32[]{:S(2)}) %collective-permute-start.5) | collective-permute-done | bytes 131104 | tf_op jit(solution)/shard_map/ppermute | solution.py:67
  41.4 5.1 %collective-permute-done.9 = bf16[8,128,256]{2,1,0:T(8,128)(2,1)S(1)} collective-permute-done((bf16[8,128,256]{2,1,0:T(8,128)(2,1)S(1)}, bf16[8,128,256]{2,1,0:T(8,128)(2,1)S(1)}, u32[]{:S(2)}, u32[]{:S(2)}) %collective-permute-start.9) | collective-permute-done | bytes 524320 | tf_op jit(solution)/shard_map/ppermute | solution.py:67
  48.7 4.2 %collective-permute-done.12 = bf16[4,128,256]{2,1,0:T(8,128)(2,1)S(1)} collective-permute-done((bf16[4,128,256]{2,1,0:T(8,128)(2,1)S(1)}, bf16[4,128,256]{2,1,0:T(8,128)(2,1)S(1)}, u32[]{:S(2)}, u32[]{:S(2)}) %collective-permute-start.12) | collective-permute-done | bytes 262176 | tf_op jit(solution)/shard_map/ppermute | solution.py:67
  53.0 3.1 %collective-permute-done.11 = bf16[4,128,256]{2,1,0:T(8,128)(2,1)S(1)} collective-permute-done((bf16[4,128,256]{2,1,0:T(8,128)(2,1)S(1)}, bf16[4,128,256]{2,1,0:T(8,128)(2,1)S(1)}, u32[]{:S(2)}, u32[]{:S(2)}) %collective-permute-start.11) | collective-permute-done | bytes 262176 | tf_op jit(solution)/shard_map/ppermute | solution.py:67
  58.8 3.0 %collective-permute-start.15 = (bf16[4,8,128,256]{3,2,1,0:T(8,128)(2,1)S(1)}, bf16[4,8,128,256]{3,2,1,0:T(8,128)(2,1)}, u32[]{:S(2)}, u32[]{:S(2)}) collective-permute-start(bf16[4,8,128,256]{3,2,1,0:T(8,128)(2,1)S(1)} %pad_maximum_fusion), channel_id=1, source_target_pairs={{0,136},{16,112},{1,137},{17,113},{2,138},{18,114},{3,139},{19,115... | collective-permute-start | bytes 6291464 | tf_op jit(solution)/shard_map/ppermute | solution.py:67
  64.3 14.9 %collective-permute-done.19.refs_14_.refs_5_ = bf16[22,64,256]{2,1,0:T(8,128)(2,1)S(1)} collective-permute-done((bf16[22,64,256]{2,1,0:T(8,128)(2,1)}, bf16[22,64,256]{2,1,0:T(8,128)(2,1)S(1)}, u32[]{:S(2)}, u32[]{:S(2)}) %collective-permute-start.19) | collective-permute-done | bytes 720928 | tf_op jit(solution)/shard_map/ppermute | solution.py:67
  80.1 2.7 %collective-permute-start.20 = (bf16[22,64,256]{2,1,0:T(8,128)(2,1)}, bf16[22,64,256]{2,1,0:T(8,128)(2,1)S(1)}, u32[]{:S(2)}, u32[]{:S(2)}) collective-permute-start(bf16[22,64,256]{2,1,0:T(8,128)(2,1)} %copy-done.4), channel_id=1, source_target_pairs={{0,7},{16,23},{1,0},{17,16},{2,1},{18,17},{3,2},{19,18},{4,3},{20,... | collective-permute-start | bytes 2162696 | tf_op jit(solution)/shard_map/ppermute | solution.py:67
  82.8 3.1 %collective-permute-done.16 = bf16[4,8,128,256]{3,2,1,0:T(8,128)(2,1)} collective-permute-done((bf16[4,8,128,256]{3,2,1,0:T(8,128)(2,1)S(1)}, bf16[4,8,128,256]{3,2,1,0:T(8,128)(2,1)}, u32[]{:S(2)}, u32[]{:S(2)}) %collective-permute-start.16) | collective-permute-done | bytes 2097184 | tf_op jit(solution)/shard_map/ppermute | solution.py:67
  85.9 2.4 %collective-permute-start.22 = (bf16[22,64,256]{2,1,0:T(8,128)(2,1)}, bf16[22,64,256]{2,1,0:T(8,128)(2,1)}, u32[]{:S(2)}, u32[]{:S(2)}) collective-permute-start(bf16[22,64,256]{2,1,0:T(8,128)(2,1)} %collective-permute-done.21.refs_19_.refs_9_), channel_id=1, source_target_pairs={{0,1},{16,17},{1,2},{17,18},{2,3},{18,19},{3,4},{19,20},{4,5},{20,... | collective-permute-start | bytes 2162696 | tf_op jit(solution)/shard_map/ppermute | solution.py:67
  90.6 2.3 %slice.27 = bf16[2,8,128,256]{3,2,1,0:T(8,128)(2,1)} slice(bf16[4,8,128,256]{3,2,1,0:T(8,128)(2,1)} %collective-permute-done.15), slice={[2:4], [0:8], [0:128], [0:256]} | slice | bytes 2097152 | tf_op jit(solution)/shard_map/slice | solution.py:76
  92.9 3.2 %collective-permute-start.18 = (bf16[2,8,128,256]{3,2,1,0:T(8,128)(2,1)}, bf16[2,8,128,256]{3,2,1,0:T(8,128)(2,1)S(1)}, u32[]{:S(2)}, u32[]{:S(2)}) collective-permute-start(bf16[2,8,128,256]{3,2,1,0:T(8,128)(2,1)} %slice.27), channel_id=1, source_target_pairs={{0,136},{16,112},{1,137},{17,113},{2,138},{18,114},{3,139},{19,115... | collective-permute-start | bytes 3145736 | tf_op jit(solution)/shard_map/ppermute | solution.py:67
  98.1 4.2 %collective-permute-done.22.refs_18_.refs_8_ = bf16[22,64,256]{2,1,0:T(8,128)(2,1)} collective-permute-done((bf16[22,64,256]{2,1,0:T(8,128)(2,1)}, bf16[22,64,256]{2,1,0:T(8,128)(2,1)}, u32[]{:S(2)}, u32[]{:S(2)}) %collective-permute-start.22) | collective-permute-done | bytes 720928 | tf_op jit(solution)/shard_map/ppermute | solution.py:67
  103.3 2.7 %collective-permute-start.23 = (bf16[11,64,256]{2,1,0:T(8,128)(2,1)S(1)}, bf16[11,64,256]{2,1,0:T(8,128)(2,1)S(1)}, u32[]{:S(2)}, u32[]{:S(2)}) collective-permute-start(bf16[11,64,256]{2,1,0:T(8,128)(2,1)S(1)} %slice.28), channel_id=1, source_target_pairs={{0,1},{16,17},{1,2},{17,18},{2,3},{18,19},{3,4},{19,20},{4,5},{20,... | collective-permute-start | bytes 1081352 | tf_op jit(solution)/shard_map/ppermute | solution.py:67
  107.4 3.7 %collective-permute-done.23.refs_16_ = bf16[11,64,256]{2,1,0:T(8,128)(2,1)S(1)} collective-permute-done((bf16[11,64,256]{2,1,0:T(8,128)(2,1)S(1)}, bf16[11,64,256]{2,1,0:T(8,128)(2,1)S(1)}, u32[]{:S(2)}, u32[]{:S(2)}) %collective-permute-start.23) | collective-permute-done | bytes 360480 | tf_op jit(solution)/shard_map/ppermute | solution.py:67
  111.2 2.9 %collective-permute-done.24.refs_17_.refs_7_ = bf16[11,64,256]{2,1,0:T(8,128)(2,1)S(1)} collective-permute-done((bf16[11,64,256]{2,1,0:T(8,128)(2,1)S(1)}, bf16[11,64,256]{2,1,0:T(8,128)(2,1)S(1)}, u32[]{:S(2)}, u32[]{:S(2)}) %collective-permute-start.24) | collective-permute-done | bytes 360480 | tf_op jit(solution)/shard_map/ppermute | solution.py:67
  115.1 21.8 %tile_products.1 = (f32[24,128,256]{2,1,0:T(8,128)}, bf16[24,128,256]{2,1,0:T(8,128)(2,1)}) custom-call(s32[16]{0:T(128)} %min.8.refs_0_, s32[384]{0:T(512)} %fusion.9.refs_1_, s32[384]{0:T(512)} %get-tuple-element.32.refs_2_, s32[384]{0:T(512)} %get-tuple-element.39.refs_3_, s32[3]{0:T(128)} %pad_add_fusion.1.refs_4_.refs_0_, ...), custom_call_target="tpu_custom_call" | custom-call | flops 3221225472 | bytes 31457280 | tf_op jit(solution)/shard_map/tile_products/pallas_call | solution.py:204
  137.0 3.6 %collective-permute-done.25 = bf16[24,128,256]{2,1,0:T(8,128)(2,1)S(1)} collective-permute-done((bf16[24,128,256]{2,1,0:T(8,128)(2,1)}, bf16[24,128,256]{2,1,0:T(8,128)(2,1)S(1)}, u32[]{:S(2)}, u32[]{:S(2)}) %collective-permute-start.25) | collective-permute-done | bytes 1572896 | tf_op jit(solution)/shard_map/ppermute | solution.py:67
  141.8 9.2 %combine_cores.1 = (bf16[2,8,192,256]{3,2,1,0:T(8,128)(2,1)}, f32[256,256]{1,0:T(8,128)}) custom-call(s32[3]{0:T(128)} %pad_add_fusion.1.refs_4_.refs_0_, f32[2,8,192,256]{3,2,1,0:T(8,128)} %bitcast.42, bf16[2,8,192,256]{3,2,1,0:T(8,128)(2,1)} %bitcast.44, bf16[22,64,256]{2,1,0:T(8,128)(2,1)} %copy-done.3, ...), custom_call_target="tpu_custom_call" | custom-call | flops 402653184 | bytes 8388608 | tf_op jit(solution)/shard_map/combine_cores/pallas_call | solution.py:162
  153.2 8.3 %all-to-all-start.1 = ((f32[16,16,256]{2,1,0:T(8,128)}), f32[16,16,256]{2,1,0:T(8,128)S(1)}, u32[]{:S(2)}, u32[]{:S(2)}) async-start(f32[16,16,256]{2,1,0:T(8,128)} %bitcast.50), calls=%async_computation.1 | async-start | bytes 524288 | tf_op jit(solution)/shard_map/all_to_all | solution.py:323
  161.5 13.3 %all-to-all-done.1 = f32[16,16,256]{2,1,0:T(8,128)S(1)} async-done(((f32[16,16,256]{2,1,0:T(8,128)}), f32[16,16,256]{2,1,0:T(8,128)S(1)}, u32[]{:S(2)}, u32[]{:S(2)}) %all-to-all-start.1) | async-done | bytes 262176 | tf_op jit(solution)/shard_map/all_to_all | solution.py:323
  176.0 7.7 %all-to-all-start.2 = ((bf16[8,192,256]{2,1,0:T(8,128)(2,1)}), bf16[8,192,256]{2,1,0:T(8,128)(2,1)S(1)}, u32[]{:S(2)}, u32[]{:S(2)}) async-start(bf16[8,192,256]{2,1,0:T(8,128)(2,1)} %fusion), calls=%async_computation.2 | async-start | bytes 1572864 | tf_op jit(solution)/shard_map/all_to_all | solution.py:326
  184.9 4.6 %collective-permute-start.28 = (f32[16,256]{1,0:T(8,128)S(1)}, f32[16,256]{1,0:T(8,128)S(1)}, u32[]{:S(2)}, u32[]{:S(2)}) collective-permute-start(f32[16,256]{1,0:T(8,128)S(1)} %add.252), channel_id=1, source_target_pairs={{0,128},{16,144},{1,129},{17,145},{2,130},{18,146},{3,131},{19,147... | collective-permute-start | bytes 49160 | tf_op jit(solution)/shard_map/ppermute | solution.py:67
  192.0 2.9 %collective-permute-done.29 = f32[16,256]{1,0:T(8,128)S(1)} collective-permute-done((f32[16,256]{1,0:T(8,128)S(1)}, f32[16,256]{1,0:T(8,128)S(1)}, u32[]{:S(2)}, u32[]{:S(2)}) %collective-permute-start.29) | collective-permute-done | bytes 16416 | tf_op jit(solution)/shard_map/ppermute | solution.py:67
  195.1 5.1 %collective-permute-done.30 = f32[16,256]{1,0:T(8,128)S(1)} collective-permute-done((f32[16,256]{1,0:T(8,128)S(1)}, f32[16,256]{1,0:T(8,128)S(1)}, u32[]{:S(2)}, u32[]{:S(2)}) %collective-permute-start.30) | collective-permute-done | bytes 16416 | tf_op jit(solution)/shard_map/ppermute | solution.py:67
  200.2 4.6 %all-to-all-done.2 = bf16[8,192,256]{2,1,0:T(8,128)(2,1)S(1)} async-done(((bf16[8,192,256]{2,1,0:T(8,128)(2,1)}), bf16[8,192,256]{2,1,0:T(8,128)(2,1)S(1)}, u32[]{:S(2)}, u32[]{:S(2)}) %all-to-all-start.2) | async-done | bytes 786464 | tf_op jit(solution)/shard_map/all_to_all | solution.py:326
  205.5 4.8 %all-to-all-start.3 = ((f32[16,16,256]{2,1,0:T(8,128)}), f32[16,16,256]{2,1,0:T(8,128)S(1)}, u32[]{:S(2)}, u32[]{:S(2)}) async-start(f32[16,16,256]{2,1,0:T(8,128)} %broadcast_in_dim.43), calls=%async_computation.3 | async-start | bytes 524288 | tf_op jit(solution)/shard_map/all_to_all | solution.py:331
  211.3 9.6 %all-to-all-done.3 = f32[16,16,256]{2,1,0:T(8,128)S(1)} async-done(((f32[16,16,256]{2,1,0:T(8,128)}), f32[16,16,256]{2,1,0:T(8,128)S(1)}, u32[]{:S(2)}, u32[]{:S(2)}) %all-to-all-start.3) | async-done | bytes 262176 | tf_op jit(solution)/shard_map/all_to_all | solution.py:331
  (120 shorter events, 40.2 us)
Async XLA Ops:
  2.5 23.6 %collective-permute-start.1 = (bf16[64,256]{1,0:T(8,128)(2,1)S(1)}, bf16[64,256]{1,0:T(8,128)(2,1)S(1)}, u32[]{:S(2)}, u32[]{:S(2)}) collective-permute-start(bf16[64,256]{1,0:T(8,128)(2,1)S(1)} %get-tuple-element.31), channel_id=1, source_target_pairs={{0,136},{16,112},{1,137},{17,113},{2,138},{18,114},{3,139},{19,115... | collective-permute-start | bytes 98312 | tf_op jit(solution)/shard_map/ppermute | solution.py:67
  5.3 20.7 %collective-permute-start.2 = (bf16[64,256]{1,0:T(8,128)(2,1)S(1)}, bf16[64,256]{1,0:T(8,128)(2,1)S(1)}, u32[]{:S(2)}, u32[]{:S(2)}) collective-permute-start(bf16[64,256]{1,0:T(8,128)(2,1)S(1)} %get-tuple-element.31), channel_id=1, source_target_pairs={{0,128},{16,80},{1,129},{17,81},{2,130},{18,82},{3,131},{19,83},{4... | collective-permute-start | bytes 98312 | tf_op jit(solution)/shard_map/ppermute | solution.py:67
  6.1 19.9 %collective-permute-start.3 = (bf16[64,256]{1,0:T(8,128)(2,1)S(1)}, bf16[64,256]{1,0:T(8,128)(2,1)S(1)}, u32[]{:S(2)}, u32[]{:S(2)}) collective-permute-start(bf16[64,256]{1,0:T(8,128)(2,1)S(1)} %get-tuple-element.31), channel_id=1, source_target_pairs={{0,8},{16,48},{1,9},{17,49},{2,10},{18,50},{3,11},{19,51},{4,12},{... | collective-permute-start | bytes 98312 | tf_op jit(solution)/shard_map/ppermute | solution.py:67
  7.0 30.1 %collective-permute-start.7 = (bf16[192,256]{1,0:T(8,128)(2,1)S(1)}, bf16[192,256]{1,0:T(8,128)(2,1)S(1)}, u32[]{:S(2)}, u32[]{:S(2)}) collective-permute-start(bf16[192,256]{1,0:T(8,128)(2,1)S(1)} %get-tuple-element.40), channel_id=1, source_target_pairs={{0,8},{16,24},{1,9},{17,25},{2,10},{18,26},{3,11},{19,27},{4,12},{... | collective-permute-start | bytes 294920 | tf_op jit(solution)/shard_map/ppermute | solution.py:67
  9.7 27.5 %all-to-all-start = ((bf16[8,128,256]{2,1,0:T(8,128)(2,1)}), bf16[8,128,256]{2,1,0:T(8,128)(2,1)S(1)}, u32[]{:S(2)}, u32[]{:S(2)}) async-start(bf16[8,128,256]{2,1,0:T(8,128)(2,1)} %broadcast_in_dim.42), calls=%async_computation | async-start | bytes 1048576 | tf_op jit(solution)/shard_map/all_to_all | solution.py:43
  26.1 7.0 %collective-permute-start.4 = (bf16[4,64,256]{2,1,0:T(8,128)(2,1)S(1)}, bf16[4,64,256]{2,1,0:T(8,128)(2,1)S(1)}, u32[]{:S(2)}, u32[]{:S(2)}) collective-permute-start(bf16[4,64,256]{2,1,0:T(8,128)(2,1)S(1)} %pad_maximum_fusion.1), channel_id=1, source_target_pairs={{0,96},{16,152},{1,97},{17,153},{2,98},{18,154},{3,99},{19,155},{4... | collective-permute-start | bytes 393224 | tf_op jit(solution)/shard_map/ppermute | solution.py:67
  29.2 6.6 %collective-permute-start.5 = (bf16[4,64,256]{2,1,0:T(8,128)(2,1)S(1)}, bf16[4,64,256]{2,1,0:T(8,128)(2,1)S(1)}, u32[]{:S(2)}, u32[]{:S(2)}) collective-permute-start(bf16[4,64,256]{2,1,0:T(8,128)(2,1)S(1)} %pad_maximum_fusion.1), channel_id=1, source_target_pairs={{0,64},{16,144},{1,65},{17,145},{2,66},{18,146},{3,67},{19,147},{4... | collective-permute-start | bytes 393224 | tf_op jit(solution)/shard_map/ppermute | solution.py:67
  29.8 7.2 %collective-permute-start.6 = (bf16[4,64,256]{2,1,0:T(8,128)(2,1)S(1)}, bf16[4,64,256]{2,1,0:T(8,128)(2,1)S(1)}, u32[]{:S(2)}, u32[]{:S(2)}) collective-permute-start(bf16[4,64,256]{2,1,0:T(8,128)(2,1)S(1)} %pad_maximum_fusion.1), channel_id=1, source_target_pairs={{0,32},{16,24},{1,33},{17,25},{2,34},{18,26},{3,35},{19,27},{4,36}... | collective-permute-start | bytes 393224 | tf_op jit(solution)/shard_map/ppermute | solution.py:67
  37.2 76.9 %collective-permute-start.8 = (bf16[8,24,128,128]{3,2,1,0:T(8,128)(2,1)}, bf16[8,24,128,128]{3,2,1,0:T(8,128)(2,1)}, u32[]{:S(2)}, u32[]{:S(2)}) collective-permute-start(bf16[8,24,128,128]{3,2,1,0:T(8,128)(2,1)} %pick_tiles.1), channel_id=1, source_target_pairs={{0,16},{16,0},{1,17},{17,1},{2,18},{18,2},{3,19},{19,3},{4,20},{20... | collective-permute-start | bytes 18874376 | tf_op jit(solution)/shard_map/ppermute | solution.py:67
  37.3 9.3 %collective-permute-start.9 = (bf16[8,128,256]{2,1,0:T(8,128)(2,1)S(1)}, bf16[8,128,256]{2,1,0:T(8,128)(2,1)S(1)}, u32[]{:S(2)}, u32[]{:S(2)}) collective-permute-start(bf16[8,128,256]{2,1,0:T(8,128)(2,1)S(1)} %all-to-all-done), channel_id=1, source_target_pairs={{0,96},{16,152},{1,97},{17,153},{2,98},{18,154},{3,99},{19,155},{4... | collective-permute-start | bytes 1572872 | tf_op jit(solution)/shard_map/ppermute | solution.py:67
  37.9 10.5 %collective-permute-start.10 = (bf16[8,128,256]{2,1,0:T(8,128)(2,1)S(1)}, bf16[8,128,256]{2,1,0:T(8,128)(2,1)S(1)}, u32[]{:S(2)}, u32[]{:S(2)}) collective-permute-start(bf16[8,128,256]{2,1,0:T(8,128)(2,1)S(1)} %all-to-all-done), channel_id=1, source_target_pairs={{0,32},{16,24},{1,33},{17,25},{2,34},{18,26},{3,35},{19,27},{4,36}... | collective-permute-start | bytes 1572872 | tf_op jit(solution)/shard_map/ppermute | solution.py:67
  39.4 18.0 %collective-permute-start.13 = (bf16[22,64,256]{2,1,0:T(8,128)(2,1)S(1)}, bf16[22,64,256]{2,1,0:T(8,128)(2,1)}, u32[]{:S(2)}, u32[]{:S(2)}) collective-permute-start(bf16[22,64,256]{2,1,0:T(8,128)(2,1)S(1)} %constant_dynamic-update-slice_fusion.refs_12_.refs_3_), channel_id=1, source_target_pairs={{0,1},{16,17},{1,2},{17,18},{2,3},{18,19},{3,4},{19,20},{4,5},{20,... | collective-permute-start | bytes 2162696 | tf_op jit(solution)/shard_map/ppermute | solution.py:67
  40.8 17.7 %collective-permute-start.14 = (bf16[22,64,256]{2,1,0:T(8,128)(2,1)S(1)}, bf16[22,64,256]{2,1,0:T(8,128)(2,1)}, u32[]{:S(2)}, u32[]{:S(2)}) collective-permute-start(bf16[22,64,256]{2,1,0:T(8,128)(2,1)S(1)} %constant_dynamic-update-slice_fusion.refs_12_.refs_3_), channel_id=1, source_target_pairs={{0,7},{16,23},{1,0},{17,16},{2,1},{18,17},{3,2},{19,18},{4,3},{20,... | collective-permute-start | bytes 2162696 | tf_op jit(solution)/shard_map/ppermute | solution.py:67
  46.5 6.4 %collective-permute-start.12 = (bf16[4,128,256]{2,1,0:T(8,128)(2,1)S(1)}, bf16[4,128,256]{2,1,0:T(8,128)(2,1)S(1)}, u32[]{:S(2)}, u32[]{:S(2)}) collective-permute-start(bf16[4,128,256]{2,1,0:T(8,128)(2,1)S(1)} %slice.25), channel_id=1, source_target_pairs={{0,96},{16,152},{1,97},{17,153},{2,98},{18,154},{3,99},{19,155},{4... | collective-permute-start | bytes 786440 | tf_op jit(solution)/shard_map/ppermute | solution.py:67
  48.4 7.7 %collective-permute-start.11 = (bf16[4,128,256]{2,1,0:T(8,128)(2,1)S(1)}, bf16[4,128,256]{2,1,0:T(8,128)(2,1)S(1)}, u32[]{:S(2)}, u32[]{:S(2)}) collective-permute-start(bf16[4,128,256]{2,1,0:T(8,128)(2,1)S(1)} %slice.24), channel_id=1, source_target_pairs={{0,32},{16,24},{1,33},{17,25},{2,34},{18,26},{3,35},{19,27},{4,36}... | collective-permute-start | bytes 786440 | tf_op jit(solution)/shard_map/ppermute | solution.py:67
  58.6 27.4 %collective-permute-start.16 = (bf16[4,8,128,256]{3,2,1,0:T(8,128)(2,1)S(1)}, bf16[4,8,128,256]{3,2,1,0:T(8,128)(2,1)}, u32[]{:S(2)}, u32[]{:S(2)}) collective-permute-start(bf16[4,8,128,256]{3,2,1,0:T(8,128)(2,1)S(1)} %pad_maximum_fusion), channel_id=1, source_target_pairs={{0,8},{16,48},{1,9},{17,49},{2,10},{18,50},{3,11},{19,51},{4,12},{... | collective-permute-start | bytes 6291464 | tf_op jit(solution)/shard_map/ppermute | solution.py:67
  58.8 31.7 %collective-permute-start.15 = (bf16[4,8,128,256]{3,2,1,0:T(8,128)(2,1)S(1)}, bf16[4,8,128,256]{3,2,1,0:T(8,128)(2,1)}, u32[]{:S(2)}, u32[]{:S(2)}) collective-permute-start(bf16[4,8,128,256]{3,2,1,0:T(8,128)(2,1)S(1)} %pad_maximum_fusion), channel_id=1, source_target_pairs={{0,136},{16,112},{1,137},{17,113},{2,138},{18,114},{3,139},{19,115... | collective-permute-start | bytes 6291464 | tf_op jit(solution)/shard_map/ppermute | solution.py:67
  61.8 17.3 %collective-permute-start.19 = (bf16[22,64,256]{2,1,0:T(8,128)(2,1)}, bf16[22,64,256]{2,1,0:T(8,128)(2,1)S(1)}, u32[]{:S(2)}, u32[]{:S(2)}) collective-permute-start(bf16[22,64,256]{2,1,0:T(8,128)(2,1)} %collective-permute-done.14.refs_13_.refs_4_), channel_id=1, source_target_pairs={{0,7},{16,23},{1,0},{17,16},{2,1},{18,17},{3,2},{19,18},{4,3},{20,... | collective-permute-start | bytes 2162696 | tf_op jit(solution)/shard_map/ppermute | solution.py:67
  62.4 17.7 %collective-permute-start.21 = (bf16[22,64,256]{2,1,0:T(8,128)(2,1)}, bf16[22,64,256]{2,1,0:T(8,128)(2,1)}, u32[]{:S(2)}, u32[]{:S(2)}) collective-permute-start(bf16[22,64,256]{2,1,0:T(8,128)(2,1)} %collective-permute-done.13.refs_20_.refs_10_), channel_id=1, source_target_pairs={{0,1},{16,17},{1,2},{17,18},{2,3},{18,19},{3,4},{19,20},{4,5},{20,... | collective-permute-start | bytes 2162696 | tf_op jit(solution)/shard_map/ppermute | solution.py:67
  79.1 13.8 %collective-permute-start = (s32[8,24]{1,0:T(8,128)S(1)}, s32[8,24]{1,0:T(8,128)S(1)}, u32[]{:S(2)}, u32[]{:S(2)}) collective-permute-start(s32[8,24]{1,0:T(8,128)S(1)} %bitcast.58), channel_id=1, source_target_pairs={{0,16},{16,0},{1,17},{17,1},{2,18},{18,2},{3,19},{19,3},{4,20},{20... | collective-permute-start | bytes 2312 | tf_op jit(solution)/shard_map/ppermute | solution.py:67
  80.1 26.0 %collective-permute-start.20 = (bf16[22,64,256]{2,1,0:T(8,128)(2,1)}, bf16[22,64,256]{2,1,0:T(8,128)(2,1)S(1)}, u32[]{:S(2)}, u32[]{:S(2)}) collective-permute-start(bf16[22,64,256]{2,1,0:T(8,128)(2,1)} %copy-done.4), channel_id=1, source_target_pairs={{0,7},{16,23},{1,0},{17,16},{2,1},{18,17},{3,2},{19,18},{4,3},{20,... | collective-permute-start | bytes 2162696 | tf_op jit(solution)/shard_map/ppermute | solution.py:67
  85.9 16.4 %collective-permute-start.22 = (bf16[22,64,256]{2,1,0:T(8,128)(2,1)}, bf16[22,64,256]{2,1,0:T(8,128)(2,1)}, u32[]{:S(2)}, u32[]{:S(2)}) collective-permute-start(bf16[22,64,256]{2,1,0:T(8,128)(2,1)} %collective-permute-done.21.refs_19_.refs_9_), channel_id=1, source_target_pairs={{0,1},{16,17},{1,2},{17,18},{2,3},{18,19},{3,4},{19,20},{4,5},{20,... | collective-permute-start | bytes 2162696 | tf_op jit(solution)/shard_map/ppermute | solution.py:67
  90.6 23.4 %collective-permute-start.17 = (bf16[2,8,128,256]{3,2,1,0:T(8,128)(2,1)}, bf16[2,8,128,256]{3,2,1,0:T(8,128)(2,1)}, u32[]{:S(2)}, u32[]{:S(2)}) collective-permute-start(bf16[2,8,128,256]{3,2,1,0:T(8,128)(2,1)} %slice.26), channel_id=1, source_target_pairs={{0,8},{16,48},{1,9},{17,49},{2,10},{18,50},{3,11},{19,51},{4,12},{... | collective-permute-start | bytes 3145736 | tf_op jit(solution)/shard_map/ppermute | solution.py:67
  92.9 21.1 %collective-permute-start.18 = (bf16[2,8,128,256]{3,2,1,0:T(8,128)(2,1)}, bf16[2,8,128,256]{3,2,1,0:T(8,128)(2,1)S(1)}, u32[]{:S(2)}, u32[]{:S(2)}) collective-permute-start(bf16[2,8,128,256]{3,2,1,0:T(8,128)(2,1)} %slice.27), channel_id=1, source_target_pairs={{0,136},{16,112},{1,137},{17,113},{2,138},{18,114},{3,139},{19,115... | collective-permute-start | bytes 3145736 | tf_op jit(solution)/shard_map/ppermute | solution.py:67
  103.3 7.8 %collective-permute-start.23 = (bf16[11,64,256]{2,1,0:T(8,128)(2,1)S(1)}, bf16[11,64,256]{2,1,0:T(8,128)(2,1)S(1)}, u32[]{:S(2)}, u32[]{:S(2)}) collective-permute-start(bf16[11,64,256]{2,1,0:T(8,128)(2,1)S(1)} %slice.28), channel_id=1, source_target_pairs={{0,1},{16,17},{1,2},{17,18},{2,3},{18,19},{3,4},{19,20},{4,5},{20,... | collective-permute-start | bytes 1081352 | tf_op jit(solution)/shard_map/ppermute | solution.py:67
  106.1 8.0 %collective-permute-start.24 = (bf16[11,64,256]{2,1,0:T(8,128)(2,1)S(1)}, bf16[11,64,256]{2,1,0:T(8,128)(2,1)S(1)}, u32[]{:S(2)}, u32[]{:S(2)}) collective-permute-start(bf16[11,64,256]{2,1,0:T(8,128)(2,1)S(1)} %slice.29), channel_id=1, source_target_pairs={{0,7},{16,23},{1,0},{17,16},{2,1},{18,17},{3,2},{19,18},{4,3},{20,... | collective-permute-start | bytes 1081352 | tf_op jit(solution)/shard_map/ppermute | solution.py:67
  152.4 22.5 %collective-permute-start.26 = (bf16[8,192,256]{2,1,0:T(8,128)(2,1)S(1)}, bf16[8,192,256]{2,1,0:T(8,128)(2,1)S(1)}, u32[]{:S(2)}, u32[]{:S(2)}) collective-permute-start(bf16[8,192,256]{2,1,0:T(8,128)(2,1)S(1)} %dynamic-slice_bitcast_fusion), channel_id=1, source_target_pairs={{0,8},{16,24},{1,9},{17,25},{2,10},{18,26},{3,11},{19,27},{4,12},{... | collective-permute-start | bytes 2359304 | tf_op jit(solution)/shard_map/ppermute | solution.py:67
  153.2 21.7 %all-to-all-start.1 = ((f32[16,16,256]{2,1,0:T(8,128)}), f32[16,16,256]{2,1,0:T(8,128)S(1)}, u32[]{:S(2)}, u32[]{:S(2)}) async-start(f32[16,16,256]{2,1,0:T(8,128)} %bitcast.50), calls=%async_computation.1 | async-start | bytes 524288 | tf_op jit(solution)/shard_map/all_to_all | solution.py:323
  176.0 28.8 %all-to-all-start.2 = ((bf16[8,192,256]{2,1,0:T(8,128)(2,1)}), bf16[8,192,256]{2,1,0:T(8,128)(2,1)S(1)}, u32[]{:S(2)}, u32[]{:S(2)}) async-start(bf16[8,192,256]{2,1,0:T(8,128)(2,1)} %fusion), calls=%async_computation.2 | async-start | bytes 1572864 | tf_op jit(solution)/shard_map/all_to_all | solution.py:326
  184.9 6.3 %collective-permute-start.28 = (f32[16,256]{1,0:T(8,128)S(1)}, f32[16,256]{1,0:T(8,128)S(1)}, u32[]{:S(2)}, u32[]{:S(2)}) collective-permute-start(f32[16,256]{1,0:T(8,128)S(1)} %add.252), channel_id=1, source_target_pairs={{0,128},{16,144},{1,129},{17,145},{2,130},{18,146},{3,131},{19,147... | collective-permute-start | bytes 49160 | tf_op jit(solution)/shard_map/ppermute | solution.py:67
  195.0 5.2 %collective-permute-start.30 = (f32[16,256]{1,0:T(8,128)S(1)}, f32[16,256]{1,0:T(8,128)S(1)}, u32[]{:S(2)}, u32[]{:S(2)}) collective-permute-start(f32[16,256]{1,0:T(8,128)S(1)} %add.254), channel_id=1, source_target_pairs={{0,64},{16,80},{1,65},{17,81},{2,66},{18,82},{3,67},{19,83},{4,68}... | collective-permute-start | bytes 49160 | tf_op jit(solution)/shard_map/ppermute | solution.py:67
  205.5 15.4 %all-to-all-start.3 = ((f32[16,16,256]{2,1,0:T(8,128)}), f32[16,16,256]{2,1,0:T(8,128)S(1)}, u32[]{:S(2)}, u32[]{:S(2)}) async-start(f32[16,16,256]{2,1,0:T(8,128)} %broadcast_in_dim.43), calls=%async_computation.3 | async-start | bytes 524288 | tf_op jit(solution)/shard_map/all_to_all | solution.py:331
  (17 other events, 371.0 us)

commit v4 on v3

--- a/solution.py
+++ b/solution.py
@@ -128,9 +128,9 @@
         other_out[...] = totals[half:].astype(other_out.dtype)
 
 
-def combine_kernel(places, here, own, other, *rest):
+def features_kernel(places, here, partial, *rest):
     pieces = rest[: len(places)]
-    partial, gradient, features, sem = rest[len(places):]
+    gradient, features, sem = rest[len(places):]
     step = pl.program_id(0)
 
     @pl.when(step == 0)
@@ -146,40 +146,47 @@
             copy.wait()
 
     total = gradient[...]
-    ahead = lax.rem(step - here[2] + NZ, NZ)
-    for low in range(2):
-        rows = (own[low, 0] + other[low, 0].astype(jnp.float32)).astype(partial.dtype)
-        partial[low, 0] = rows
-        near = lax.bitwise_xor(low, here[1])
-        lanes = jnp.concatenate([features[ahead, 3 * near + n] for n in range(3)], axis=0)
-        total += lax.dot_general(lanes, rows, (((0,), (0,)), ((), ())), preferred_element_type=jnp.float32)
+    for part in range(2):
+        place = 2 * step + part
+        ahead = lax.rem(place - here[2] + NZ, NZ)
+        for low in range(2):
+            near = lax.bitwise_xor(low, here[1])
+            lanes = jnp.concatenate([features[ahead, 3 * near + n] for n in range(3)], axis=0)
+            total += lax.dot_general(
+                lanes, partial[low, part], (((0,), (0,)), ((), ())), preferred_element_type=jnp.float32)
     gradient[...] = total
 
 
-def combine(own, other, pieces, places, here):
-    width = own.shape[-1]
-    block = pl.BlockSpec((2, 1, 192, width), lambda d, here: (0, d, 0, 0))
+def features_product(partial, pieces, places, here):
+    width = partial.shape[-1]
     return pl.pallas_call(
-        lambda *refs: combine_kernel(places, *refs),
-        out_shape=(
-            jax.ShapeDtypeStruct((2, NZ, 192, width), jnp.bfloat16),
-            jax.ShapeDtypeStruct((width, width), jnp.float32),
-        ),
+        lambda *refs: features_kernel(places, *refs),
+        out_shape=jax.ShapeDtypeStruct((width, width), jnp.float32),
         grid_spec=pltpu.PrefetchScalarGridSpec(
             num_scalar_prefetch=1,
-            grid=(NZ,),
-            in_specs=[block, block] + [pl.BlockSpec(memory_space=pl.ANY)] * NZ,
-            out_specs=(block, pl.BlockSpec((width, width), lambda d, here: (0, 0))),
+            grid=(NZ // 2,),
+            in_specs=[pl.BlockSpec((2, 2, 192, width), lambda d, here: (0, d, 0, 0))]
+            + [pl.BlockSpec(memory_space=pl.ANY)] * NZ,
+            out_specs=pl.BlockSpec((width, width), lambda d, here: (0, 0)),
             scratch_shapes=[pltpu.VMEM((NZ, 6, 64, width), jnp.bfloat16), pltpu.SemaphoreType.DMA((NZ,))],
         ),
         compiler_params=pltpu.CompilerParams(vmem_limit_bytes=56 << 20),
-        cost_estimate=pl.CostEstimate(flops=2 * 3072 * width * width, bytes_accessed=8 << 20, transcendentals=0),
-        name="combine_cores",
-    )(here, own.reshape(2, NZ, 192, width), other.reshape(2, NZ, 192, width), *pieces)
-
-
-def pick_kernel(side, tiles, picked):
-    picked[...] = tiles[:, 0]
+        cost_estimate=pl.CostEstimate(flops=2 * 3072 * width * width, bytes_accessed=4 << 20, transcendentals=0),
+        name="features_product",
+    )(here, partial, *pieces)
+
+
+def pick_kernel(side, tiles, picked, held, in_sem, out_sem):
+    groups = range(picked.shape[0])
+    reads = [pltpu.make_async_copy(tiles.at[g, side[0]], held.at[g], in_sem.at[g]) for g in groups]
+    writes = [pltpu.make_async_copy(held.at[g], picked.at[g], out_sem.at[g]) for g in groups]
+    for read in reads:
+        read.start()
+    for read, write in zip(reads, writes):
+        read.wait()
+        write.start()
+    for write in writes:
+        write.wait()
 
 
 def pick(tiles, side):
@@ -189,10 +196,16 @@
         out_shape=jax.ShapeDtypeStruct((groups, slots, block, block), tiles.dtype),
         grid_spec=pltpu.PrefetchScalarGridSpec(
             num_scalar_prefetch=1,
-            grid=(groups,),
-            in_specs=[pl.BlockSpec((1, 1, slots, block, block), lambda g, side: (g, side[0], 0, 0, 0))],
-            out_specs=pl.BlockSpec((1, slots, block, block), lambda g, side: (g, 0, 0, 0)),
+            grid=(),
+            in_specs=[pl.BlockSpec(memory_space=pl.ANY)],
+            out_specs=pl.BlockSpec(memory_space=pl.ANY),
+            scratch_shapes=[
+                pltpu.VMEM((groups, slots, block, block), tiles.dtype),
+                pltpu.SemaphoreType.DMA((groups,)),
+                pltpu.SemaphoreType.DMA((groups,)),
+            ],
         ),
+        compiler_params=pltpu.CompilerParams(vmem_limit_bytes=16 << 20),
         cost_estimate=pl.CostEstimate(flops=0, bytes_accessed=12 << 20, transcendentals=0),
         name="pick_tiles",
     )(side.reshape(1).astype(jnp.int32), tiles)
@@ -255,11 +268,9 @@
     full_line = spread_over(full, z_lines())
     half_line = jnp.stack([half] + [send(half, along_s(-d)) for d in (1, 2, 3)])
     half_q = [half_line] + [send(half_line, along_q(-d)) for d in (1, 2, 3)]
-    picked = pick(by_parity, 1 - core)
     half_plane = jnp.concatenate(
         half_q + [rooted_features.reshape(-1, 64, width), far_features.reshape(-1, 64, width)])
-    half_plane, full_line, picked = together(half_plane, full_line, picked)
-    received = send(picked, flip)
+    half_plane, full_line = together(half_plane, full_line)
     half_z = {0: [half_plane]}
     behind, ahead = ring_first(half_plane, along_z)
     half_z[7], half_z[1] = [behind], [ahead]
@@ -267,15 +278,18 @@
     q_behind, q_ahead = ring_first(full_line, along_q)
     full_q[3], full_q[1], full_q[2] = [q_behind], [q_ahead], ring_last(q_behind, q_ahead, along_q)
     full_plane = stacked([full_q[d] for d in range(4)])
-    full_plane, behind, ahead = together(full_plane, behind, ahead)
-    full_s = {0: [full_plane]}
-    s_behind, s_ahead = ring_first(full_plane, along_s)
-    full_s[3], full_s[1], full_s[2] = [s_behind], [s_ahead], ring_last(s_behind, s_ahead, along_s)
+    full_plane, behind, ahead, side = together(full_plane, behind, ahead, 1 - core)
+    first, second = full_plane[:2], full_plane[2:]
+    first_behind, second_ahead = send(first, along_s(1)), send(second, along_s(-1))
+    second_behind, first_ahead = send(second, along_s(1)), send(first, along_s(-1))
+    full_s = [[first, second], [first_ahead, second_ahead],
+              [send(first_behind, along_s(1)), send(second_ahead, along_s(-1))], [first_behind, second_behind]]
+    received = send(pick(by_parity, side), flip)
     for d in (2, 3):
         behind, ahead = send(behind, along_z(1)), send(ahead, along_z(-1))
         half_z[NZ - d], half_z[d] = [behind], [ahead]
     half_z[4] = ring_last(behind, ahead, along_z)
-    full_found = [full_s[d] for d in range(4)]
+    full_found = full_s
     half_found = [half_z[d] for d in range(NZ)]
 
     codes = jnp.stack([kept_codes, received_codes])
@@ -317,7 +331,8 @@
 
     here = jnp.stack([core, own_rep // NZ, z]).astype(jnp.int32)
     own, other = products(by_parity, received, chunks, places, counts, unit0, unit1, columns, here)
-    partial, local_weight = combine(own, send(other, flip), feature_pieces, feature_places, here)
+    partial = (own + send(other, flip).astype(jnp.float32)).astype(jnp.bfloat16).reshape(2, NZ, -1, width)
+    local_weight = features_product(partial, feature_pieces, feature_places, here)
     near = lax.dynamic_index_in_dim(partial, own_rep // NZ, 0, keepdims=False)
     across = send(lax.dynamic_index_in_dim(partial, 1 - own_rep // NZ, 0, keepdims=False), across_x())
     own_rows = lax.all_to_all(local_weight, "rep", 0, 0, tiled=True).reshape(16, 16, width).sum(axis=0)

time: 225 us -> 219 us (0.973)
  Pallas kernels: 38.9 us -> 31.7 us
  waiting for transfers between devices: 91.6 us -> 97.2 us
  other arithmetic: 5.42 us -> 10.1 us
  starting transfers between devices: 70.1 us -> 65.7 us
  local copies, waits for them, and re-layouts: 13.7 us -> 10.5 us
    slice x6 -> x4, local copies, waits for them, and re-layouts: 5.66 us -> 0.09 us  [ring_last(): return [send(behind[:half], along(1)), send(ahead[half:], along(-1))]]
    all_to_all x1, waiting for transfers between devices: 0.01 us -> 5.49 us  [spread_over(): lax.all_to_all(copies, BOTH, 0, 0, axis_index_groups=places, tiled=True)]
    pallas_call x1, Pallas kernels: 7.83 us -> 3.26 us  [pick(): pl.pallas_call(pick_kernel, out_shape=jax.ShapeDtypeStruct((groups, slots...]
    pallas_call x1, Pallas kernels: 9.23 us -> 5.96 us  [features_product(): pl.pallas_call(lambda *refs: features_kernel(places, *refs), out_shape=ja...]
    all_to_all x1, waiting for transfers between devices: 13.3 us -> 10.1 us  [body(): lax.all_to_all(local_weight, 'rep', 0, 0, tiled=True).reshape(16, 16, width)]
    all_to_all x1, starting transfers between devices: 7.71 us -> 4.85 us  [body(): lax.all_to_all(line, BOTH, 0, 0, axis_index_groups=z_lines(), tiled=True)]
    convert_element_type x0 -> x1, other arithmetic: none -> 2.37 us  [body(): (own + send(other, flip).astype(jnp.float32)).astype(jnp.bfloat16)]
    ppermute x31 -> x33, waiting for transfers between devices: 64.1 us -> 66.3 us  [send(): return lax.ppermute(value, BOTH, moves)]
  transfers between devices with their start and end apart: 35 -> 37, of which waited for: 21 -> 20; matrix products, arithmetic and copies ran while one was open for 5% -> 4% of each run, Pallas kernels for 4% -> 3%
where the time goes in v4:
time: 219 us; the launch traced here: 217 us
  waiting for transfers between devices  97.2 us (44%)
  starting transfers between devices  65.7 us (30%)
  Pallas kernels  31.7 us (14%)
  local copies, waits for them, and re-layouts  10.5 us (5%)
  other arithmetic  10.1 us (5%)
    ppermute x33, waiting for transfers between devices, send(): return lax.ppermute(value, BOTH, moves)  66.3 us
    ppermute x33, starting transfers between devices, send(): return lax.ppermute(value, BOTH, moves)  40.1 us
    pallas_call x1, Pallas kernels, products(): pl.pallas_call(lambda *refs: products_kernel(places, *refs), out_shape=(j...  22.5 us
    all_to_all x1, waiting for transfers between devices, body(): lax.all_to_all(local_weight, 'rep', 0, 0, tiled=True).reshape(16, 16, width)  10.1 us
    all_to_all x1, waiting for transfers between devices, body(): weight_grad = lax.all_to_all(spread, 'rep', 0, 0, tiled=True)  9.6 us
    all_to_all x1, starting transfers between devices, spread_over(): lax.all_to_all(copies, BOTH, 0, 0, axis_index_groups=places, tiled=True)  8.58 us
    all_to_all x1, starting transfers between devices, body(): lax.all_to_all(local_weight, 'rep', 0, 0, tiled=True).reshape(16, 16, width)  7.38 us
    unnamed x35, local copies, waits for them, and re-layouts  6.16 us
  transfers between devices with their start and end apart: 37, of which 20 were waited for; matrix products, arithmetic and copies ran while one was open for 4% of the time, Pallas kernels for 3%

profile of v4, /device:TPU:32, one launch (start us, length us, event | category | flops | bytes accessed | tf_op | source)
XLA Modules:
  0.0 217.1 jit_solution(17352106788640620297)
XLA Ops:
  2.5 3.1 %collective-permute-start.2 = (bf16[64,256]{1,0:T(8,128)(2,1)S(1)}, bf16[64,256]{1,0:T(8,128)(2,1)S(1)}, u32[]{:S(2)}, u32[]{:S(2)}) collective-permute-start(bf16[64,256]{1,0:T(8,128)(2,1)S(1)} %get-tuple-element.27), channel_id=1, source_target_pairs={{0,128},{16,80},{1,129},{17,81},{2,130},{18,82},{3,131},{19,83},{4... | collective-permute-start | bytes 98312 | tf_op jit(solution)/shard_map/ppermute | solution.py:67
  6.2 2.6 %collective-permute-start.1 = (bf16[64,256]{1,0:T(8,128)(2,1)S(1)}, bf16[64,256]{1,0:T(8,128)(2,1)S(1)}, u32[]{:S(2)}, u32[]{:S(2)}) collective-permute-start(bf16[64,256]{1,0:T(8,128)(2,1)S(1)} %get-tuple-element.27), channel_id=1, source_target_pairs={{0,136},{16,112},{1,137},{17,113},{2,138},{18,114},{3,139},{19,115... | collective-permute-start | bytes 98312 | tf_op jit(solution)/shard_map/ppermute | solution.py:67
  9.7 8.6 %all-to-all-start = ((bf16[8,128,256]{2,1,0:T(8,128)(2,1)}), bf16[8,128,256]{2,1,0:T(8,128)(2,1)S(1)}, u32[]{:S(2)}, u32[]{:S(2)}) async-start(bf16[8,128,256]{2,1,0:T(8,128)(2,1)} %broadcast_in_dim.42), calls=%async_computation | async-start | bytes 1048576 | tf_op jit(solution)/shard_map/all_to_all | solution.py:43
  18.3 3.1 %collective-permute-start.4 = (bf16[4,64,256]{2,1,0:T(8,128)(2,1)S(1)}, bf16[4,64,256]{2,1,0:T(8,128)(2,1)S(1)}, u32[]{:S(2)}, u32[]{:S(2)}) collective-permute-start(bf16[4,64,256]{2,1,0:T(8,128)(2,1)S(1)} %pad_maximum_fusion.1), channel_id=1, source_target_pairs={{0,96},{16,152},{1,97},{17,153},{2,98},{18,154},{3,99},{19,155},{4... | collective-permute-start | bytes 393224 | tf_op jit(solution)/shard_map/ppermute | solution.py:67
  25.3 2.6 %collective-permute-done.5 = bf16[4,64,256]{2,1,0:T(8,128)(2,1)S(1)} collective-permute-done((bf16[4,64,256]{2,1,0:T(8,128)(2,1)S(1)}, bf16[4,64,256]{2,1,0:T(8,128)(2,1)S(1)}, u32[]{:S(2)}, u32[]{:S(2)}) %collective-permute-start.5) | collective-permute-done | bytes 131104 | tf_op jit(solution)/shard_map/ppermute | solution.py:67
  29.3 5.5 %all-to-all-done = bf16[8,128,256]{2,1,0:T(8,128)(2,1)S(1)} async-done(((bf16[8,128,256]{2,1,0:T(8,128)(2,1)}), bf16[8,128,256]{2,1,0:T(8,128)(2,1)S(1)}, u32[]{:S(2)}, u32[]{:S(2)}) %all-to-all-start) | async-done | bytes 524320 | tf_op jit(solution)/shard_map/all_to_all | solution.py:43
  34.8 3.2 %collective-permute-start.8 = (bf16[8,128,256]{2,1,0:T(8,128)(2,1)S(1)}, bf16[8,128,256]{2,1,0:T(8,128)(2,1)S(1)}, u32[]{:S(2)}, u32[]{:S(2)}) collective-permute-start(bf16[8,128,256]{2,1,0:T(8,128)(2,1)S(1)} %all-to-all-done), channel_id=1, source_target_pairs={{0,96},{16,152},{1,97},{17,153},{2,98},{18,154},{3,99},{19,155},{4... | collective-permute-start | bytes 1572872 | tf_op jit(solution)/shard_map/ppermute | solution.py:67
  40.1 5.1 %collective-permute-done.9 = bf16[8,128,256]{2,1,0:T(8,128)(2,1)S(1)} collective-permute-done((bf16[8,128,256]{2,1,0:T(8,128)(2,1)S(1)}, bf16[8,128,256]{2,1,0:T(8,128)(2,1)S(1)}, u32[]{:S(2)}, u32[]{:S(2)}) %collective-permute-start.9) | collective-permute-done | bytes 524320 | tf_op jit(solution)/shard_map/ppermute | solution.py:67
  45.4 3.3 %collective-permute-start.11 = (bf16[4,128,256]{2,1,0:T(8,128)(2,1)S(1)}, bf16[4,128,256]{2,1,0:T(8,128)(2,1)S(1)}, u32[]{:S(2)}, u32[]{:S(2)}) collective-permute-start(bf16[4,128,256]{2,1,0:T(8,128)(2,1)S(1)} %slice.25), channel_id=1, source_target_pairs={{0,96},{16,152},{1,97},{17,153},{2,98},{18,154},{3,99},{19,155},{4... | collective-permute-start | bytes 786440 | tf_op jit(solution)/shard_map/ppermute | solution.py:67
  48.7 4.2 %collective-permute-done.10 = bf16[4,128,256]{2,1,0:T(8,128)(2,1)S(1)} collective-permute-done((bf16[4,128,256]{2,1,0:T(8,128)(2,1)S(1)}, bf16[4,128,256]{2,1,0:T(8,128)(2,1)S(1)}, u32[]{:S(2)}, u32[]{:S(2)}) %collective-permute-start.10) | collective-permute-done | bytes 262176 | tf_op jit(solution)/shard_map/ppermute | solution.py:67
  55.4 4.6 %copy-done.1 = bf16[16,24,128,128]{3,2,1,0:T(8,128)(2,1)S(1)} copy-done((bf16[16,24,128,128]{3,2,1,0:T(8,128)(2,1)S(1)}, bf16[16,24,128,128]{3,2,1,0:T(8,128)(2,1)}, u32[]{:S(2)}) %copy-start.1) | copy-done | bytes 12582936
  60.0 3.3 %pick_tiles.1 = bf16[8,24,128,128]{3,2,1,0:T(8,128)(2,1)} custom-call(s32[1]{0:T(128)} %bitcast.18.side, bf16[8,2,24,128,128]{4,3,2,1,0:T(8,128)(2,1)S(1)} %bitcast.42), custom_call_target="tpu_custom_call" | custom-call | bytes 12582912 | tf_op jit(solution)/shard_map/pick_tiles/pallas_call | solution.py:194
  64.0 3.0 %collective-permute-start.21 = (bf16[22,64,256]{2,1,0:T(8,128)(2,1)}, bf16[22,64,256]{2,1,0:T(8,128)(2,1)}, u32[]{:S(2)}, u32[]{:S(2)}) collective-permute-start(bf16[22,64,256]{2,1,0:T(8,128)(2,1)} %collective-permute-done.13.refs_16_.refs_3_), channel_id=1, source_target_pairs={{0,7},{16,23},{1,0},{17,16},{2,1},{18,17},{3,2},{19,18},{4,3},{20,... | collective-permute-start | bytes 2162696 | tf_op jit(solution)/shard_map/ppermute | solution.py:67
  71.6 12.2 %collective-permute-done.23.refs_22_.refs_8_ = bf16[22,64,256]{2,1,0:T(8,128)(2,1)} collective-permute-done((bf16[22,64,256]{2,1,0:T(8,128)(2,1)}, bf16[22,64,256]{2,1,0:T(8,128)(2,1)}, u32[]{:S(2)}, u32[]{:S(2)}) %collective-permute-start.23) | collective-permute-done | bytes 720928 | tf_op jit(solution)/shard_map/ppermute | solution.py:67
  83.8 3.0 %collective-permute-start.22 = (bf16[22,64,256]{2,1,0:T(8,128)(2,1)}, bf16[22,64,256]{2,1,0:T(8,128)(2,1)S(1)}, u32[]{:S(2)}, u32[]{:S(2)}) collective-permute-start(bf16[22,64,256]{2,1,0:T(8,128)(2,1)} %collective-permute-done.21.refs_17_.refs_4_), channel_id=1, source_target_pairs={{0,7},{16,23},{1,0},{17,16},{2,1},{18,17},{3,2},{19,18},{4,3},{20,... | collective-permute-start | bytes 2162696 | tf_op jit(solution)/shard_map/ppermute | solution.py:67
  88.8 13.9 %collective-permute-done.24.refs_21_.refs_7_ = bf16[22,64,256]{2,1,0:T(8,128)(2,1)S(1)} collective-permute-done((bf16[22,64,256]{2,1,0:T(8,128)(2,1)}, bf16[22,64,256]{2,1,0:T(8,128)(2,1)S(1)}, u32[]{:S(2)}, u32[]{:S(2)}) %collective-permute-start.24) | collective-permute-done | bytes 720928 | tf_op jit(solution)/shard_map/ppermute | solution.py:67
  102.7 3.2 %collective-permute-start.19 = (bf16[2,8,128,256]{3,2,1,0:T(8,128)(2,1)}, bf16[2,8,128,256]{3,2,1,0:T(8,128)(2,1)}, u32[]{:S(2)}, u32[]{:S(2)}) collective-permute-start(bf16[2,8,128,256]{3,2,1,0:T(8,128)(2,1)} %collective-permute-done.16), channel_id=1, source_target_pairs={{0,136},{16,112},{1,137},{17,113},{2,138},{18,114},{3,139},{19,115... | collective-permute-start | bytes 3145736 | tf_op jit(solution)/shard_map/ppermute | solution.py:67
  108.1 3.0 %collective-permute-start.26 = (bf16[11,64,256]{2,1,0:T(8,128)(2,1)S(1)}, bf16[11,64,256]{2,1,0:T(8,128)(2,1)S(1)}, u32[]{:S(2)}, u32[]{:S(2)}) collective-permute-start(bf16[11,64,256]{2,1,0:T(8,128)(2,1)S(1)} %slice.27), channel_id=1, source_target_pairs={{0,7},{16,23},{1,0},{17,16},{2,1},{18,17},{3,2},{19,18},{4,3},{20,... | collective-permute-start | bytes 1081352 | tf_op jit(solution)/shard_map/ppermute | solution.py:67
  112.4 5.3 %collective-permute-done.25.refs_19_ = bf16[11,64,256]{2,1,0:T(8,128)(2,1)S(1)} collective-permute-done((bf16[11,64,256]{2,1,0:T(8,128)(2,1)S(1)}, bf16[11,64,256]{2,1,0:T(8,128)(2,1)S(1)}, u32[]{:S(2)}, u32[]{:S(2)}) %collective-permute-start.25) | collective-permute-done | bytes 360480 | tf_op jit(solution)/shard_map/ppermute | solution.py:67
  118.9 22.5 %tile_products.1 = (f32[24,128,256]{2,1,0:T(8,128)}, bf16[24,128,256]{2,1,0:T(8,128)(2,1)}) custom-call(s32[16]{0:T(128)} %min.8.refs_0_, s32[384]{0:T(512)} %fusion.9.refs_1_, s32[384]{0:T(512)} %get-tuple-element.28.refs_2_, s32[384]{0:T(512)} %get-tuple-element.37.refs_3_, s32[3]{0:T(128)} %pad_add_fusion.1.refs_4_.refs_0_, ...), custom_call_target="tpu_custom_call" | custom-call | flops 3221225472 | bytes 31457280 | tf_op jit(solution)/shard_map/tile_products/pallas_call | solution.py:217
  141.5 3.6 %collective-permute-done.27 = bf16[24,128,256]{2,1,0:T(8,128)(2,1)S(1)} collective-permute-done((bf16[24,128,256]{2,1,0:T(8,128)(2,1)}, bf16[24,128,256]{2,1,0:T(8,128)(2,1)S(1)}, u32[]{:S(2)}, u32[]{:S(2)}) %collective-permute-start.27) | collective-permute-done | bytes 1572896 | tf_op jit(solution)/shard_map/ppermute | solution.py:67
  148.6 6.0 %features_product.1 = f32[256,256]{1,0:T(8,128)} custom-call(s32[3]{0:T(128)} %pad_add_fusion.1.refs_4_.refs_0_, bf16[2,8,192,256]{3,2,1,0:T(8,128)(2,1)} %bitcast.44, bf16[22,64,256]{2,1,0:T(8,128)(2,1)} %copy-done.5, bf16[22,64,256]{2,1,0:T(8,128)(2,1)} %collective-permute-done.13.refs_16_.refs_3_, ...), custom_call_target="tpu_custom_call" | custom-call | flops 402653184 | bytes 4194304 | tf_op jit(solution)/shard_map/features_product/pallas_call | solution.py:162
  154.6 7.4 %all-to-all-start.1 = ((f32[16,16,256]{2,1,0:T(8,128)}), f32[16,16,256]{2,1,0:T(8,128)S(1)}, u32[]{:S(2)}, u32[]{:S(2)}) async-start(f32[16,16,256]{2,1,0:T(8,128)} %bitcast.49), calls=%async_computation.1 | async-start | bytes 524288 | tf_op jit(solution)/shard_map/all_to_all | solution.py:338
  162.0 10.1 %all-to-all-done.1 = f32[16,16,256]{2,1,0:T(8,128)S(1)} async-done(((f32[16,16,256]{2,1,0:T(8,128)}), f32[16,16,256]{2,1,0:T(8,128)S(1)}, u32[]{:S(2)}, u32[]{:S(2)}) %all-to-all-start.1) | async-done | bytes 262176 | tf_op jit(solution)/shard_map/all_to_all | solution.py:338
  174.3 4.9 %all-to-all-start.2 = ((bf16[8,192,256]{2,1,0:T(8,128)(2,1)}), bf16[8,192,256]{2,1,0:T(8,128)(2,1)S(1)}, u32[]{:S(2)}, u32[]{:S(2)}) async-start(bf16[8,192,256]{2,1,0:T(8,128)(2,1)} %fusion), calls=%async_computation.2 | async-start | bytes 1572864 | tf_op jit(solution)/shard_map/all_to_all | solution.py:341
  180.3 2.5 %collective-permute-start.30 = (f32[16,256]{1,0:T(8,128)S(1)}, f32[16,256]{1,0:T(8,128)S(1)}, u32[]{:S(2)}, u32[]{:S(2)}) collective-permute-start(f32[16,256]{1,0:T(8,128)S(1)} %add.256), channel_id=1, source_target_pairs={{0,128},{16,144},{1,129},{17,145},{2,130},{18,146},{3,131},{19,147... | collective-permute-start | bytes 49160 | tf_op jit(solution)/shard_map/ppermute | solution.py:67
  182.8 2.8 %collective-permute-done.30 = f32[16,256]{1,0:T(8,128)S(1)} collective-permute-done((f32[16,256]{1,0:T(8,128)S(1)}, f32[16,256]{1,0:T(8,128)S(1)}, u32[]{:S(2)}, u32[]{:S(2)}) %collective-permute-start.30) | collective-permute-done | bytes 16416 | tf_op jit(solution)/shard_map/ppermute | solution.py:67
  185.7 3.6 %collective-permute-done.31 = f32[16,256]{1,0:T(8,128)S(1)} collective-permute-done((f32[16,256]{1,0:T(8,128)S(1)}, f32[16,256]{1,0:T(8,128)S(1)}, u32[]{:S(2)}, u32[]{:S(2)}) %collective-permute-start.31) | collective-permute-done | bytes 16416 | tf_op jit(solution)/shard_map/ppermute | solution.py:67
  190.6 4.0 %collective-permute-done.32 = f32[16,256]{1,0:T(8,128)S(1)} collective-permute-done((f32[16,256]{1,0:T(8,128)S(1)}, f32[16,256]{1,0:T(8,128)S(1)}, u32[]{:S(2)}, u32[]{:S(2)}) %collective-permute-start.32) | collective-permute-done | bytes 16416 | tf_op jit(solution)/shard_map/ppermute | solution.py:67
  194.6 5.7 %all-to-all-done.2 = bf16[8,192,256]{2,1,0:T(8,128)(2,1)S(1)} async-done(((bf16[8,192,256]{2,1,0:T(8,128)(2,1)}), bf16[8,192,256]{2,1,0:T(8,128)(2,1)S(1)}, u32[]{:S(2)}, u32[]{:S(2)}) %all-to-all-start.2) | async-done | bytes 786464 | tf_op jit(solution)/shard_map/all_to_all | solution.py:341
  201.0 4.8 %all-to-all-start.3 = ((f32[16,16,256]{2,1,0:T(8,128)}), f32[16,16,256]{2,1,0:T(8,128)S(1)}, u32[]{:S(2)}, u32[]{:S(2)}) async-start(f32[16,16,256]{2,1,0:T(8,128)} %broadcast_in_dim.43), calls=%async_computation.3 | async-start | bytes 524288 | tf_op jit(solution)/shard_map/all_to_all | solution.py:346
  206.8 9.6 %all-to-all-done.3 = f32[16,16,256]{2,1,0:T(8,128)S(1)} async-done(((f32[16,16,256]{2,1,0:T(8,128)}), f32[16,16,256]{2,1,0:T(8,128)S(1)}, u32[]{:S(2)}, u32[]{:S(2)}) %all-to-all-start.3) | async-done | bytes 262176 | tf_op jit(solution)/shard_map/all_to_all | solution.py:346
  (122 shorter events, 35.8 us)
Async XLA Ops:
  2.5 15.8 %collective-permute-start.2 = (bf16[64,256]{1,0:T(8,128)(2,1)S(1)}, bf16[64,256]{1,0:T(8,128)(2,1)S(1)}, u32[]{:S(2)}, u32[]{:S(2)}) collective-permute-start(bf16[64,256]{1,0:T(8,128)(2,1)S(1)} %get-tuple-element.27), channel_id=1, source_target_pairs={{0,128},{16,80},{1,129},{17,81},{2,130},{18,82},{3,131},{19,83},{4... | collective-permute-start | bytes 98312 | tf_op jit(solution)/shard_map/ppermute | solution.py:67
  5.6 12.7 %collective-permute-start.3 = (bf16[64,256]{1,0:T(8,128)(2,1)S(1)}, bf16[64,256]{1,0:T(8,128)(2,1)S(1)}, u32[]{:S(2)}, u32[]{:S(2)}) collective-permute-start(bf16[64,256]{1,0:T(8,128)(2,1)S(1)} %get-tuple-element.27), channel_id=1, source_target_pairs={{0,8},{16,48},{1,9},{17,49},{2,10},{18,50},{3,11},{19,51},{4,12},{... | collective-permute-start | bytes 98312 | tf_op jit(solution)/shard_map/ppermute | solution.py:67
  6.2 12.1 %collective-permute-start.1 = (bf16[64,256]{1,0:T(8,128)(2,1)S(1)}, bf16[64,256]{1,0:T(8,128)(2,1)S(1)}, u32[]{:S(2)}, u32[]{:S(2)}) collective-permute-start(bf16[64,256]{1,0:T(8,128)(2,1)S(1)} %get-tuple-element.27), channel_id=1, source_target_pairs={{0,136},{16,112},{1,137},{17,113},{2,138},{18,114},{3,139},{19,115... | collective-permute-start | bytes 98312 | tf_op jit(solution)/shard_map/ppermute | solution.py:67
  8.8 20.5 %collective-permute-start.7 = (bf16[192,256]{1,0:T(8,128)(2,1)S(1)}, bf16[192,256]{1,0:T(8,128)(2,1)S(1)}, u32[]{:S(2)}, u32[]{:S(2)}) collective-permute-start(bf16[192,256]{1,0:T(8,128)(2,1)S(1)} %get-tuple-element.38), channel_id=1, source_target_pairs={{0,8},{16,24},{1,9},{17,25},{2,10},{18,26},{3,11},{19,27},{4,12},{... | collective-permute-start | bytes 294920 | tf_op jit(solution)/shard_map/ppermute | solution.py:67
  9.7 25.1 %all-to-all-start = ((bf16[8,128,256]{2,1,0:T(8,128)(2,1)}), bf16[8,128,256]{2,1,0:T(8,128)(2,1)S(1)}, u32[]{:S(2)}, u32[]{:S(2)}) async-start(bf16[8,128,256]{2,1,0:T(8,128)(2,1)} %broadcast_in_dim.42), calls=%async_computation | async-start | bytes 1048576 | tf_op jit(solution)/shard_map/all_to_all | solution.py:43
  18.3 7.0 %collective-permute-start.4 = (bf16[4,64,256]{2,1,0:T(8,128)(2,1)S(1)}, bf16[4,64,256]{2,1,0:T(8,128)(2,1)S(1)}, u32[]{:S(2)}, u32[]{:S(2)}) collective-permute-start(bf16[4,64,256]{2,1,0:T(8,128)(2,1)S(1)} %pad_maximum_fusion.1), channel_id=1, source_target_pairs={{0,96},{16,152},{1,97},{17,153},{2,98},{18,154},{3,99},{19,155},{4... | collective-permute-start | bytes 393224 | tf_op jit(solution)/shard_map/ppermute | solution.py:67
  21.4 6.6 %collective-permute-start.5 = (bf16[4,64,256]{2,1,0:T(8,128)(2,1)S(1)}, bf16[4,64,256]{2,1,0:T(8,128)(2,1)S(1)}, u32[]{:S(2)}, u32[]{:S(2)}) collective-permute-start(bf16[4,64,256]{2,1,0:T(8,128)(2,1)S(1)} %pad_maximum_fusion.1), channel_id=1, source_target_pairs={{0,64},{16,144},{1,65},{17,145},{2,66},{18,146},{3,67},{19,147},{4... | collective-permute-start | bytes 393224 | tf_op jit(solution)/shard_map/ppermute | solution.py:67
  22.0 7.2 %collective-permute-start.6 = (bf16[4,64,256]{2,1,0:T(8,128)(2,1)S(1)}, bf16[4,64,256]{2,1,0:T(8,128)(2,1)S(1)}, u32[]{:S(2)}, u32[]{:S(2)}) collective-permute-start(bf16[4,64,256]{2,1,0:T(8,128)(2,1)S(1)} %pad_maximum_fusion.1), channel_id=1, source_target_pairs={{0,32},{16,24},{1,33},{17,25},{2,34},{18,26},{3,35},{19,27},{4,36}... | collective-permute-start | bytes 393224 | tf_op jit(solution)/shard_map/ppermute | solution.py:67
  34.8 10.4 %collective-permute-start.9 = (bf16[8,128,256]{2,1,0:T(8,128)(2,1)S(1)}, bf16[8,128,256]{2,1,0:T(8,128)(2,1)S(1)}, u32[]{:S(2)}, u32[]{:S(2)}) collective-permute-start(bf16[8,128,256]{2,1,0:T(8,128)(2,1)S(1)} %all-to-all-done), channel_id=1, source_target_pairs={{0,32},{16,24},{1,33},{17,25},{2,34},{18,26},{3,35},{19,27},{4,36}... | collective-permute-start | bytes 1572872 | tf_op jit(solution)/shard_map/ppermute | solution.py:67
  34.8 10.5 %collective-permute-start.8 = (bf16[8,128,256]{2,1,0:T(8,128)(2,1)S(1)}, bf16[8,128,256]{2,1,0:T(8,128)(2,1)S(1)}, u32[]{:S(2)}, u32[]{:S(2)}) collective-permute-start(bf16[8,128,256]{2,1,0:T(8,128)(2,1)S(1)} %all-to-all-done), channel_id=1, source_target_pairs={{0,96},{16,152},{1,97},{17,153},{2,98},{18,154},{3,99},{19,155},{4... | collective-permute-start | bytes 1572872 | tf_op jit(solution)/shard_map/ppermute | solution.py:67
  38.1 17.3 %collective-permute-start.12 = (bf16[22,64,256]{2,1,0:T(8,128)(2,1)S(1)}, bf16[22,64,256]{2,1,0:T(8,128)(2,1)}, u32[]{:S(2)}, u32[]{:S(2)}) collective-permute-start(bf16[22,64,256]{2,1,0:T(8,128)(2,1)S(1)} %constant_dynamic-update-slice_fusion.refs_15_.refs_2_), channel_id=1, source_target_pairs={{0,1},{16,17},{1,2},{17,18},{2,3},{18,19},{3,4},{19,20},{4,5},{20,... | collective-permute-start | bytes 2162696 | tf_op jit(solution)/shard_map/ppermute | solution.py:67
  38.1 17.3 %collective-permute-start.13 = (bf16[22,64,256]{2,1,0:T(8,128)(2,1)S(1)}, bf16[22,64,256]{2,1,0:T(8,128)(2,1)}, u32[]{:S(2)}, u32[]{:S(2)}) collective-permute-start(bf16[22,64,256]{2,1,0:T(8,128)(2,1)S(1)} %constant_dynamic-update-slice_fusion.refs_15_.refs_2_), channel_id=1, source_target_pairs={{0,7},{16,23},{1,0},{17,16},{2,1},{18,17},{3,2},{19,18},{4,3},{20,... | collective-permute-start | bytes 2162696 | tf_op jit(solution)/shard_map/ppermute | solution.py:67
  45.2 7.7 %collective-permute-start.10 = (bf16[4,128,256]{2,1,0:T(8,128)(2,1)S(1)}, bf16[4,128,256]{2,1,0:T(8,128)(2,1)S(1)}, u32[]{:S(2)}, u32[]{:S(2)}) collective-permute-start(bf16[4,128,256]{2,1,0:T(8,128)(2,1)S(1)} %slice.24), channel_id=1, source_target_pairs={{0,32},{16,24},{1,33},{17,25},{2,34},{18,26},{3,35},{19,27},{4,36}... | collective-permute-start | bytes 786440 | tf_op jit(solution)/shard_map/ppermute | solution.py:67
  45.4 7.5 %collective-permute-start.11 = (bf16[4,128,256]{2,1,0:T(8,128)(2,1)S(1)}, bf16[4,128,256]{2,1,0:T(8,128)(2,1)S(1)}, u32[]{:S(2)}, u32[]{:S(2)}) collective-permute-start(bf16[4,128,256]{2,1,0:T(8,128)(2,1)S(1)} %slice.25), channel_id=1, source_target_pairs={{0,96},{16,152},{1,97},{17,153},{2,98},{18,154},{3,99},{19,155},{4... | collective-permute-start | bytes 786440 | tf_op jit(solution)/shard_map/ppermute | solution.py:67
  63.2 55.6 %collective-permute-start.14 = (bf16[8,24,128,128]{3,2,1,0:T(8,128)(2,1)}, bf16[8,24,128,128]{3,2,1,0:T(8,128)(2,1)}, u32[]{:S(2)}, u32[]{:S(2)}) collective-permute-start(bf16[8,24,128,128]{3,2,1,0:T(8,128)(2,1)} %pick_tiles.1), channel_id=1, source_target_pairs={{0,16},{16,0},{1,17},{17,1},{2,18},{18,2},{3,19},{19,3},{4,20},{20... | collective-permute-start | bytes 18874376 | tf_op jit(solution)/shard_map/ppermute | solution.py:67
  63.4 7.0 %collective-permute-start = (s32[8,24]{1,0:T(8,128)S(1)}, s32[8,24]{1,0:T(8,128)S(1)}, u32[]{:S(2)}, u32[]{:S(2)}) collective-permute-start(s32[8,24]{1,0:T(8,128)S(1)} %bitcast.60), channel_id=1, source_target_pairs={{0,16},{16,0},{1,17},{17,1},{2,18},{18,2},{3,19},{19,3},{4,20},{20... | collective-permute-start | bytes 2312 | tf_op jit(solution)/shard_map/ppermute | solution.py:67
  64.0 19.8 %collective-permute-start.23 = (bf16[22,64,256]{2,1,0:T(8,128)(2,1)}, bf16[22,64,256]{2,1,0:T(8,128)(2,1)}, u32[]{:S(2)}, u32[]{:S(2)}) collective-permute-start(bf16[22,64,256]{2,1,0:T(8,128)(2,1)} %collective-permute-done.12.refs_23_.refs_9_), channel_id=1, source_target_pairs={{0,1},{16,17},{1,2},{17,18},{2,3},{18,19},{3,4},{19,20},{4,5},{20,... | collective-permute-start | bytes 2162696 | tf_op jit(solution)/shard_map/ppermute | solution.py:67
  64.0 19.8 %collective-permute-start.21 = (bf16[22,64,256]{2,1,0:T(8,128)(2,1)}, bf16[22,64,256]{2,1,0:T(8,128)(2,1)}, u32[]{:S(2)}, u32[]{:S(2)}) collective-permute-start(bf16[22,64,256]{2,1,0:T(8,128)(2,1)} %collective-permute-done.13.refs_16_.refs_3_), channel_id=1, source_target_pairs={{0,7},{16,23},{1,0},{17,16},{2,1},{18,17},{3,2},{19,18},{4,3},{20,... | collective-permute-start | bytes 2162696 | tf_op jit(solution)/shard_map/ppermute | solution.py:67
  68.4 18.4 %collective-permute-start.17 = (bf16[2,8,128,256]{3,2,1,0:T(8,128)(2,1)}, bf16[2,8,128,256]{3,2,1,0:T(8,128)(2,1)S(1)}, u32[]{:S(2)}, u32[]{:S(2)}) collective-permute-start(bf16[2,8,128,256]{3,2,1,0:T(8,128)(2,1)} %get-tuple-element.32), channel_id=1, source_target_pairs={{0,8},{16,48},{1,9},{17,49},{2,10},{18,50},{3,11},{19,51},{4,12},{... | collective-permute-start | bytes 3145736 | tf_op jit(solution)/shard_map/ppermute | solution.py:67
  70.4 16.7 %collective-permute-start.16 = (bf16[2,8,128,256]{3,2,1,0:T(8,128)(2,1)}, bf16[2,8,128,256]{3,2,1,0:T(8,128)(2,1)}, u32[]{:S(2)}, u32[]{:S(2)}) collective-permute-start(bf16[2,8,128,256]{3,2,1,0:T(8,128)(2,1)} %get-tuple-element.31), channel_id=1, source_target_pairs={{0,136},{16,112},{1,137},{17,113},{2,138},{18,114},{3,139},{19,115... | collective-permute-start | bytes 3145736 | tf_op jit(solution)/shard_map/ppermute | solution.py:67
  83.8 18.9 %collective-permute-start.24 = (bf16[22,64,256]{2,1,0:T(8,128)(2,1)}, bf16[22,64,256]{2,1,0:T(8,128)(2,1)S(1)}, u32[]{:S(2)}, u32[]{:S(2)}) collective-permute-start(bf16[22,64,256]{2,1,0:T(8,128)(2,1)} %collective-permute-done.23.refs_22_.refs_8_), channel_id=1, source_target_pairs={{0,1},{16,17},{1,2},{17,18},{2,3},{18,19},{3,4},{19,20},{4,5},{20,... | collective-permute-start | bytes 2162696 | tf_op jit(solution)/shard_map/ppermute | solution.py:67
  83.8 18.9 %collective-permute-start.22 = (bf16[22,64,256]{2,1,0:T(8,128)(2,1)}, bf16[22,64,256]{2,1,0:T(8,128)(2,1)S(1)}, u32[]{:S(2)}, u32[]{:S(2)}) collective-permute-start(bf16[22,64,256]{2,1,0:T(8,128)(2,1)} %collective-permute-done.21.refs_17_.refs_4_), channel_id=1, source_target_pairs={{0,7},{16,23},{1,0},{17,16},{2,1},{18,17},{3,2},{19,18},{4,3},{20,... | collective-permute-start | bytes 2162696 | tf_op jit(solution)/shard_map/ppermute | solution.py:67
  86.8 21.2 %collective-permute-start.15 = (bf16[2,8,128,256]{3,2,1,0:T(8,128)(2,1)}, bf16[2,8,128,256]{3,2,1,0:T(8,128)(2,1)}, u32[]{:S(2)}, u32[]{:S(2)}) collective-permute-start(bf16[2,8,128,256]{3,2,1,0:T(8,128)(2,1)} %get-tuple-element.32), channel_id=1, source_target_pairs={{0,136},{16,112},{1,137},{17,113},{2,138},{18,114},{3,139},{19,115... | collective-permute-start | bytes 3145736 | tf_op jit(solution)/shard_map/ppermute | solution.py:67
  87.1 21.0 %collective-permute-start.20 = (bf16[2,8,128,256]{3,2,1,0:T(8,128)(2,1)}, bf16[2,8,128,256]{3,2,1,0:T(8,128)(2,1)}, u32[]{:S(2)}, u32[]{:S(2)}) collective-permute-start(bf16[2,8,128,256]{3,2,1,0:T(8,128)(2,1)} %get-tuple-element.31), channel_id=1, source_target_pairs={{0,8},{16,48},{1,9},{17,49},{2,10},{18,50},{3,11},{19,51},{4,12},{... | collective-permute-start | bytes 3145736 | tf_op jit(solution)/shard_map/ppermute | solution.py:67
  102.7 16.1 %collective-permute-start.18 = (bf16[2,8,128,256]{3,2,1,0:T(8,128)(2,1)S(1)}, bf16[2,8,128,256]{3,2,1,0:T(8,128)(2,1)}, u32[]{:S(2)}, u32[]{:S(2)}) collective-permute-start(bf16[2,8,128,256]{3,2,1,0:T(8,128)(2,1)S(1)} %collective-permute-done.17), channel_id=1, source_target_pairs={{0,8},{16,48},{1,9},{17,49},{2,10},{18,50},{3,11},{19,51},{4,12},{... | collective-permute-start | bytes 3145736 | tf_op jit(solution)/shard_map/ppermute | solution.py:67
  102.7 16.1 %collective-permute-start.19 = (bf16[2,8,128,256]{3,2,1,0:T(8,128)(2,1)}, bf16[2,8,128,256]{3,2,1,0:T(8,128)(2,1)}, u32[]{:S(2)}, u32[]{:S(2)}) collective-permute-start(bf16[2,8,128,256]{3,2,1,0:T(8,128)(2,1)} %collective-permute-done.16), channel_id=1, source_target_pairs={{0,136},{16,112},{1,137},{17,113},{2,138},{18,114},{3,139},{19,115... | collective-permute-start | bytes 3145736 | tf_op jit(solution)/shard_map/ppermute | solution.py:67
  108.0 9.7 %collective-permute-start.25 = (bf16[11,64,256]{2,1,0:T(8,128)(2,1)S(1)}, bf16[11,64,256]{2,1,0:T(8,128)(2,1)S(1)}, u32[]{:S(2)}, u32[]{:S(2)}) collective-permute-start(bf16[11,64,256]{2,1,0:T(8,128)(2,1)S(1)} %slice.26), channel_id=1, source_target_pairs={{0,1},{16,17},{1,2},{17,18},{2,3},{18,19},{3,4},{19,20},{4,5},{20,... | collective-permute-start | bytes 1081352 | tf_op jit(solution)/shard_map/ppermute | solution.py:67
  108.1 9.6 %collective-permute-start.26 = (bf16[11,64,256]{2,1,0:T(8,128)(2,1)S(1)}, bf16[11,64,256]{2,1,0:T(8,128)(2,1)S(1)}, u32[]{:S(2)}, u32[]{:S(2)}) collective-permute-start(bf16[11,64,256]{2,1,0:T(8,128)(2,1)S(1)} %slice.27), channel_id=1, source_target_pairs={{0,7},{16,23},{1,0},{17,16},{2,1},{18,17},{3,2},{19,18},{4,3},{20,... | collective-permute-start | bytes 1081352 | tf_op jit(solution)/shard_map/ppermute | solution.py:67
  147.5 24.5 %collective-permute-start.28 = (bf16[8,192,256]{2,1,0:T(8,128)(2,1)S(1)}, bf16[8,192,256]{2,1,0:T(8,128)(2,1)S(1)}, u32[]{:S(2)}, u32[]{:S(2)}) collective-permute-start(bf16[8,192,256]{2,1,0:T(8,128)(2,1)S(1)} %dynamic-slice_bitcast_fusion), channel_id=1, source_target_pairs={{0,8},{16,24},{1,9},{17,25},{2,10},{18,26},{3,11},{19,27},{4,12},{... | collective-permute-start | bytes 2359304 | tf_op jit(solution)/shard_map/ppermute | solution.py:67
  154.6 17.5 %all-to-all-start.1 = ((f32[16,16,256]{2,1,0:T(8,128)}), f32[16,16,256]{2,1,0:T(8,128)S(1)}, u32[]{:S(2)}, u32[]{:S(2)}) async-start(f32[16,16,256]{2,1,0:T(8,128)} %bitcast.49), calls=%async_computation.1 | async-start | bytes 524288 | tf_op jit(solution)/shard_map/all_to_all | solution.py:338
  174.3 26.0 %all-to-all-start.2 = ((bf16[8,192,256]{2,1,0:T(8,128)(2,1)}), bf16[8,192,256]{2,1,0:T(8,128)(2,1)S(1)}, u32[]{:S(2)}, u32[]{:S(2)}) async-start(bf16[8,192,256]{2,1,0:T(8,128)(2,1)} %fusion), calls=%async_computation.2 | async-start | bytes 1572864 | tf_op jit(solution)/shard_map/all_to_all | solution.py:341
  201.0 15.4 %all-to-all-start.3 = ((f32[16,16,256]{2,1,0:T(8,128)}), f32[16,16,256]{2,1,0:T(8,128)S(1)}, u32[]{:S(2)}, u32[]{:S(2)}) async-start(f32[16,16,256]{2,1,0:T(8,128)} %broadcast_in_dim.43), calls=%async_computation.3 | async-start | bytes 524288 | tf_op jit(solution)/shard_map/all_to_all | solution.py:346
  (18 other events, 344.2 us)

commit v5 on v4

--- a/solution.py
+++ b/solution.py
@@ -205,7 +205,7 @@
                 pltpu.SemaphoreType.DMA((groups,)),
             ],
         ),
-        compiler_params=pltpu.CompilerParams(vmem_limit_bytes=16 << 20),
+        compiler_params=pltpu.CompilerParams(vmem_limit_bytes=56 << 20),
         cost_estimate=pl.CostEstimate(flops=0, bytes_accessed=12 << 20, transcendentals=0),
         name="pick_tiles",
     )(side.reshape(1).astype(jnp.int32), tiles)
@@ -268,25 +268,29 @@
     full_line = spread_over(full, z_lines())
     half_line = jnp.stack([half] + [send(half, along_s(-d)) for d in (1, 2, 3)])
     half_q = [half_line] + [send(half_line, along_q(-d)) for d in (1, 2, 3)]
+    half_q[1], side = together(half_q[1], 1 - core)
+    picked = pick(by_parity, side)
     half_plane = jnp.concatenate(
         half_q + [rooted_features.reshape(-1, 64, width), far_features.reshape(-1, 64, width)])
-    half_plane, full_line = together(half_plane, full_line)
     half_z = {0: [half_plane]}
     behind, ahead = ring_first(half_plane, along_z)
     half_z[7], half_z[1] = [behind], [ahead]
     full_q = {0: [full_line]}
     q_behind, q_ahead = ring_first(full_line, along_q)
+    q_behind, q_ahead, behind, ahead = together(q_behind, q_ahead, behind, ahead)
     full_q[3], full_q[1], full_q[2] = [q_behind], [q_ahead], ring_last(q_behind, q_ahead, along_q)
     full_plane = stacked([full_q[d] for d in range(4)])
-    full_plane, behind, ahead, side = together(full_plane, behind, ahead, 1 - core)
+    full_plane, picked = together(full_plane, picked)
+    received = send(picked, flip)
     first, second = full_plane[:2], full_plane[2:]
     first_behind, second_ahead = send(first, along_s(1)), send(second, along_s(-1))
     second_behind, first_ahead = send(second, along_s(1)), send(first, along_s(-1))
     full_s = [[first, second], [first_ahead, second_ahead],
               [send(first_behind, along_s(1)), send(second_ahead, along_s(-1))], [first_behind, second_behind]]
-    received = send(pick(by_parity, side), flip)
     for d in (2, 3):
         behind, ahead = send(behind, along_z(1)), send(ahead, along_z(-1))
+        if d == 2:
+            behind, ahead, received = together(behind, ahead, received)
         half_z[NZ - d], half_z[d] = [behind], [ahead]
     half_z[4] = ring_last(behind, ahead, along_z)
     full_found = full_s

time: 219 us -> 211 us (0.963)
  local copies, waits for them, and re-layouts: 10.5 us -> 5.62 us
    unnamed x35, local copies, waits for them, and re-layouts: 6.16 us -> 1.53 us
    pallas_call x1, Pallas kernels: 3.26 us -> 5.55 us  [pick(): pl.pallas_call(pick_kernel, out_shape=jax.ShapeDtypeStruct((groups, slots...]
  transfers between devices with their start and end apart: 37 -> 37, of which waited for: 20 -> 22; matrix products, arithmetic and copies ran while one was open for 4% -> 3% of each run, Pallas kernels for 3% -> 5%
where the time goes in v5:
time: 211 us; the launch traced here: 210 us
  waiting for transfers between devices  96.6 us (46%)
  starting transfers between devices  65.5 us (31%)
  Pallas kernels  31.8 us (15%)
  other arithmetic  8.87 us (4%)
  local copies, waits for them, and re-layouts  5.62 us (3%)
    ppermute x33, waiting for transfers between devices, send(): return lax.ppermute(value, BOTH, moves)  66.2 us
    ppermute x33, starting transfers between devices, send(): return lax.ppermute(value, BOTH, moves)  40.9 us
    pallas_call x1, Pallas kernels, products(): pl.pallas_call(lambda *refs: products_kernel(places, *refs), out_shape=(j...  20.3 us
    all_to_all x1, waiting for transfers between devices, body(): lax.all_to_all(local_weight, 'rep', 0, 0, tiled=True).reshape(16, 16, width)  10.6 us
    all_to_all x1, waiting for transfers between devices, body(): weight_grad = lax.all_to_all(spread, 'rep', 0, 0, tiled=True)  9.6 us
    all_to_all x1, starting transfers between devices, spread_over(): lax.all_to_all(copies, BOTH, 0, 0, axis_index_groups=places, tiled=True)  8.58 us
    all_to_all x1, starting transfers between devices, body(): lax.all_to_all(local_weight, 'rep', 0, 0, tiled=True).reshape(16, 16, width)  6.18 us
    all_to_all x1, waiting for transfers between devices, body(): lax.all_to_all(line, BOTH, 0, 0, axis_index_groups=z_lines(), tiled=True)  6 us
  transfers between devices with their start and end apart: 37, of which 22 were waited for; matrix products, arithmetic and copies ran while one was open for 3% of the time, Pallas kernels for 5%

profile of v5, /device:TPU:32, one launch (start us, length us, event | category | flops | bytes accessed | tf_op | source)
XLA Modules:
  0.0 210.3 jit_solution(2211266410503801435)
XLA Ops:
  2.5 3.1 %collective-permute-start.4 = (bf16[64,256]{1,0:T(8,128)(2,1)S(1)}, bf16[64,256]{1,0:T(8,128)(2,1)S(1)}, u32[]{:S(2)}, u32[]{:S(2)}) collective-permute-start(bf16[64,256]{1,0:T(8,128)(2,1)S(1)} %get-tuple-element.37), channel_id=1, source_target_pairs={{0,128},{16,80},{1,129},{17,81},{2,130},{18,82},{3,131},{19,83},{4... | collective-permute-start | bytes 98312 | tf_op jit(solution)/shard_map/ppermute | solution.py:67
  6.2 2.6 %collective-permute-start.3 = (bf16[64,256]{1,0:T(8,128)(2,1)S(1)}, bf16[64,256]{1,0:T(8,128)(2,1)S(1)}, u32[]{:S(2)}, u32[]{:S(2)}) collective-permute-start(bf16[64,256]{1,0:T(8,128)(2,1)S(1)} %get-tuple-element.37), channel_id=1, source_target_pairs={{0,136},{16,112},{1,137},{17,113},{2,138},{18,114},{3,139},{19,115... | collective-permute-start | bytes 98312 | tf_op jit(solution)/shard_map/ppermute | solution.py:67
  9.7 8.6 %all-to-all-start = ((bf16[8,128,256]{2,1,0:T(8,128)(2,1)}), bf16[8,128,256]{2,1,0:T(8,128)(2,1)S(1)}, u32[]{:S(2)}, u32[]{:S(2)}) async-start(bf16[8,128,256]{2,1,0:T(8,128)(2,1)} %broadcast_in_dim.42), calls=%async_computation | async-start | bytes 1048576 | tf_op jit(solution)/shard_map/all_to_all | solution.py:43
  18.3 3.1 %collective-permute-start.6 = (bf16[4,64,256]{2,1,0:T(8,128)(2,1)S(1)}, bf16[4,64,256]{2,1,0:T(8,128)(2,1)S(1)}, u32[]{:S(2)}, u32[]{:S(2)}) collective-permute-start(bf16[4,64,256]{2,1,0:T(8,128)(2,1)S(1)} %pad_maximum_fusion.1), channel_id=1, source_target_pairs={{0,96},{16,152},{1,97},{17,153},{2,98},{18,154},{3,99},{19,155},{4... | collective-permute-start | bytes 393224 | tf_op jit(solution)/shard_map/ppermute | solution.py:67
  23.0 2.3 %collective-permute-done.6 = bf16[4,64,256]{2,1,0:T(8,128)(2,1)S(1)} collective-permute-done((bf16[4,64,256]{2,1,0:T(8,128)(2,1)S(1)}, bf16[4,64,256]{2,1,0:T(8,128)(2,1)S(1)}, u32[]{:S(2)}, u32[]{:S(2)}) %collective-permute-start.6) | collective-permute-done | bytes 131104 | tf_op jit(solution)/shard_map/ppermute | solution.py:67
  25.3 2.6 %collective-permute-done.7 = bf16[4,64,256]{2,1,0:T(8,128)(2,1)S(1)} collective-permute-done((bf16[4,64,256]{2,1,0:T(8,128)(2,1)S(1)}, bf16[4,64,256]{2,1,0:T(8,128)(2,1)S(1)}, u32[]{:S(2)}, u32[]{:S(2)}) %collective-permute-start.7) | collective-permute-done | bytes 131104 | tf_op jit(solution)/shard_map/ppermute | solution.py:67
  31.4 4.2 %all-to-all-done = bf16[8,128,256]{2,1,0:T(8,128)(2,1)S(1)} async-done(((bf16[8,128,256]{2,1,0:T(8,128)(2,1)}), bf16[8,128,256]{2,1,0:T(8,128)(2,1)S(1)}, u32[]{:S(2)}, u32[]{:S(2)}) %all-to-all-start) | async-done | bytes 524320 | tf_op jit(solution)/shard_map/all_to_all | solution.py:43
  35.6 3.2 %collective-permute-start.2 = (bf16[8,128,256]{2,1,0:T(8,128)(2,1)S(1)}, bf16[8,128,256]{2,1,0:T(8,128)(2,1)S(1)}, u32[]{:S(2)}, u32[]{:S(2)}) collective-permute-start(bf16[8,128,256]{2,1,0:T(8,128)(2,1)S(1)} %all-to-all-done), channel_id=1, source_target_pairs={{0,96},{16,152},{1,97},{17,153},{2,98},{18,154},{3,99},{19,155},{4... | collective-permute-start | bytes 1572872 | tf_op jit(solution)/shard_map/ppermute | solution.py:67
  38.9 7.8 %collective-permute-done.10.refs_23_.refs_9_ = bf16[22,64,256]{2,1,0:T(8,128)(2,1)S(1)} collective-permute-done((bf16[22,64,256]{2,1,0:T(8,128)(2,1)S(1)}, bf16[22,64,256]{2,1,0:T(8,128)(2,1)S(1)}, u32[]{:S(2)}, u32[]{:S(2)}) %collective-permute-start.10) | collective-permute-done | bytes 720928 | tf_op jit(solution)/shard_map/ppermute | solution.py:67
  48.1 3.3 %collective-permute-start.15 = (bf16[4,128,256]{2,1,0:T(8,128)(2,1)S(1)}, bf16[4,128,256]{2,1,0:T(8,128)(2,1)S(1)}, u32[]{:S(2)}, u32[]{:S(2)}) collective-permute-start(bf16[4,128,256]{2,1,0:T(8,128)(2,1)S(1)} %slice.19), channel_id=1, source_target_pairs={{0,96},{16,152},{1,97},{17,153},{2,98},{18,154},{3,99},{19,155},{4... | collective-permute-start | bytes 786440 | tf_op jit(solution)/shard_map/ppermute | solution.py:67
  51.4 5.6 %pick_tiles.1 = bf16[8,24,128,128]{3,2,1,0:T(8,128)(2,1)} custom-call(s32[1]{0:T(128)} %bitcast.18.side, bf16[8,2,24,128,128]{4,3,2,1,0:T(8,128)(2,1)} %bitcast.41), custom_call_target="tpu_custom_call" | custom-call | bytes 12582912 | tf_op jit(solution)/shard_map/pick_tiles/pallas_call | solution.py:194
  60.9 3.1 %collective-permute-start.18 = (bf16[2,8,128,256]{3,2,1,0:T(8,128)(2,1)S(1)}, bf16[2,8,128,256]{3,2,1,0:T(8,128)(2,1)}, u32[]{:S(2)}, u32[]{:S(2)}) collective-permute-start(bf16[2,8,128,256]{3,2,1,0:T(8,128)(2,1)S(1)} %get-tuple-element.41), channel_id=1, source_target_pairs={{0,136},{16,112},{1,137},{17,113},{2,138},{18,114},{3,139},{19,115... | collective-permute-start | bytes 3145736 | tf_op jit(solution)/shard_map/ppermute | solution.py:67
  64.0 12.1 %collective-permute-done.12.refs_22_.refs_8_ = bf16[22,64,256]{2,1,0:T(8,128)(2,1)} collective-permute-done((bf16[22,64,256]{2,1,0:T(8,128)(2,1)S(1)}, bf16[22,64,256]{2,1,0:T(8,128)(2,1)}, u32[]{:S(2)}, u32[]{:S(2)}) %collective-permute-start.12) | collective-permute-done | bytes 720928 | tf_op jit(solution)/shard_map/ppermute | solution.py:67
  83.8 12.1 %collective-permute-done.24.refs_21_.refs_7_ = bf16[22,64,256]{2,1,0:T(8,128)(2,1)S(1)} collective-permute-done((bf16[22,64,256]{2,1,0:T(8,128)(2,1)}, bf16[22,64,256]{2,1,0:T(8,128)(2,1)S(1)}, u32[]{:S(2)}, u32[]{:S(2)}) %collective-permute-start.24) | collective-permute-done | bytes 720928 | tf_op jit(solution)/shard_map/ppermute | solution.py:67
  103.7 5.8 %collective-permute-done.20 = bf16[2,8,128,256]{3,2,1,0:T(8,128)(2,1)} collective-permute-done((bf16[2,8,128,256]{3,2,1,0:T(8,128)(2,1)}, bf16[2,8,128,256]{3,2,1,0:T(8,128)(2,1)}, u32[]{:S(2)}, u32[]{:S(2)}) %collective-permute-start.20) | collective-permute-done | bytes 1048608 | tf_op jit(solution)/shard_map/ppermute | solution.py:67
  112.6 20.3 %tile_products.1 = (f32[24,128,256]{2,1,0:T(8,128)}, bf16[24,128,256]{2,1,0:T(8,128)(2,1)}) custom-call(s32[16]{0:T(128)} %min.8.refs_0_, s32[384]{0:T(512)} %fusion.9.refs_1_, s32[384]{0:T(512)} %get-tuple-element.38.refs_2_, s32[384]{0:T(512)} %get-tuple-element.47.refs_3_, s32[3]{0:T(128)} %pad_add_fusion.1.refs_4_.refs_0_, ...), custom_call_target="tpu_custom_call" | custom-call | flops 3221225472 | bytes 31457280 | tf_op jit(solution)/shard_map/tile_products/pallas_call | solution.py:217
  133.4 3.2 %collective-permute-done.27 = bf16[24,128,256]{2,1,0:T(8,128)(2,1)S(1)} collective-permute-done((bf16[24,128,256]{2,1,0:T(8,128)(2,1)}, bf16[24,128,256]{2,1,0:T(8,128)(2,1)S(1)}, u32[]{:S(2)}, u32[]{:S(2)}) %collective-permute-start.27) | collective-permute-done | bytes 1572896 | tf_op jit(solution)/shard_map/ppermute | solution.py:67
  136.7 2.4 %add_convert_fusion = bf16[24,128,256]{2,1,0:T(8,128)(2,1)S(1)} fusion(f32[24,128,256]{2,1,0:T(8,128)} %get-tuple-element.30, bf16[24,128,256]{2,1,0:T(8,128)(2,1)S(1)} %collective-permute-done.27), kind=kLoop, calls=%fused_computation | loop fusion | flops 2359296 | bytes 6291456 | tf_op jit(solution)/shard_map/convert_element_type | solution.py:338
  139.1 2.9 %collective-permute-start.28 = (bf16[8,192,256]{2,1,0:T(8,128)(2,1)S(1)}, bf16[8,192,256]{2,1,0:T(8,128)(2,1)S(1)}, u32[]{:S(2)}, u32[]{:S(2)}) collective-permute-start(bf16[8,192,256]{2,1,0:T(8,128)(2,1)S(1)} %dynamic-slice_bitcast_fusion), channel_id=1, source_target_pairs={{0,8},{16,24},{1,9},{17,25},{2,10},{18,26},{3,11},{19,27},{4,12},{... | collective-permute-start | bytes 2359304 | tf_op jit(solution)/shard_map/ppermute | solution.py:67
  142.0 6.0 %features_product.1 = f32[256,256]{1,0:T(8,128)} custom-call(s32[3]{0:T(128)} %pad_add_fusion.1.refs_4_.refs_0_, bf16[2,8,192,256]{3,2,1,0:T(8,128)(2,1)} %bitcast.44, bf16[22,64,256]{2,1,0:T(8,128)(2,1)} %copy-done.5, bf16[22,64,256]{2,1,0:T(8,128)(2,1)} %copy-done.7, bf16[22,64,256]{2,1,0:T(8,128)(2,1)} %copy-done.8, bf16[22,64,256]{2,1,0:T(8,128)(2,1)} %copy-done.3, ...), custom_call_target="tpu_custom_call" | custom-call | flops 402653184 | bytes 4194304 | tf_op jit(solution)/shard_map/features_product/pallas_call | solution.py:162
  148.0 6.2 %all-to-all-start.1 = ((f32[16,16,256]{2,1,0:T(8,128)}), f32[16,16,256]{2,1,0:T(8,128)S(1)}, u32[]{:S(2)}, u32[]{:S(2)}) async-start(f32[16,16,256]{2,1,0:T(8,128)} %bitcast.50), calls=%async_computation.1 | async-start | bytes 524288 | tf_op jit(solution)/shard_map/all_to_all | solution.py:342
  154.2 10.6 %all-to-all-done.1 = f32[16,16,256]{2,1,0:T(8,128)S(1)} async-done(((f32[16,16,256]{2,1,0:T(8,128)}), f32[16,16,256]{2,1,0:T(8,128)S(1)}, u32[]{:S(2)}, u32[]{:S(2)}) %all-to-all-start.1) | async-done | bytes 262176 | tf_op jit(solution)/shard_map/all_to_all | solution.py:342
  164.8 2.2 %fusion = bf16[8,192,256]{2,1,0:T(8,128)(2,1)} fusion(bf16[8,192,256]{2,1,0:T(8,128)(2,1)S(1)} %collective-permute-done.28, bf16[2,8,192,256]{3,2,1,0:T(8,128)(2,1)} %bitcast.45, s32[]{:T(128)S(6)} %select_n.208), kind=kLoop, calls=%fused_computation.3 | loop fusion | flops 1572864 | bytes 2359300 | tf_op jit(solution)/shard_map/convert_element_type | solution.py:343
  167.0 5.1 %all-to-all-start.2 = ((bf16[8,192,256]{2,1,0:T(8,128)(2,1)}), bf16[8,192,256]{2,1,0:T(8,128)(2,1)S(1)}, u32[]{:S(2)}, u32[]{:S(2)}) async-start(bf16[8,192,256]{2,1,0:T(8,128)(2,1)} %fusion), calls=%async_computation.2 | async-start | bytes 1572864 | tf_op jit(solution)/shard_map/all_to_all | solution.py:345
  173.2 2.3 %collective-permute-start.30 = (f32[16,256]{1,0:T(8,128)S(1)}, f32[16,256]{1,0:T(8,128)S(1)}, u32[]{:S(2)}, u32[]{:S(2)}) collective-permute-start(f32[16,256]{1,0:T(8,128)S(1)} %add.256), channel_id=1, source_target_pairs={{0,128},{16,144},{1,129},{17,145},{2,130},{18,146},{3,131},{19,147... | collective-permute-start | bytes 49160 | tf_op jit(solution)/shard_map/ppermute | solution.py:67
  175.5 3.0 %collective-permute-done.30 = f32[16,256]{1,0:T(8,128)S(1)} collective-permute-done((f32[16,256]{1,0:T(8,128)S(1)}, f32[16,256]{1,0:T(8,128)S(1)}, u32[]{:S(2)}, u32[]{:S(2)}) %collective-permute-start.30) | collective-permute-done | bytes 16416 | tf_op jit(solution)/shard_map/ppermute | solution.py:67
  178.5 3.7 %collective-permute-done.31 = f32[16,256]{1,0:T(8,128)S(1)} collective-permute-done((f32[16,256]{1,0:T(8,128)S(1)}, f32[16,256]{1,0:T(8,128)S(1)}, u32[]{:S(2)}, u32[]{:S(2)}) %collective-permute-start.31) | collective-permute-done | bytes 16416 | tf_op jit(solution)/shard_map/ppermute | solution.py:67
  182.2 2.5 %collective-permute-start.32 = (f32[16,256]{1,0:T(8,128)S(1)}, f32[16,256]{1,0:T(8,128)S(1)}, u32[]{:S(2)}, u32[]{:S(2)}) collective-permute-start(f32[16,256]{1,0:T(8,128)S(1)} %add.258), channel_id=1, source_target_pairs={{0,64},{16,80},{1,65},{17,81},{2,66},{18,82},{3,67},{19,83},{4,68}... | collective-permute-start | bytes 49160 | tf_op jit(solution)/shard_map/ppermute | solution.py:67
  184.7 2.8 %collective-permute-done.32 = f32[16,256]{1,0:T(8,128)S(1)} collective-permute-done((f32[16,256]{1,0:T(8,128)S(1)}, f32[16,256]{1,0:T(8,128)S(1)}, u32[]{:S(2)}, u32[]{:S(2)}) %collective-permute-start.32) | collective-permute-done | bytes 16416 | tf_op jit(solution)/shard_map/ppermute | solution.py:67
  187.5 6.0 %all-to-all-done.2 = bf16[8,192,256]{2,1,0:T(8,128)(2,1)S(1)} async-done(((bf16[8,192,256]{2,1,0:T(8,128)(2,1)}), bf16[8,192,256]{2,1,0:T(8,128)(2,1)S(1)}, u32[]{:S(2)}, u32[]{:S(2)}) %all-to-all-start.2) | async-done | bytes 786464 | tf_op jit(solution)/shard_map/all_to_all | solution.py:345
  194.2 4.8 %all-to-all-start.3 = ((f32[16,16,256]{2,1,0:T(8,128)}), f32[16,16,256]{2,1,0:T(8,128)S(1)}, u32[]{:S(2)}, u32[]{:S(2)}) async-start(f32[16,16,256]{2,1,0:T(8,128)} %broadcast_in_dim.43), calls=%async_computation.3 | async-start | bytes 524288 | tf_op jit(solution)/shard_map/all_to_all | solution.py:350
  200.0 9.6 %all-to-all-done.3 = f32[16,16,256]{2,1,0:T(8,128)S(1)} async-done(((f32[16,16,256]{2,1,0:T(8,128)}), f32[16,16,256]{2,1,0:T(8,128)S(1)}, u32[]{:S(2)}, u32[]{:S(2)}) %all-to-all-start.3) | async-done | bytes 262176 | tf_op jit(solution)/shard_map/all_to_all | solution.py:350
  (122 shorter events, 36.3 us)
Async XLA Ops:
  2.5 15.8 %collective-permute-start.4 = (bf16[64,256]{1,0:T(8,128)(2,1)S(1)}, bf16[64,256]{1,0:T(8,128)(2,1)S(1)}, u32[]{:S(2)}, u32[]{:S(2)}) collective-permute-start(bf16[64,256]{1,0:T(8,128)(2,1)S(1)} %get-tuple-element.37), channel_id=1, source_target_pairs={{0,128},{16,80},{1,129},{17,81},{2,130},{18,82},{3,131},{19,83},{4... | collective-permute-start | bytes 98312 | tf_op jit(solution)/shard_map/ppermute | solution.py:67
  5.6 12.7 %collective-permute-start.5 = (bf16[64,256]{1,0:T(8,128)(2,1)S(1)}, bf16[64,256]{1,0:T(8,128)(2,1)S(1)}, u32[]{:S(2)}, u32[]{:S(2)}) collective-permute-start(bf16[64,256]{1,0:T(8,128)(2,1)S(1)} %get-tuple-element.37), channel_id=1, source_target_pairs={{0,8},{16,48},{1,9},{17,49},{2,10},{18,50},{3,11},{19,51},{4,12},{... | collective-permute-start | bytes 98312 | tf_op jit(solution)/shard_map/ppermute | solution.py:67
  6.2 12.1 %collective-permute-start.3 = (bf16[64,256]{1,0:T(8,128)(2,1)S(1)}, bf16[64,256]{1,0:T(8,128)(2,1)S(1)}, u32[]{:S(2)}, u32[]{:S(2)}) collective-permute-start(bf16[64,256]{1,0:T(8,128)(2,1)S(1)} %get-tuple-element.37), channel_id=1, source_target_pairs={{0,136},{16,112},{1,137},{17,113},{2,138},{18,114},{3,139},{19,115... | collective-permute-start | bytes 98312 | tf_op jit(solution)/shard_map/ppermute | solution.py:67
  8.8 20.5 %collective-permute-start.9 = (bf16[192,256]{1,0:T(8,128)(2,1)S(1)}, bf16[192,256]{1,0:T(8,128)(2,1)S(1)}, u32[]{:S(2)}, u32[]{:S(2)}) collective-permute-start(bf16[192,256]{1,0:T(8,128)(2,1)S(1)} %get-tuple-element.48), channel_id=1, source_target_pairs={{0,8},{16,24},{1,9},{17,25},{2,10},{18,26},{3,11},{19,27},{4,12},{... | collective-permute-start | bytes 294920 | tf_op jit(solution)/shard_map/ppermute | solution.py:67
  9.7 25.9 %all-to-all-start = ((bf16[8,128,256]{2,1,0:T(8,128)(2,1)}), bf16[8,128,256]{2,1,0:T(8,128)(2,1)S(1)}, u32[]{:S(2)}, u32[]{:S(2)}) async-start(bf16[8,128,256]{2,1,0:T(8,128)(2,1)} %broadcast_in_dim.42), calls=%async_computation | async-start | bytes 1048576 | tf_op jit(solution)/shard_map/all_to_all | solution.py:43
  18.3 7.0 %collective-permute-start.6 = (bf16[4,64,256]{2,1,0:T(8,128)(2,1)S(1)}, bf16[4,64,256]{2,1,0:T(8,128)(2,1)S(1)}, u32[]{:S(2)}, u32[]{:S(2)}) collective-permute-start(bf16[4,64,256]{2,1,0:T(8,128)(2,1)S(1)} %pad_maximum_fusion.1), channel_id=1, source_target_pairs={{0,96},{16,152},{1,97},{17,153},{2,98},{18,154},{3,99},{19,155},{4... | collective-permute-start | bytes 393224 | tf_op jit(solution)/shard_map/ppermute | solution.py:67
  21.4 6.6 %collective-permute-start.7 = (bf16[4,64,256]{2,1,0:T(8,128)(2,1)S(1)}, bf16[4,64,256]{2,1,0:T(8,128)(2,1)S(1)}, u32[]{:S(2)}, u32[]{:S(2)}) collective-permute-start(bf16[4,64,256]{2,1,0:T(8,128)(2,1)S(1)} %pad_maximum_fusion.1), channel_id=1, source_target_pairs={{0,64},{16,144},{1,65},{17,145},{2,66},{18,146},{3,67},{19,147},{4... | collective-permute-start | bytes 393224 | tf_op jit(solution)/shard_map/ppermute | solution.py:67
  22.0 7.2 %collective-permute-start.8 = (bf16[4,64,256]{2,1,0:T(8,128)(2,1)S(1)}, bf16[4,64,256]{2,1,0:T(8,128)(2,1)S(1)}, u32[]{:S(2)}, u32[]{:S(2)}) collective-permute-start(bf16[4,64,256]{2,1,0:T(8,128)(2,1)S(1)} %pad_maximum_fusion.1), channel_id=1, source_target_pairs={{0,32},{16,24},{1,33},{17,25},{2,34},{18,26},{3,35},{19,27},{4,36}... | collective-permute-start | bytes 393224 | tf_op jit(solution)/shard_map/ppermute | solution.py:67
  29.3 17.3 %collective-permute-start.10 = (bf16[22,64,256]{2,1,0:T(8,128)(2,1)S(1)}, bf16[22,64,256]{2,1,0:T(8,128)(2,1)S(1)}, u32[]{:S(2)}, u32[]{:S(2)}) collective-permute-start(bf16[22,64,256]{2,1,0:T(8,128)(2,1)S(1)} %constant_dynamic-update-slice_fusion.refs_15_.refs_2_), channel_id=1, source_target_pairs={{0,1},{16,17},{1,2},{17,18},{2,3},{18,19},{3,4},{19,20},{4,5},{20,... | collective-permute-start | bytes 2162696 | tf_op jit(solution)/shard_map/ppermute | solution.py:67
  30.9 17.1 %collective-permute-start.11 = (bf16[22,64,256]{2,1,0:T(8,128)(2,1)S(1)}, bf16[22,64,256]{2,1,0:T(8,128)(2,1)S(1)}, u32[]{:S(2)}, u32[]{:S(2)}) collective-permute-start(bf16[22,64,256]{2,1,0:T(8,128)(2,1)S(1)} %constant_dynamic-update-slice_fusion.refs_15_.refs_2_), channel_id=1, source_target_pairs={{0,7},{16,23},{1,0},{17,16},{2,1},{18,17},{3,2},{19,18},{4,3},{20,... | collective-permute-start | bytes 2162696 | tf_op jit(solution)/shard_map/ppermute | solution.py:67
  35.6 12.3 %collective-permute-start.1 = (bf16[8,128,256]{2,1,0:T(8,128)(2,1)S(1)}, bf16[8,128,256]{2,1,0:T(8,128)(2,1)S(1)}, u32[]{:S(2)}, u32[]{:S(2)}) collective-permute-start(bf16[8,128,256]{2,1,0:T(8,128)(2,1)S(1)} %all-to-all-done), channel_id=1, source_target_pairs={{0,32},{16,24},{1,33},{17,25},{2,34},{18,26},{3,35},{19,27},{4,36}... | collective-permute-start | bytes 1572872 | tf_op jit(solution)/shard_map/ppermute | solution.py:67
  35.6 12.3 %collective-permute-start.2 = (bf16[8,128,256]{2,1,0:T(8,128)(2,1)S(1)}, bf16[8,128,256]{2,1,0:T(8,128)(2,1)S(1)}, u32[]{:S(2)}, u32[]{:S(2)}) collective-permute-start(bf16[8,128,256]{2,1,0:T(8,128)(2,1)S(1)} %all-to-all-done), channel_id=1, source_target_pairs={{0,96},{16,152},{1,97},{17,153},{2,98},{18,154},{3,99},{19,155},{4... | collective-permute-start | bytes 1572872 | tf_op jit(solution)/shard_map/ppermute | solution.py:67
  48.0 9.0 %collective-permute-start.14 = (bf16[4,128,256]{2,1,0:T(8,128)(2,1)S(1)}, bf16[4,128,256]{2,1,0:T(8,128)(2,1)S(1)}, u32[]{:S(2)}, u32[]{:S(2)}) collective-permute-start(bf16[4,128,256]{2,1,0:T(8,128)(2,1)S(1)} %slice.18), channel_id=1, source_target_pairs={{0,32},{16,24},{1,33},{17,25},{2,34},{18,26},{3,35},{19,27},{4,36}... | collective-permute-start | bytes 786440 | tf_op jit(solution)/shard_map/ppermute | solution.py:67
  48.1 8.9 %collective-permute-start.15 = (bf16[4,128,256]{2,1,0:T(8,128)(2,1)S(1)}, bf16[4,128,256]{2,1,0:T(8,128)(2,1)S(1)}, u32[]{:S(2)}, u32[]{:S(2)}) collective-permute-start(bf16[4,128,256]{2,1,0:T(8,128)(2,1)S(1)} %slice.19), channel_id=1, source_target_pairs={{0,96},{16,152},{1,97},{17,153},{2,98},{18,154},{3,99},{19,155},{4... | collective-permute-start | bytes 786440 | tf_op jit(solution)/shard_map/ppermute | solution.py:67
  57.4 20.7 %collective-permute-start.16 = (bf16[8,24,128,128]{3,2,1,0:T(8,128)(2,1)}, bf16[8,24,128,128]{3,2,1,0:T(8,128)(2,1)}, u32[]{:S(2)}, u32[]{:S(2)}) collective-permute-start(bf16[8,24,128,128]{3,2,1,0:T(8,128)(2,1)} %pick_tiles.1), channel_id=1, source_target_pairs={{0,16},{16,0},{1,17},{17,1},{2,18},{18,2},{3,19},{19,3},{4,20},{20... | collective-permute-start | bytes 18874376 | tf_op jit(solution)/shard_map/ppermute | solution.py:67
  57.5 18.7 %collective-permute-start.12 = (bf16[22,64,256]{2,1,0:T(8,128)(2,1)S(1)}, bf16[22,64,256]{2,1,0:T(8,128)(2,1)}, u32[]{:S(2)}, u32[]{:S(2)}) collective-permute-start(bf16[22,64,256]{2,1,0:T(8,128)(2,1)S(1)} %collective-permute-done.10.refs_23_.refs_9_), channel_id=1, source_target_pairs={{0,1},{16,17},{1,2},{17,18},{2,3},{18,19},{3,4},{19,20},{4,5},{20,... | collective-permute-start | bytes 2162696 | tf_op jit(solution)/shard_map/ppermute | solution.py:67
  59.5 18.5 %collective-permute-start.13 = (bf16[22,64,256]{2,1,0:T(8,128)(2,1)S(1)}, bf16[22,64,256]{2,1,0:T(8,128)(2,1)S(1)}, u32[]{:S(2)}, u32[]{:S(2)}) collective-permute-start(bf16[22,64,256]{2,1,0:T(8,128)(2,1)S(1)} %collective-permute-done.11.refs_16_.refs_3_), channel_id=1, source_target_pairs={{0,7},{16,23},{1,0},{17,16},{2,1},{18,17},{3,2},{19,18},{4,3},{20,... | collective-permute-start | bytes 2162696 | tf_op jit(solution)/shard_map/ppermute | solution.py:67
  60.8 21.3 %collective-permute-start.19 = (bf16[2,8,128,256]{3,2,1,0:T(8,128)(2,1)}, bf16[2,8,128,256]{3,2,1,0:T(8,128)(2,1)}, u32[]{:S(2)}, u32[]{:S(2)}) collective-permute-start(bf16[2,8,128,256]{3,2,1,0:T(8,128)(2,1)} %get-tuple-element.42), channel_id=1, source_target_pairs={{0,8},{16,48},{1,9},{17,49},{2,10},{18,50},{3,11},{19,51},{4,12},{... | collective-permute-start | bytes 3145736 | tf_op jit(solution)/shard_map/ppermute | solution.py:67
  60.9 22.5 %collective-permute-start.18 = (bf16[2,8,128,256]{3,2,1,0:T(8,128)(2,1)S(1)}, bf16[2,8,128,256]{3,2,1,0:T(8,128)(2,1)}, u32[]{:S(2)}, u32[]{:S(2)}) collective-permute-start(bf16[2,8,128,256]{3,2,1,0:T(8,128)(2,1)S(1)} %get-tuple-element.41), channel_id=1, source_target_pairs={{0,136},{16,112},{1,137},{17,113},{2,138},{18,114},{3,139},{19,115... | collective-permute-start | bytes 3145736 | tf_op jit(solution)/shard_map/ppermute | solution.py:67
  78.0 17.9 %collective-permute-start.24 = (bf16[22,64,256]{2,1,0:T(8,128)(2,1)}, bf16[22,64,256]{2,1,0:T(8,128)(2,1)S(1)}, u32[]{:S(2)}, u32[]{:S(2)}) collective-permute-start(bf16[22,64,256]{2,1,0:T(8,128)(2,1)} %collective-permute-done.12.refs_22_.refs_8_), channel_id=1, source_target_pairs={{0,1},{16,17},{1,2},{17,18},{2,3},{18,19},{3,4},{19,20},{4,5},{20,... | collective-permute-start | bytes 2162696 | tf_op jit(solution)/shard_map/ppermute | solution.py:67
  79.8 22.3 %collective-permute-start.17 = (bf16[2,8,128,256]{3,2,1,0:T(8,128)(2,1)}, bf16[2,8,128,256]{3,2,1,0:T(8,128)(2,1)}, u32[]{:S(2)}, u32[]{:S(2)}) collective-permute-start(bf16[2,8,128,256]{3,2,1,0:T(8,128)(2,1)} %get-tuple-element.42), channel_id=1, source_target_pairs={{0,136},{16,112},{1,137},{17,113},{2,138},{18,114},{3,139},{19,115... | collective-permute-start | bytes 3145736 | tf_op jit(solution)/shard_map/ppermute | solution.py:67
  81.6 18.7 %collective-permute-start.23 = (bf16[22,64,256]{2,1,0:T(8,128)(2,1)S(1)}, bf16[22,64,256]{2,1,0:T(8,128)(2,1)S(1)}, u32[]{:S(2)}, u32[]{:S(2)}) collective-permute-start(bf16[22,64,256]{2,1,0:T(8,128)(2,1)S(1)} %collective-permute-done.13.refs_17_.refs_4_), channel_id=1, source_target_pairs={{0,7},{16,23},{1,0},{17,16},{2,1},{18,17},{3,2},{19,18},{4,3},{20,... | collective-permute-start | bytes 2162696 | tf_op jit(solution)/shard_map/ppermute | solution.py:67
  82.1 21.6 %collective-permute-start.22 = (bf16[2,8,128,256]{3,2,1,0:T(8,128)(2,1)S(1)}, bf16[2,8,128,256]{3,2,1,0:T(8,128)(2,1)}, u32[]{:S(2)}, u32[]{:S(2)}) collective-permute-start(bf16[2,8,128,256]{3,2,1,0:T(8,128)(2,1)S(1)} %get-tuple-element.41), channel_id=1, source_target_pairs={{0,8},{16,48},{1,9},{17,49},{2,10},{18,50},{3,11},{19,51},{4,12},{... | collective-permute-start | bytes 3145736 | tf_op jit(solution)/shard_map/ppermute | solution.py:67
  83.4 26.0 %collective-permute-start.20 = (bf16[2,8,128,256]{3,2,1,0:T(8,128)(2,1)}, bf16[2,8,128,256]{3,2,1,0:T(8,128)(2,1)}, u32[]{:S(2)}, u32[]{:S(2)}) collective-permute-start(bf16[2,8,128,256]{3,2,1,0:T(8,128)(2,1)} %collective-permute-done.19), channel_id=1, source_target_pairs={{0,8},{16,48},{1,9},{17,49},{2,10},{18,50},{3,11},{19,51},{4,12},{... | collective-permute-start | bytes 3145736 | tf_op jit(solution)/shard_map/ppermute | solution.py:67
  95.9 15.1 %collective-permute-start.21 = (bf16[2,8,128,256]{3,2,1,0:T(8,128)(2,1)}, bf16[2,8,128,256]{3,2,1,0:T(8,128)(2,1)}, u32[]{:S(2)}, u32[]{:S(2)}) collective-permute-start(bf16[2,8,128,256]{3,2,1,0:T(8,128)(2,1)} %collective-permute-done.18), channel_id=1, source_target_pairs={{0,136},{16,112},{1,137},{17,113},{2,138},{18,114},{3,139},{19,115... | collective-permute-start | bytes 3145736 | tf_op jit(solution)/shard_map/ppermute | solution.py:67
  100.3 10.8 %collective-permute-start.25 = (bf16[11,64,256]{2,1,0:T(8,128)(2,1)S(1)}, bf16[11,64,256]{2,1,0:T(8,128)(2,1)S(1)}, u32[]{:S(2)}, u32[]{:S(2)}) collective-permute-start(bf16[11,64,256]{2,1,0:T(8,128)(2,1)S(1)} %slice.24), channel_id=1, source_target_pairs={{0,1},{16,17},{1,2},{17,18},{2,3},{18,19},{3,4},{19,20},{4,5},{20,... | collective-permute-start | bytes 1081352 | tf_op jit(solution)/shard_map/ppermute | solution.py:67
  102.1 9.8 %collective-permute-start.26 = (bf16[11,64,256]{2,1,0:T(8,128)(2,1)S(1)}, bf16[11,64,256]{2,1,0:T(8,128)(2,1)S(1)}, u32[]{:S(2)}, u32[]{:S(2)}) collective-permute-start(bf16[11,64,256]{2,1,0:T(8,128)(2,1)S(1)} %slice.25), channel_id=1, source_target_pairs={{0,7},{16,23},{1,0},{17,16},{2,1},{18,17},{3,2},{19,18},{4,3},{20,... | collective-permute-start | bytes 1081352 | tf_op jit(solution)/shard_map/ppermute | solution.py:67
  139.1 25.6 %collective-permute-start.28 = (bf16[8,192,256]{2,1,0:T(8,128)(2,1)S(1)}, bf16[8,192,256]{2,1,0:T(8,128)(2,1)S(1)}, u32[]{:S(2)}, u32[]{:S(2)}) collective-permute-start(bf16[8,192,256]{2,1,0:T(8,128)(2,1)S(1)} %dynamic-slice_bitcast_fusion), channel_id=1, source_target_pairs={{0,8},{16,24},{1,9},{17,25},{2,10},{18,26},{3,11},{19,27},{4,12},{... | collective-permute-start | bytes 2359304 | tf_op jit(solution)/shard_map/ppermute | solution.py:67
  148.0 16.7 %all-to-all-start.1 = ((f32[16,16,256]{2,1,0:T(8,128)}), f32[16,16,256]{2,1,0:T(8,128)S(1)}, u32[]{:S(2)}, u32[]{:S(2)}) async-start(f32[16,16,256]{2,1,0:T(8,128)} %bitcast.50), calls=%async_computation.1 | async-start | bytes 524288 | tf_op jit(solution)/shard_map/all_to_all | solution.py:342
  167.0 26.5 %all-to-all-start.2 = ((bf16[8,192,256]{2,1,0:T(8,128)(2,1)}), bf16[8,192,256]{2,1,0:T(8,128)(2,1)S(1)}, u32[]{:S(2)}, u32[]{:S(2)}) async-start(bf16[8,192,256]{2,1,0:T(8,128)(2,1)} %fusion), calls=%async_computation.2 | async-start | bytes 1572864 | tf_op jit(solution)/shard_map/all_to_all | solution.py:345
  173.2 5.2 %collective-permute-start.30 = (f32[16,256]{1,0:T(8,128)S(1)}, f32[16,256]{1,0:T(8,128)S(1)}, u32[]{:S(2)}, u32[]{:S(2)}) collective-permute-start(f32[16,256]{1,0:T(8,128)S(1)} %add.256), channel_id=1, source_target_pairs={{0,128},{16,144},{1,129},{17,145},{2,130},{18,146},{3,131},{19,147... | collective-permute-start | bytes 49160 | tf_op jit(solution)/shard_map/ppermute | solution.py:67
  194.2 15.4 %all-to-all-start.3 = ((f32[16,16,256]{2,1,0:T(8,128)}), f32[16,16,256]{2,1,0:T(8,128)S(1)}, u32[]{:S(2)}, u32[]{:S(2)}) async-start(f32[16,16,256]{2,1,0:T(8,128)} %broadcast_in_dim.43), calls=%async_computation.3 | async-start | bytes 524288 | tf_op jit(solution)/shard_map/all_to_all | solution.py:350
  (18 other events, 426.2 us)

commit v6 on v5

--- a/solution.py
+++ b/solution.py
@@ -102,24 +102,24 @@
             copy.wait()
 
     slots = kept.shape[2]
-    for side, tiles in ((0, kept), (1, received)):
-        base = (side * pl.num_programs(0) + step) * slots
-
-        def batch(i, _):
-            found = []
+    starts = [(side * pl.num_programs(0) + step) * slots for side in range(2)]
+
+    def batch(i, _):
+        found = []
+        for side, base in enumerate(starts):
             for k in range(UNROLL):
                 slot = i * UNROLL + k
                 entry = base + slot
-                tile = tiles[0, 0, slot] if side == 0 else tiles[0, slot]
+                tile = received[0, slot] if side else kept[0, 0, slot]
                 rows = jnp.concatenate([units[unit0[entry]], units[unit1[entry]]], axis=0)
                 found.append((columns[entry], lax.dot_general(
                     tile, rows, (((0,), (0,)), ((), ())), preferred_element_type=jnp.float32)))
-            for column, product in found:
-                totals[column] += product
-            return 0
-
-        live = counts[side * pl.num_programs(0) + step]
-        lax.fori_loop(0, (live + UNROLL - 1) // UNROLL, batch, 0)
+        for column, product in found:
+            totals[column] += product
+        return 0
+
+    live = jnp.maximum(counts[step], counts[pl.num_programs(0) + step])
+    lax.fori_loop(0, (live + UNROLL - 1) // UNROLL, batch, 0)
 
     @pl.when(step == pl.num_programs(0) - 1)
     def _():
@@ -268,32 +268,31 @@
     full_line = spread_over(full, z_lines())
     half_line = jnp.stack([half] + [send(half, along_s(-d)) for d in (1, 2, 3)])
     half_q = [half_line] + [send(half_line, along_q(-d)) for d in (1, 2, 3)]
-    half_q[1], side = together(half_q[1], 1 - core)
-    picked = pick(by_parity, side)
     half_plane = jnp.concatenate(
         half_q + [rooted_features.reshape(-1, 64, width), far_features.reshape(-1, 64, width)])
     half_z = {0: [half_plane]}
     behind, ahead = ring_first(half_plane, along_z)
+    q_behind, q_ahead = ring_first(full_line, along_q)
+    q_behind, q_ahead, behind, ahead, side = together(q_behind, q_ahead, behind, ahead, 1 - core)
+    picked = pick(by_parity, side)
     half_z[7], half_z[1] = [behind], [ahead]
-    full_q = {0: [full_line]}
-    q_behind, q_ahead = ring_first(full_line, along_q)
-    q_behind, q_ahead, behind, ahead = together(q_behind, q_ahead, behind, ahead)
-    full_q[3], full_q[1], full_q[2] = [q_behind], [q_ahead], ring_last(q_behind, q_ahead, along_q)
-    full_plane = stacked([full_q[d] for d in range(4)])
-    full_plane, picked = together(full_plane, picked)
+    first = jnp.stack([full_line, q_ahead])
+    q_opposite = send(q_behind, along_q(1))
+    first_behind, first_ahead = ring_first(first, along_s)
+    behind, ahead = send(behind, along_z(1)), send(ahead, along_z(-1))
+    q_opposite, first_behind, first_ahead, behind, ahead, picked = together(
+        q_opposite, first_behind, first_ahead, behind, ahead, picked)
     received = send(picked, flip)
-    first, second = full_plane[:2], full_plane[2:]
-    first_behind, second_ahead = send(first, along_s(1)), send(second, along_s(-1))
-    second_behind, first_ahead = send(second, along_s(1)), send(first, along_s(-1))
-    full_s = [[first, second], [first_ahead, second_ahead],
-              [send(first_behind, along_s(1)), send(second_ahead, along_s(-1))], [first_behind, second_behind]]
-    for d in (2, 3):
-        behind, ahead = send(behind, along_z(1)), send(ahead, along_z(-1))
-        if d == 2:
-            behind, ahead, received = together(behind, ahead, received)
-        half_z[NZ - d], half_z[d] = [behind], [ahead]
+    half_z[6], half_z[2] = [behind], [ahead]
+    second = jnp.stack([q_opposite, q_behind])
+    second_behind, second_ahead = ring_first(second, along_s)
+    behind, ahead = send(behind, along_z(1)), send(ahead, along_z(-1))
+    second_behind, second_ahead, behind, ahead, received = together(
+        second_behind, second_ahead, behind, ahead, received)
+    half_z[5], half_z[3] = [behind], [ahead]
     half_z[4] = ring_last(behind, ahead, along_z)
-    full_found = full_s
+    full_found = [[first, second], [first_ahead, second_ahead],
+                  [send(first_behind, along_s(1)), send(second_ahead, along_s(-1))], [first_behind, second_behind]]
     half_found = [half_z[d] for d in range(NZ)]
 
     codes = jnp.stack([kept_codes, received_codes])

time: 211 us -> 208 us (0.986)
  starting transfers between devices: 65.5 us -> 60 us
    ppermute x33 -> x32, starting transfers between devices: 40.9 us -> 34.6 us  [send(): return lax.ppermute(value, BOTH, moves)]
    ppermute x33 -> x32, waiting for transfers between devices: 66.2 us -> 68.8 us  [send(): return lax.ppermute(value, BOTH, moves)]
  transfers between devices with their start and end apart: 37 -> 36, of which waited for: 22 -> 21; matrix products, arithmetic and copies ran while one was open for 3% -> 3% of each run, Pallas kernels for 5% -> 6%
where the time goes in v6:
time: 208 us
  waiting for transfers between devices  98.3 us (47%)
  starting transfers between devices  60 us (29%)
  Pallas kernels  32 us (15%)
  other arithmetic  10 us (5%)
  local copies, waits for them, and re-layouts  5.6 us (3%)
    ppermute x32, waiting for transfers between devices, send(): return lax.ppermute(value, BOTH, moves)  68.8 us
    ppermute x32, starting transfers between devices, send(): return lax.ppermute(value, BOTH, moves)  34.6 us
    pallas_call x1, Pallas kernels, products(): pl.pallas_call(lambda *refs: products_kernel(places, *refs), out_shape=(j...  20.5 us
    all_to_all x1, waiting for transfers between devices, body(): lax.all_to_all(local_weight, 'rep', 0, 0, tiled=True).reshape(16, 16, width)  10.1 us
    all_to_all x1, waiting for transfers between devices, body(): weight_grad = lax.all_to_all(spread, 'rep', 0, 0, tiled=True)  9.6 us
    all_to_all x1, starting transfers between devices, spread_over(): lax.all_to_all(copies, BOTH, 0, 0, axis_index_groups=places, tiled=True)  8.58 us
    all_to_all x1, starting transfers between devices, body(): lax.all_to_all(local_weight, 'rep', 0, 0, tiled=True).reshape(16, 16, width)  7.1 us
    pallas_call x1, Pallas kernels, features_product(): pl.pallas_call(lambda *refs: features_kernel(places, *refs), out_shape=ja...  5.95 us
  transfers between devices with their start and end apart: 36, of which 21 were waited for; matrix products, arithmetic and copies ran while one was open for 3% of the time, Pallas kernels for 6%

profile of v6, /device:TPU:32, one launch (start us, length us, event | category | flops | bytes accessed | tf_op | source)
XLA Modules:
  0.0 208.0 jit_solution(10979975133634167134)
XLA Ops:
  2.5 3.1 %collective-permute-start.4 = (bf16[64,256]{1,0:T(8,128)(2,1)S(1)}, bf16[64,256]{1,0:T(8,128)(2,1)S(1)}, u32[]{:S(2)}, u32[]{:S(2)}) collective-permute-start(bf16[64,256]{1,0:T(8,128)(2,1)S(1)} %get-tuple-element.47), channel_id=1, source_target_pairs={{0,128},{16,80},{1,129},{17,81},{2,130},{18,82},{3,131},{19,83},{4... | collective-permute-start | bytes 98312 | tf_op jit(solution)/shard_map/ppermute | solution.py:67
  6.2 2.6 %collective-permute-start.3 = (bf16[64,256]{1,0:T(8,128)(2,1)S(1)}, bf16[64,256]{1,0:T(8,128)(2,1)S(1)}, u32[]{:S(2)}, u32[]{:S(2)}) collective-permute-start(bf16[64,256]{1,0:T(8,128)(2,1)S(1)} %get-tuple-element.47), channel_id=1, source_target_pairs={{0,136},{16,112},{1,137},{17,113},{2,138},{18,114},{3,139},{19,115... | collective-permute-start | bytes 98312 | tf_op jit(solution)/shard_map/ppermute | solution.py:67
  9.7 8.6 %all-to-all-start = ((bf16[8,128,256]{2,1,0:T(8,128)(2,1)}), bf16[8,128,256]{2,1,0:T(8,128)(2,1)S(1)}, u32[]{:S(2)}, u32[]{:S(2)}) async-start(bf16[8,128,256]{2,1,0:T(8,128)(2,1)} %broadcast_in_dim.42), calls=%async_computation | async-start | bytes 1048576 | tf_op jit(solution)/shard_map/all_to_all | solution.py:43
  18.3 3.1 %collective-permute-start.6 = (bf16[4,64,256]{2,1,0:T(8,128)(2,1)S(1)}, bf16[4,64,256]{2,1,0:T(8,128)(2,1)S(1)}, u32[]{:S(2)}, u32[]{:S(2)}) collective-permute-start(bf16[4,64,256]{2,1,0:T(8,128)(2,1)S(1)} %pad_maximum_fusion.2), channel_id=1, source_target_pairs={{0,96},{16,152},{1,97},{17,153},{2,98},{18,154},{3,99},{19,155},{4... | collective-permute-start | bytes 393224 | tf_op jit(solution)/shard_map/ppermute | solution.py:67
  23.0 2.3 %collective-permute-done.6 = bf16[4,64,256]{2,1,0:T(8,128)(2,1)S(1)} collective-permute-done((bf16[4,64,256]{2,1,0:T(8,128)(2,1)S(1)}, bf16[4,64,256]{2,1,0:T(8,128)(2,1)S(1)}, u32[]{:S(2)}, u32[]{:S(2)}) %collective-permute-start.6) | collective-permute-done | bytes 131104 | tf_op jit(solution)/shard_map/ppermute | solution.py:67
  25.3 2.6 %collective-permute-done.7 = bf16[4,64,256]{2,1,0:T(8,128)(2,1)S(1)} collective-permute-done((bf16[4,64,256]{2,1,0:T(8,128)(2,1)S(1)}, bf16[4,64,256]{2,1,0:T(8,128)(2,1)S(1)}, u32[]{:S(2)}, u32[]{:S(2)}) %collective-permute-start.7) | collective-permute-done | bytes 131104 | tf_op jit(solution)/shard_map/ppermute | solution.py:67
  31.4 4.2 %all-to-all-done = bf16[8,128,256]{2,1,0:T(8,128)(2,1)S(1)} async-done(((bf16[8,128,256]{2,1,0:T(8,128)(2,1)}), bf16[8,128,256]{2,1,0:T(8,128)(2,1)S(1)}, u32[]{:S(2)}, u32[]{:S(2)}) %all-to-all-start) | async-done | bytes 524320 | tf_op jit(solution)/shard_map/all_to_all | solution.py:43
  35.6 3.2 %collective-permute-start.2 = (bf16[8,128,256]{2,1,0:T(8,128)(2,1)S(1)}, bf16[8,128,256]{2,1,0:T(8,128)(2,1)}, u32[]{:S(2)}, u32[]{:S(2)}) collective-permute-start(bf16[8,128,256]{2,1,0:T(8,128)(2,1)S(1)} %all-to-all-done), channel_id=1, source_target_pairs={{0,96},{16,152},{1,97},{17,153},{2,98},{18,154},{3,99},{19,155},{4... | collective-permute-start | bytes 1572872 | tf_op jit(solution)/shard_map/ppermute | solution.py:67
  38.9 7.8 %collective-permute-done.10.refs_23_.refs_9_ = bf16[22,64,256]{2,1,0:T(8,128)(2,1)S(1)} collective-permute-done((bf16[22,64,256]{2,1,0:T(8,128)(2,1)S(1)}, bf16[22,64,256]{2,1,0:T(8,128)(2,1)S(1)}, u32[]{:S(2)}, u32[]{:S(2)}) %collective-permute-start.10) | collective-permute-done | bytes 720928 | tf_op jit(solution)/shard_map/ppermute | solution.py:67
  49.5 3.1 %collective-permute-start.14 = (bf16[2,8,128,256]{3,2,1,0:T(8,128)(2,1)S(1)}, bf16[2,8,128,256]{3,2,1,0:T(8,128)(2,1)S(1)}, u32[]{:S(2)}, u32[]{:S(2)}) collective-permute-start(bf16[2,8,128,256]{3,2,1,0:T(8,128)(2,1)S(1)} %pad_maximum_fusion), channel_id=1, source_target_pairs={{0,136},{16,112},{1,137},{17,113},{2,138},{18,114},{3,139},{19,115... | collective-permute-start | bytes 3145736 | tf_op jit(solution)/shard_map/ppermute | solution.py:67
  52.7 1.9 collective-permute-start.15
  54.7 5.6 %pick_tiles.1 = bf16[8,24,128,128]{3,2,1,0:T(8,128)(2,1)} custom-call(s32[1]{0:T(128)} %bitcast.16.side, bf16[8,2,24,128,128]{4,3,2,1,0:T(8,128)(2,1)} %bitcast.40), custom_call_target="tpu_custom_call" | custom-call | bytes 12582912 | tf_op jit(solution)/shard_map/pick_tiles/pallas_call | solution.py:194
  60.4 7.3 %collective-permute-done.12 = bf16[8,128,256]{2,1,0:T(8,128)(2,1)S(1)} collective-permute-done((bf16[8,128,256]{2,1,0:T(8,128)(2,1)S(1)}, bf16[8,128,256]{2,1,0:T(8,128)(2,1)S(1)}, u32[]{:S(2)}, u32[]{:S(2)}) %collective-permute-start.12) | collective-permute-done | bytes 524320 | tf_op jit(solution)/shard_map/ppermute | solution.py:67
  71.4 3.2 %collective-permute-start.18 = (bf16[2,8,128,256]{3,2,1,0:T(8,128)(2,1)S(1)}, bf16[2,8,128,256]{3,2,1,0:T(8,128)(2,1)}, u32[]{:S(2)}, u32[]{:S(2)}) collective-permute-start(bf16[2,8,128,256]{3,2,1,0:T(8,128)(2,1)S(1)} %pad_maximum_fusion.1), channel_id=1, source_target_pairs={{0,136},{16,112},{1,137},{17,113},{2,138},{18,114},{3,139},{19,115... | collective-permute-start | bytes 3145736 | tf_op jit(solution)/shard_map/ppermute | solution.py:67
  76.7 16.1 %collective-permute-done.19.refs_21_.refs_7_ = bf16[22,64,256]{2,1,0:T(8,128)(2,1)S(1)} collective-permute-done((bf16[22,64,256]{2,1,0:T(8,128)(2,1)}, bf16[22,64,256]{2,1,0:T(8,128)(2,1)S(1)}, u32[]{:S(2)}, u32[]{:S(2)}) %collective-permute-start.19) | collective-permute-done | bytes 720928 | tf_op jit(solution)/shard_map/ppermute | solution.py:67
  92.8 1.9 collective-permute-done.20.refs_18_.refs_5_
  94.8 3.3 %collective-permute-start.23 = (bf16[2,8,128,256]{3,2,1,0:T(8,128)(2,1)}, bf16[2,8,128,256]{3,2,1,0:T(8,128)(2,1)}, u32[]{:S(2)}, u32[]{:S(2)}) collective-permute-start(bf16[2,8,128,256]{3,2,1,0:T(8,128)(2,1)} %collective-permute-done.18), channel_id=1, source_target_pairs={{0,136},{16,112},{1,137},{17,113},{2,138},{18,114},{3,139},{19,115... | collective-permute-start | bytes 3145736 | tf_op jit(solution)/shard_map/ppermute | solution.py:67
  103.6 7.5 %collective-permute-done.22 = bf16[2,8,128,256]{3,2,1,0:T(8,128)(2,1)} collective-permute-done((bf16[2,8,128,256]{3,2,1,0:T(8,128)(2,1)}, bf16[2,8,128,256]{3,2,1,0:T(8,128)(2,1)}, u32[]{:S(2)}, u32[]{:S(2)}) %collective-permute-start.22) | collective-permute-done | bytes 1048608 | tf_op jit(solution)/shard_map/ppermute | solution.py:67
  112.0 20.5 %tile_products.1 = (f32[24,128,256]{2,1,0:T(8,128)}, bf16[24,128,256]{2,1,0:T(8,128)(2,1)}) custom-call(s32[16]{0:T(128)} %min.8.refs_0_, s32[384]{0:T(512)} %fusion.9.refs_1_, s32[384]{0:T(512)} %get-tuple-element.48.refs_2_, s32[384]{0:T(512)} %get-tuple-element.55.refs_3_, s32[3]{0:T(128)} %pad_add_fusion.1.refs_4_.refs_0_, ...), custom_call_target="tpu_custom_call" | custom-call | flops 3221225472 | bytes 31457280 | tf_op jit(solution)/shard_map/tile_products/pallas_call | solution.py:217
  132.6 3.6 %collective-permute-done.26 = bf16[24,128,256]{2,1,0:T(8,128)(2,1)S(1)} collective-permute-done((bf16[24,128,256]{2,1,0:T(8,128)(2,1)}, bf16[24,128,256]{2,1,0:T(8,128)(2,1)S(1)}, u32[]{:S(2)}, u32[]{:S(2)}) %collective-permute-start.26) | collective-permute-done | bytes 1572896 | tf_op jit(solution)/shard_map/ppermute | solution.py:67
  136.2 2.4 %add_convert_fusion = bf16[24,128,256]{2,1,0:T(8,128)(2,1)S(1)} fusion(f32[24,128,256]{2,1,0:T(8,128)} %get-tuple-element.40, bf16[24,128,256]{2,1,0:T(8,128)(2,1)S(1)} %collective-permute-done.26), kind=kLoop, calls=%fused_computation | loop fusion | flops 2359296 | bytes 6291456 | tf_op jit(solution)/shard_map/convert_element_type | solution.py:337
  139.8 6.0 %features_product.1 = f32[256,256]{1,0:T(8,128)} custom-call(s32[3]{0:T(128)} %pad_add_fusion.1.refs_4_.refs_0_, bf16[2,8,192,256]{3,2,1,0:T(8,128)(2,1)} %bitcast.43, bf16[22,64,256]{2,1,0:T(8,128)(2,1)} %copy-done.6, bf16[22,64,256]{2,1,0:T(8,128)(2,1)} %copy-done.8, bf16[22,64,256]{2,1,0:T(8,128)(2,1)} %collective-permute-done.16.refs_17_.refs_4_, ...), custom_call_target="tpu_custom_call" | custom-call | flops 402653184 | bytes 4194304 | tf_op jit(solution)/shard_map/features_product/pallas_call | solution.py:162
  145.7 7.1 %all-to-all-start.1 = ((f32[16,16,256]{2,1,0:T(8,128)}), f32[16,16,256]{2,1,0:T(8,128)S(1)}, u32[]{:S(2)}, u32[]{:S(2)}) async-start(f32[16,16,256]{2,1,0:T(8,128)} %bitcast.48), calls=%async_computation.1 | async-start | bytes 524288 | tf_op jit(solution)/shard_map/all_to_all | solution.py:341
  152.8 10.1 %all-to-all-done.1 = f32[16,16,256]{2,1,0:T(8,128)S(1)} async-done(((f32[16,16,256]{2,1,0:T(8,128)}), f32[16,16,256]{2,1,0:T(8,128)S(1)}, u32[]{:S(2)}, u32[]{:S(2)}) %all-to-all-start.1) | async-done | bytes 262176 | tf_op jit(solution)/shard_map/all_to_all | solution.py:341
  163.0 2.2 %fusion = bf16[8,192,256]{2,1,0:T(8,128)(2,1)} fusion(bf16[8,192,256]{2,1,0:T(8,128)(2,1)S(1)} %collective-permute-done.27, bf16[2,8,192,256]{3,2,1,0:T(8,128)(2,1)} %bitcast.44, s32[]{:T(128)S(6)} %select_n.208), kind=kLoop, calls=%fused_computation.2 | loop fusion | flops 1572864 | bytes 2359300 | tf_op jit(solution)/shard_map/convert_element_type | solution.py:342
  165.2 4.9 %all-to-all-start.2 = ((bf16[8,192,256]{2,1,0:T(8,128)(2,1)}), bf16[8,192,256]{2,1,0:T(8,128)(2,1)S(1)}, u32[]{:S(2)}, u32[]{:S(2)}) async-start(bf16[8,192,256]{2,1,0:T(8,128)(2,1)} %fusion), calls=%async_computation.2 | async-start | bytes 1572864 | tf_op jit(solution)/shard_map/all_to_all | solution.py:344
  172.9 3.5 %collective-permute-done.29 = f32[16,256]{1,0:T(8,128)S(1)} collective-permute-done((f32[16,256]{1,0:T(8,128)S(1)}, f32[16,256]{1,0:T(8,128)S(1)}, u32[]{:S(2)}, u32[]{:S(2)}) %collective-permute-start.29) | collective-permute-done | bytes 16416 | tf_op jit(solution)/shard_map/ppermute | solution.py:67
  176.5 3.7 %collective-permute-done.30 = f32[16,256]{1,0:T(8,128)S(1)} collective-permute-done((f32[16,256]{1,0:T(8,128)S(1)}, f32[16,256]{1,0:T(8,128)S(1)}, u32[]{:S(2)}, u32[]{:S(2)}) %collective-permute-start.30) | collective-permute-done | bytes 16416 | tf_op jit(solution)/shard_map/ppermute | solution.py:67
  180.3 5.1 %collective-permute-done.31 = f32[16,256]{1,0:T(8,128)S(1)} collective-permute-done((f32[16,256]{1,0:T(8,128)S(1)}, f32[16,256]{1,0:T(8,128)S(1)}, u32[]{:S(2)}, u32[]{:S(2)}) %collective-permute-start.31) | collective-permute-done | bytes 16416 | tf_op jit(solution)/shard_map/ppermute | solution.py:67
  185.5 5.7 %all-to-all-done.2 = bf16[8,192,256]{2,1,0:T(8,128)(2,1)S(1)} async-done(((bf16[8,192,256]{2,1,0:T(8,128)(2,1)}), bf16[8,192,256]{2,1,0:T(8,128)(2,1)S(1)}, u32[]{:S(2)}, u32[]{:S(2)}) %all-to-all-start.2) | async-done | bytes 786464 | tf_op jit(solution)/shard_map/all_to_all | solution.py:344
  191.9 4.8 %all-to-all-start.3 = ((f32[16,16,256]{2,1,0:T(8,128)}), f32[16,16,256]{2,1,0:T(8,128)S(1)}, u32[]{:S(2)}, u32[]{:S(2)}) async-start(f32[16,16,256]{2,1,0:T(8,128)} %broadcast_in_dim.43), calls=%async_computation.3 | async-start | bytes 524288 | tf_op jit(solution)/shard_map/all_to_all | solution.py:349
  197.7 9.6 %all-to-all-done.3 = f32[16,16,256]{2,1,0:T(8,128)S(1)} async-done(((f32[16,16,256]{2,1,0:T(8,128)}), f32[16,16,256]{2,1,0:T(8,128)S(1)}, u32[]{:S(2)}, u32[]{:S(2)}) %all-to-all-start.3) | async-done | bytes 262176 | tf_op jit(solution)/shard_map/all_to_all | solution.py:349
  (121 shorter events, 30.2 us)
Async XLA Ops:
  2.5 15.8 %collective-permute-start.4 = (bf16[64,256]{1,0:T(8,128)(2,1)S(1)}, bf16[64,256]{1,0:T(8,128)(2,1)S(1)}, u32[]{:S(2)}, u32[]{:S(2)}) collective-permute-start(bf16[64,256]{1,0:T(8,128)(2,1)S(1)} %get-tuple-element.47), channel_id=1, source_target_pairs={{0,128},{16,80},{1,129},{17,81},{2,130},{18,82},{3,131},{19,83},{4... | collective-permute-start | bytes 98312 | tf_op jit(solution)/shard_map/ppermute | solution.py:67
  5.6 12.7 %collective-permute-start.5 = (bf16[64,256]{1,0:T(8,128)(2,1)S(1)}, bf16[64,256]{1,0:T(8,128)(2,1)S(1)}, u32[]{:S(2)}, u32[]{:S(2)}) collective-permute-start(bf16[64,256]{1,0:T(8,128)(2,1)S(1)} %get-tuple-element.47), channel_id=1, source_target_pairs={{0,8},{16,48},{1,9},{17,49},{2,10},{18,50},{3,11},{19,51},{4,12},{... | collective-permute-start | bytes 98312 | tf_op jit(solution)/shard_map/ppermute | solution.py:67
  6.2 12.1 %collective-permute-start.3 = (bf16[64,256]{1,0:T(8,128)(2,1)S(1)}, bf16[64,256]{1,0:T(8,128)(2,1)S(1)}, u32[]{:S(2)}, u32[]{:S(2)}) collective-permute-start(bf16[64,256]{1,0:T(8,128)(2,1)S(1)} %get-tuple-element.47), channel_id=1, source_target_pairs={{0,136},{16,112},{1,137},{17,113},{2,138},{18,114},{3,139},{19,115... | collective-permute-start | bytes 98312 | tf_op jit(solution)/shard_map/ppermute | solution.py:67
  8.8 20.5 %collective-permute-start.9 = (bf16[192,256]{1,0:T(8,128)(2,1)S(1)}, bf16[192,256]{1,0:T(8,128)(2,1)S(1)}, u32[]{:S(2)}, u32[]{:S(2)}) collective-permute-start(bf16[192,256]{1,0:T(8,128)(2,1)S(1)} %get-tuple-element.56), channel_id=1, source_target_pairs={{0,8},{16,24},{1,9},{17,25},{2,10},{18,26},{3,11},{19,27},{4,12},{... | collective-permute-start | bytes 294920 | tf_op jit(solution)/shard_map/ppermute | solution.py:67
  9.7 25.9 %all-to-all-start = ((bf16[8,128,256]{2,1,0:T(8,128)(2,1)}), bf16[8,128,256]{2,1,0:T(8,128)(2,1)S(1)}, u32[]{:S(2)}, u32[]{:S(2)}) async-start(bf16[8,128,256]{2,1,0:T(8,128)(2,1)} %broadcast_in_dim.42), calls=%async_computation | async-start | bytes 1048576 | tf_op jit(solution)/shard_map/all_to_all | solution.py:43
  18.3 7.0 %collective-permute-start.6 = (bf16[4,64,256]{2,1,0:T(8,128)(2,1)S(1)}, bf16[4,64,256]{2,1,0:T(8,128)(2,1)S(1)}, u32[]{:S(2)}, u32[]{:S(2)}) collective-permute-start(bf16[4,64,256]{2,1,0:T(8,128)(2,1)S(1)} %pad_maximum_fusion.2), channel_id=1, source_target_pairs={{0,96},{16,152},{1,97},{17,153},{2,98},{18,154},{3,99},{19,155},{4... | collective-permute-start | bytes 393224 | tf_op jit(solution)/shard_map/ppermute | solution.py:67
  21.4 6.6 %collective-permute-start.7 = (bf16[4,64,256]{2,1,0:T(8,128)(2,1)S(1)}, bf16[4,64,256]{2,1,0:T(8,128)(2,1)S(1)}, u32[]{:S(2)}, u32[]{:S(2)}) collective-permute-start(bf16[4,64,256]{2,1,0:T(8,128)(2,1)S(1)} %pad_maximum_fusion.2), channel_id=1, source_target_pairs={{0,64},{16,144},{1,65},{17,145},{2,66},{18,146},{3,67},{19,147},{4... | collective-permute-start | bytes 393224 | tf_op jit(solution)/shard_map/ppermute | solution.py:67
  22.0 7.2 %collective-permute-start.8 = (bf16[4,64,256]{2,1,0:T(8,128)(2,1)S(1)}, bf16[4,64,256]{2,1,0:T(8,128)(2,1)S(1)}, u32[]{:S(2)}, u32[]{:S(2)}) collective-permute-start(bf16[4,64,256]{2,1,0:T(8,128)(2,1)S(1)} %pad_maximum_fusion.2), channel_id=1, source_target_pairs={{0,32},{16,24},{1,33},{17,25},{2,34},{18,26},{3,35},{19,27},{4,36}... | collective-permute-start | bytes 393224 | tf_op jit(solution)/shard_map/ppermute | solution.py:67
  29.3 17.3 %collective-permute-start.10 = (bf16[22,64,256]{2,1,0:T(8,128)(2,1)S(1)}, bf16[22,64,256]{2,1,0:T(8,128)(2,1)S(1)}, u32[]{:S(2)}, u32[]{:S(2)}) collective-permute-start(bf16[22,64,256]{2,1,0:T(8,128)(2,1)S(1)} %constant_dynamic-update-slice_fusion.refs_15_.refs_2_), channel_id=1, source_target_pairs={{0,1},{16,17},{1,2},{17,18},{2,3},{18,19},{3,4},{19,20},{4,5},{20,... | collective-permute-start | bytes 2162696 | tf_op jit(solution)/shard_map/ppermute | solution.py:67
  30.9 17.1 %collective-permute-start.11 = (bf16[22,64,256]{2,1,0:T(8,128)(2,1)S(1)}, bf16[22,64,256]{2,1,0:T(8,128)(2,1)S(1)}, u32[]{:S(2)}, u32[]{:S(2)}) collective-permute-start(bf16[22,64,256]{2,1,0:T(8,128)(2,1)S(1)} %constant_dynamic-update-slice_fusion.refs_15_.refs_2_), channel_id=1, source_target_pairs={{0,7},{16,23},{1,0},{17,16},{2,1},{18,17},{3,2},{19,18},{4,3},{20,... | collective-permute-start | bytes 2162696 | tf_op jit(solution)/shard_map/ppermute | solution.py:67
  35.6 12.3 %collective-permute-start.1 = (bf16[8,128,256]{2,1,0:T(8,128)(2,1)S(1)}, bf16[8,128,256]{2,1,0:T(8,128)(2,1)S(1)}, u32[]{:S(2)}, u32[]{:S(2)}) collective-permute-start(bf16[8,128,256]{2,1,0:T(8,128)(2,1)S(1)} %all-to-all-done), channel_id=1, source_target_pairs={{0,32},{16,24},{1,33},{17,25},{2,34},{18,26},{3,35},{19,27},{4,36}... | collective-permute-start | bytes 1572872 | tf_op jit(solution)/shard_map/ppermute | solution.py:67
  35.6 12.3 %collective-permute-start.2 = (bf16[8,128,256]{2,1,0:T(8,128)(2,1)S(1)}, bf16[8,128,256]{2,1,0:T(8,128)(2,1)}, u32[]{:S(2)}, u32[]{:S(2)}) collective-permute-start(bf16[8,128,256]{2,1,0:T(8,128)(2,1)S(1)} %all-to-all-done), channel_id=1, source_target_pairs={{0,96},{16,152},{1,97},{17,153},{2,98},{18,154},{3,99},{19,155},{4... | collective-permute-start | bytes 1572872 | tf_op jit(solution)/shard_map/ppermute | solution.py:67
  49.4 21.7 %collective-permute-start.13 = (bf16[2,8,128,256]{3,2,1,0:T(8,128)(2,1)S(1)}, bf16[2,8,128,256]{3,2,1,0:T(8,128)(2,1)S(1)}, u32[]{:S(2)}, u32[]{:S(2)}) collective-permute-start(bf16[2,8,128,256]{3,2,1,0:T(8,128)(2,1)S(1)} %pad_maximum_fusion), channel_id=1, source_target_pairs={{0,8},{16,48},{1,9},{17,49},{2,10},{18,50},{3,11},{19,51},{4,12},{... | collective-permute-start | bytes 3145736 | tf_op jit(solution)/shard_map/ppermute | solution.py:67
  49.5 21.5 %collective-permute-start.14 = (bf16[2,8,128,256]{3,2,1,0:T(8,128)(2,1)S(1)}, bf16[2,8,128,256]{3,2,1,0:T(8,128)(2,1)S(1)}, u32[]{:S(2)}, u32[]{:S(2)}) collective-permute-start(bf16[2,8,128,256]{3,2,1,0:T(8,128)(2,1)S(1)} %pad_maximum_fusion), channel_id=1, source_target_pairs={{0,136},{16,112},{1,137},{17,113},{2,138},{18,114},{3,139},{19,115... | collective-permute-start | bytes 3145736 | tf_op jit(solution)/shard_map/ppermute | solution.py:67
  52.7 15.9 %collective-permute-start.15 = (bf16[22,64,256]{2,1,0:T(8,128)(2,1)S(1)}, bf16[22,64,256]{2,1,0:T(8,128)(2,1)}, u32[]{:S(2)}, u32[]{:S(2)}) collective-permute-start(bf16[22,64,256]{2,1,0:T(8,128)(2,1)S(1)} %collective-permute-done.10.refs_23_.refs_9_), channel_id=1, source_target_pairs={{0,1},{16,17},{1,2},{17,18},{2,3},{18,19},{3,4},{19,20},{4,5},{20,... | collective-permute-start | bytes 2162696 | tf_op jit(solution)/shard_map/ppermute | solution.py:67
  54.6 15.2 %collective-permute-start.16 = (bf16[22,64,256]{2,1,0:T(8,128)(2,1)S(1)}, bf16[22,64,256]{2,1,0:T(8,128)(2,1)}, u32[]{:S(2)}, u32[]{:S(2)}) collective-permute-start(bf16[22,64,256]{2,1,0:T(8,128)(2,1)S(1)} %collective-permute-done.11.refs_16_.refs_3_), channel_id=1, source_target_pairs={{0,7},{16,23},{1,0},{17,16},{2,1},{18,17},{3,2},{19,18},{4,3},{20,... | collective-permute-start | bytes 2162696 | tf_op jit(solution)/shard_map/ppermute | solution.py:67
  54.7 12.9 %collective-permute-start.12 = (bf16[8,128,256]{2,1,0:T(8,128)(2,1)S(1)}, bf16[8,128,256]{2,1,0:T(8,128)(2,1)S(1)}, u32[]{:S(2)}, u32[]{:S(2)}) collective-permute-start(bf16[8,128,256]{2,1,0:T(8,128)(2,1)S(1)} %collective-permute-done.1), channel_id=1, source_target_pairs={{0,32},{16,24},{1,33},{17,25},{2,34},{18,26},{3,35},{19,27},{4,36}... | collective-permute-start | bytes 1572872 | tf_op jit(solution)/shard_map/ppermute | solution.py:67
  71.1 23.7 %collective-permute-start.21 = (bf16[8,24,128,128]{3,2,1,0:T(8,128)(2,1)}, bf16[8,24,128,128]{3,2,1,0:T(8,128)(2,1)}, u32[]{:S(2)}, u32[]{:S(2)}) collective-permute-start(bf16[8,24,128,128]{3,2,1,0:T(8,128)(2,1)} %pick_tiles.1), channel_id=1, source_target_pairs={{0,16},{16,0},{1,17},{17,1},{2,18},{18,2},{3,19},{19,3},{4,20},{20... | collective-permute-start | bytes 18874376 | tf_op jit(solution)/shard_map/ppermute | solution.py:67
  71.3 23.4 %collective-permute-start.17 = (bf16[2,8,128,256]{3,2,1,0:T(8,128)(2,1)S(1)}, bf16[2,8,128,256]{3,2,1,0:T(8,128)(2,1)}, u32[]{:S(2)}, u32[]{:S(2)}) collective-permute-start(bf16[2,8,128,256]{3,2,1,0:T(8,128)(2,1)S(1)} %pad_maximum_fusion.1), channel_id=1, source_target_pairs={{0,8},{16,48},{1,9},{17,49},{2,10},{18,50},{3,11},{19,51},{4,12},{... | collective-permute-start | bytes 3145736 | tf_op jit(solution)/shard_map/ppermute | solution.py:67
  71.4 23.4 %collective-permute-start.18 = (bf16[2,8,128,256]{3,2,1,0:T(8,128)(2,1)S(1)}, bf16[2,8,128,256]{3,2,1,0:T(8,128)(2,1)}, u32[]{:S(2)}, u32[]{:S(2)}) collective-permute-start(bf16[2,8,128,256]{3,2,1,0:T(8,128)(2,1)S(1)} %pad_maximum_fusion.1), channel_id=1, source_target_pairs={{0,136},{16,112},{1,137},{17,113},{2,138},{18,114},{3,139},{19,115... | collective-permute-start | bytes 3145736 | tf_op jit(solution)/shard_map/ppermute | solution.py:67
  74.6 18.2 %collective-permute-start.19 = (bf16[22,64,256]{2,1,0:T(8,128)(2,1)}, bf16[22,64,256]{2,1,0:T(8,128)(2,1)S(1)}, u32[]{:S(2)}, u32[]{:S(2)}) collective-permute-start(bf16[22,64,256]{2,1,0:T(8,128)(2,1)} %collective-permute-done.15.refs_22_.refs_8_), channel_id=1, source_target_pairs={{0,1},{16,17},{1,2},{17,18},{2,3},{18,19},{3,4},{19,20},{4,5},{20,... | collective-permute-start | bytes 2162696 | tf_op jit(solution)/shard_map/ppermute | solution.py:67
  76.5 18.2 %collective-permute-start.20 = (bf16[22,64,256]{2,1,0:T(8,128)(2,1)}, bf16[22,64,256]{2,1,0:T(8,128)(2,1)S(1)}, u32[]{:S(2)}, u32[]{:S(2)}) collective-permute-start(bf16[22,64,256]{2,1,0:T(8,128)(2,1)} %collective-permute-done.16.refs_17_.refs_4_), channel_id=1, source_target_pairs={{0,7},{16,23},{1,0},{17,16},{2,1},{18,17},{3,2},{19,18},{4,3},{20,... | collective-permute-start | bytes 2162696 | tf_op jit(solution)/shard_map/ppermute | solution.py:67
  92.8 6.4 %collective-permute-start = (s32[8,24]{1,0:T(8,128)S(1)}, s32[8,24]{1,0:T(8,128)S(1)}, u32[]{:S(2)}, u32[]{:S(2)}) collective-permute-start(s32[8,24]{1,0:T(8,128)S(1)} %bitcast.62), channel_id=1, source_target_pairs={{0,16},{16,0},{1,17},{17,1},{2,18},{18,2},{3,19},{19,3},{4,20},{20... | collective-permute-start | bytes 2312 | tf_op jit(solution)/shard_map/ppermute | solution.py:67
  94.7 16.3 %collective-permute-start.22 = (bf16[2,8,128,256]{3,2,1,0:T(8,128)(2,1)}, bf16[2,8,128,256]{3,2,1,0:T(8,128)(2,1)}, u32[]{:S(2)}, u32[]{:S(2)}) collective-permute-start(bf16[2,8,128,256]{3,2,1,0:T(8,128)(2,1)} %copy-done.10), channel_id=1, source_target_pairs={{0,8},{16,48},{1,9},{17,49},{2,10},{18,50},{3,11},{19,51},{4,12},{... | collective-permute-start | bytes 3145736 | tf_op jit(solution)/shard_map/ppermute | solution.py:67
  94.8 16.3 %collective-permute-start.23 = (bf16[2,8,128,256]{3,2,1,0:T(8,128)(2,1)}, bf16[2,8,128,256]{3,2,1,0:T(8,128)(2,1)}, u32[]{:S(2)}, u32[]{:S(2)}) collective-permute-start(bf16[2,8,128,256]{3,2,1,0:T(8,128)(2,1)} %collective-permute-done.18), channel_id=1, source_target_pairs={{0,136},{16,112},{1,137},{17,113},{2,138},{18,114},{3,139},{19,115... | collective-permute-start | bytes 3145736 | tf_op jit(solution)/shard_map/ppermute | solution.py:67
  100.2 10.9 %collective-permute-start.24 = (bf16[11,64,256]{2,1,0:T(8,128)(2,1)S(1)}, bf16[11,64,256]{2,1,0:T(8,128)(2,1)S(1)}, u32[]{:S(2)}, u32[]{:S(2)}) collective-permute-start(bf16[11,64,256]{2,1,0:T(8,128)(2,1)S(1)} %slice.6), channel_id=1, source_target_pairs={{0,1},{16,17},{1,2},{17,18},{2,3},{18,19},{3,4},{19,20},{4,5},{20,... | collective-permute-start | bytes 1081352 | tf_op jit(solution)/shard_map/ppermute | solution.py:67
  102.0 9.1 %collective-permute-start.25 = (bf16[11,64,256]{2,1,0:T(8,128)(2,1)S(1)}, bf16[11,64,256]{2,1,0:T(8,128)(2,1)S(1)}, u32[]{:S(2)}, u32[]{:S(2)}) collective-permute-start(bf16[11,64,256]{2,1,0:T(8,128)(2,1)S(1)} %slice.7), channel_id=1, source_target_pairs={{0,7},{16,23},{1,0},{17,16},{2,1},{18,17},{3,2},{19,18},{4,3},{20,... | collective-permute-start | bytes 1081352 | tf_op jit(solution)/shard_map/ppermute | solution.py:67
  138.7 24.3 %collective-permute-start.27 = (bf16[8,192,256]{2,1,0:T(8,128)(2,1)S(1)}, bf16[8,192,256]{2,1,0:T(8,128)(2,1)S(1)}, u32[]{:S(2)}, u32[]{:S(2)}) collective-permute-start(bf16[8,192,256]{2,1,0:T(8,128)(2,1)S(1)} %dynamic-slice_bitcast_fusion), channel_id=1, source_target_pairs={{0,8},{16,24},{1,9},{17,25},{2,10},{18,26},{3,11},{19,27},{4,12},{... | collective-permute-start | bytes 2359304 | tf_op jit(solution)/shard_map/ppermute | solution.py:67
  145.7 17.2 %all-to-all-start.1 = ((f32[16,16,256]{2,1,0:T(8,128)}), f32[16,16,256]{2,1,0:T(8,128)S(1)}, u32[]{:S(2)}, u32[]{:S(2)}) async-start(f32[16,16,256]{2,1,0:T(8,128)} %bitcast.48), calls=%async_computation.1 | async-start | bytes 524288 | tf_op jit(solution)/shard_map/all_to_all | solution.py:341
  165.2 26.0 %all-to-all-start.2 = ((bf16[8,192,256]{2,1,0:T(8,128)(2,1)}), bf16[8,192,256]{2,1,0:T(8,128)(2,1)S(1)}, u32[]{:S(2)}, u32[]{:S(2)}) async-start(bf16[8,192,256]{2,1,0:T(8,128)(2,1)} %fusion), calls=%async_computation.2 | async-start | bytes 1572864 | tf_op jit(solution)/shard_map/all_to_all | solution.py:344
  171.2 5.2 %collective-permute-start.29 = (f32[16,256]{1,0:T(8,128)S(1)}, f32[16,256]{1,0:T(8,128)S(1)}, u32[]{:S(2)}, u32[]{:S(2)}) collective-permute-start(f32[16,256]{1,0:T(8,128)S(1)} %add.256), channel_id=1, source_target_pairs={{0,128},{16,144},{1,129},{17,145},{2,130},{18,146},{3,131},{19,147... | collective-permute-start | bytes 49160 | tf_op jit(solution)/shard_map/ppermute | solution.py:67
  191.9 15.4 %all-to-all-start.3 = ((f32[16,16,256]{2,1,0:T(8,128)}), f32[16,16,256]{2,1,0:T(8,128)S(1)}, u32[]{:S(2)}, u32[]{:S(2)}) async-start(f32[16,16,256]{2,1,0:T(8,128)} %broadcast_in_dim.43), calls=%async_computation.3 | async-start | bytes 524288 | tf_op jit(solution)/shard_map/all_to_all | solution.py:349
  (19 other events, 397.1 us)

commit v7 on v6

--- a/solution.py
+++ b/solution.py
@@ -128,52 +128,65 @@
         other_out[...] = totals[half:].astype(other_out.dtype)
 
 
-def features_kernel(places, here, partial, *rest):
+def turn_kernel(places, *rest):
     pieces = rest[: len(places)]
-    gradient, features, sem = rest[len(places):]
-    step = pl.program_id(0)
-
-    @pl.when(step == 0)
+    turned, held, sem = rest[len(places):]
+    copies = [
+        pltpu.make_async_copy(piece.at[pl.ds(start, held.shape[1])], held.at[n], sem.at[n])
+        for n, (piece, start) in enumerate(zip(pieces, places))
+    ]
+    for copy in copies:
+        copy.start()
+    for n, copy in enumerate(copies):
+        copy.wait()
+        turned[n] = jnp.concatenate([held[n, k] for k in range(held.shape[1])], axis=0).T
+
+
+def turn_features(pieces, places):
+    width = pieces[0].shape[-1]
+    return pl.pallas_call(
+        lambda *refs: turn_kernel(places, *refs),
+        out_shape=jax.ShapeDtypeStruct((NZ, width, 384), jnp.bfloat16),
+        grid_spec=pltpu.PrefetchScalarGridSpec(
+            num_scalar_prefetch=0,
+            grid=(),
+            in_specs=[pl.BlockSpec(memory_space=pl.ANY)] * NZ,
+            out_specs=pl.BlockSpec(memory_space=pltpu.VMEM),
+            scratch_shapes=[pltpu.VMEM((NZ, 6, 64, width), jnp.bfloat16), pltpu.SemaphoreType.DMA((NZ,))],
+        ),
+        compiler_params=pltpu.CompilerParams(vmem_limit_bytes=56 << 20),
+        cost_estimate=pl.CostEstimate(flops=0, bytes_accessed=4 << 20, transcendentals=0),
+        name="turn_features",
+    )(*pieces)
+
+
+def features_kernel(here, turned, partial, gradient):
+    @pl.when(pl.program_id(0) == 0)
     def _():
-        copies = [
-            pltpu.make_async_copy(piece.at[pl.ds(start, features.shape[1])], features.at[n], sem.at[n])
-            for n, (piece, start) in enumerate(zip(pieces, places))
-        ]
-        for copy in copies:
-            copy.start()
         gradient[...] = jnp.zeros_like(gradient)
-        for copy in copies:
-            copy.wait()
-
-    total = gradient[...]
-    for part in range(2):
-        place = 2 * step + part
-        ahead = lax.rem(place - here[2] + NZ, NZ)
-        for low in range(2):
-            near = lax.bitwise_xor(low, here[1])
-            lanes = jnp.concatenate([features[ahead, 3 * near + n] for n in range(3)], axis=0)
-            total += lax.dot_general(
-                lanes, partial[low, part], (((0,), (0,)), ((), ())), preferred_element_type=jnp.float32)
-    gradient[...] = total
-
-
-def features_product(partial, pieces, places, here):
+
+    rows = jnp.concatenate([partial[here[1], 0], partial[1 - here[1], 0]], axis=0)
+    gradient[...] += jnp.dot(turned[0], rows, preferred_element_type=jnp.float32)
+
+
+def features_product(partial, turned, here):
     width = partial.shape[-1]
     return pl.pallas_call(
-        lambda *refs: features_kernel(places, *refs),
+        features_kernel,
         out_shape=jax.ShapeDtypeStruct((width, width), jnp.float32),
         grid_spec=pltpu.PrefetchScalarGridSpec(
             num_scalar_prefetch=1,
-            grid=(NZ // 2,),
-            in_specs=[pl.BlockSpec((2, 2, 192, width), lambda d, here: (0, d, 0, 0))]
-            + [pl.BlockSpec(memory_space=pl.ANY)] * NZ,
+            grid=(NZ,),
+            in_specs=[
+                pl.BlockSpec((1, width, 384), lambda d, here: (lax.rem(d - here[2] + NZ, NZ), 0, 0)),
+                pl.BlockSpec((2, 1, 192, width), lambda d, here: (0, d, 0, 0)),
+            ],
             out_specs=pl.BlockSpec((width, width), lambda d, here: (0, 0)),
-            scratch_shapes=[pltpu.VMEM((NZ, 6, 64, width), jnp.bfloat16), pltpu.SemaphoreType.DMA((NZ,))],
         ),
         compiler_params=pltpu.CompilerParams(vmem_limit_bytes=56 << 20),
         cost_estimate=pl.CostEstimate(flops=2 * 3072 * width * width, bytes_accessed=4 << 20, transcendentals=0),
         name="features_product",
-    )(here, partial, *pieces)
+    )(here, turned, partial)
 
 
 def pick_kernel(side, tiles, picked, held, in_sem, out_sem):
@@ -334,8 +347,9 @@
 
     here = jnp.stack([core, own_rep // NZ, z]).astype(jnp.int32)
     own, other = products(by_parity, received, chunks, places, counts, unit0, unit1, columns, here)
-    partial = (own + send(other, flip).astype(jnp.float32)).astype(jnp.bfloat16).reshape(2, NZ, -1, width)
-    local_weight = features_product(partial, feature_pieces, feature_places, here)
+    other, turned = together(send(other, flip), turn_features(feature_pieces, feature_places))
+    partial = (own + other.astype(jnp.float32)).astype(jnp.bfloat16).reshape(2, NZ, -1, width)
+    local_weight = features_product(partial, turned, here)
     near = lax.dynamic_index_in_dim(partial, own_rep // NZ, 0, keepdims=False)
     across = send(lax.dynamic_index_in_dim(partial, 1 - own_rep // NZ, 0, keepdims=False), across_x())
     own_rows = lax.all_to_all(local_weight, "rep", 0, 0, tiled=True).reshape(16, 16, width).sum(axis=0)
@@ -344,8 +358,8 @@
     terms = lax.all_to_all(line, BOTH, 0, 0, axis_index_groups=z_lines(), tiled=True)
     for partner in (other_core(), opposite_x(), paired_y(1), paired_y(2)):
         own_rows = own_rows + send(own_rows, partner)
-    own_rows, terms = together(own_rows, terms)
     spread = jnp.broadcast_to(own_rows[None], (16, 16, width)).reshape(256, width)
+    spread, terms = together(spread, terms)
     weight_grad = lax.all_to_all(spread, "rep", 0, 0, tiled=True)
     summed = terms.astype(jnp.float32).sum(axis=0)
 

time: 208 us -> 204 us (0.981)
  waiting for transfers between devices: 98.3 us -> 88.4 us
  Pallas kernels: 32 us -> 36.4 us
  starting transfers between devices: 60 us -> 62.7 us
    ppermute x32, waiting for transfers between devices: 68.8 us -> 64.1 us  [send(): return lax.ppermute(value, BOTH, moves)]
    pallas_call x1 -> x2, Pallas kernels: 5.95 us -> 10 us  [the longest x1 6.89 us: features_product(): pl.pallas_call(features_kernel, out_shape=jax.ShapeDtypeStruct((width, wi...]
    all_to_all x1, waiting for transfers between devices: 4.18 us -> 0.51 us  [spread_over(): lax.all_to_all(copies, BOTH, 0, 0, axis_index_groups=places, tiled=True)]
    ppermute x32, starting transfers between devices: 34.6 us -> 37.8 us  [send(): return lax.ppermute(value, BOTH, moves)]
  transfers between devices with their start and end apart: 36 -> 36, of which waited for: 21 -> 21; matrix products, arithmetic and copies ran while one was open for 3% -> 3% of each run, Pallas kernels for 6% -> 8%
where the time goes in v7:
time: 204 us; the launch traced here: 203 us
  waiting for transfers between devices  88.4 us (43%)
  starting transfers between devices  62.7 us (31%)
  Pallas kernels  36.4 us (18%)
  other arithmetic  8.22 us (4%)
  local copies, waits for them, and re-layouts  5.58 us (3%)
    ppermute x32, waiting for transfers between devices, send(): return lax.ppermute(value, BOTH, moves)  64.1 us
    ppermute x32, starting transfers between devices, send(): return lax.ppermute(value, BOTH, moves)  37.8 us
    pallas_call x1, Pallas kernels, products(): pl.pallas_call(lambda *refs: products_kernel(places, *refs), out_shape=(j...  20.8 us
    all_to_all x1, waiting for transfers between devices, body(): lax.all_to_all(local_weight, 'rep', 0, 0, tiled=True).reshape(16, 16, width)  10.1 us
    all_to_all x1, starting transfers between devices, spread_over(): lax.all_to_all(copies, BOTH, 0, 0, axis_index_groups=places, tiled=True)  8.57 us
    all_to_all x1, waiting for transfers between devices, body(): weight_grad = lax.all_to_all(spread, 'rep', 0, 0, tiled=True)  8.52 us
    all_to_all x1, starting transfers between devices, body(): lax.all_to_all(local_weight, 'rep', 0, 0, tiled=True).reshape(16, 16, width)  7.17 us
    pallas_call x1, Pallas kernels, features_product(): pl.pallas_call(features_kernel, out_shape=jax.ShapeDtypeStruct((width, wi...  6.89 us
  transfers between devices with their start and end apart: 36, of which 21 were waited for; matrix products, arithmetic and copies ran while one was open for 3% of the time, Pallas kernels for 8%

profile of v7, /device:TPU:32, one launch (start us, length us, event | category | flops | bytes accessed | tf_op | source)
XLA Modules:
  0.0 203.3 jit_solution(6017024404954565680)
XLA Ops:
  2.5 2.8 %collective-permute-start.3 = (bf16[64,256]{1,0:T(8,128)(2,1)S(1)}, bf16[64,256]{1,0:T(8,128)(2,1)S(1)}, u32[]{:S(2)}, u32[]{:S(2)}) collective-permute-start(bf16[64,256]{1,0:T(8,128)(2,1)S(1)} %get-tuple-element.51), channel_id=1, source_target_pairs={{0,136},{16,112},{1,137},{17,113},{2,138},{18,114},{3,139},{19,115... | collective-permute-start | bytes 98312 | tf_op jit(solution)/shard_map/ppermute | solution.py:67
  7.8 8.6 %all-to-all-start = ((bf16[8,128,256]{2,1,0:T(8,128)(2,1)}), bf16[8,128,256]{2,1,0:T(8,128)(2,1)S(1)}, u32[]{:S(2)}, u32[]{:S(2)}) async-start(bf16[8,128,256]{2,1,0:T(8,128)(2,1)} %broadcast_in_dim.42), calls=%async_computation | async-start | bytes 1048576 | tf_op jit(solution)/shard_map/all_to_all | solution.py:43
  18.3 3.1 %collective-permute-start.6 = (bf16[4,64,256]{2,1,0:T(8,128)(2,1)S(1)}, bf16[4,64,256]{2,1,0:T(8,128)(2,1)S(1)}, u32[]{:S(2)}, u32[]{:S(2)}) collective-permute-start(bf16[4,64,256]{2,1,0:T(8,128)(2,1)S(1)} %pad_maximum_fusion.2), channel_id=1, source_target_pairs={{0,96},{16,152},{1,97},{17,153},{2,98},{18,154},{3,99},{19,155},{4... | collective-permute-start | bytes 393224 | tf_op jit(solution)/shard_map/ppermute | solution.py:67
  23.0 2.3 %collective-permute-done.6 = bf16[4,64,256]{2,1,0:T(8,128)(2,1)S(1)} collective-permute-done((bf16[4,64,256]{2,1,0:T(8,128)(2,1)S(1)}, bf16[4,64,256]{2,1,0:T(8,128)(2,1)S(1)}, u32[]{:S(2)}, u32[]{:S(2)}) %collective-permute-start.6) | collective-permute-done | bytes 131104 | tf_op jit(solution)/shard_map/ppermute | solution.py:67
  25.3 2.6 %collective-permute-done.7 = bf16[4,64,256]{2,1,0:T(8,128)(2,1)S(1)} collective-permute-done((bf16[4,64,256]{2,1,0:T(8,128)(2,1)S(1)}, bf16[4,64,256]{2,1,0:T(8,128)(2,1)S(1)}, u32[]{:S(2)}, u32[]{:S(2)}) %collective-permute-start.7) | collective-permute-done | bytes 131104 | tf_op jit(solution)/shard_map/ppermute | solution.py:67
  31.9 1.9 collective-permute-start.1
  35.1 9.3 %collective-permute-done.10.refs_23_.refs_7_ = bf16[22,64,256]{2,1,0:T(8,128)(2,1)S(1)} collective-permute-done((bf16[22,64,256]{2,1,0:T(8,128)(2,1)S(1)}, bf16[22,64,256]{2,1,0:T(8,128)(2,1)S(1)}, u32[]{:S(2)}, u32[]{:S(2)}) %collective-permute-start.10) | collective-permute-done | bytes 720928 | tf_op jit(solution)/shard_map/ppermute | solution.py:67
  47.8 2.7 %collective-permute-start.14 = (bf16[2,8,128,256]{3,2,1,0:T(8,128)(2,1)S(1)}, bf16[2,8,128,256]{3,2,1,0:T(8,128)(2,1)S(1)}, u32[]{:S(2)}, u32[]{:S(2)}) collective-permute-start(bf16[2,8,128,256]{3,2,1,0:T(8,128)(2,1)S(1)} %pad_maximum_fusion), channel_id=1, source_target_pairs={{0,136},{16,112},{1,137},{17,113},{2,138},{18,114},{3,139},{19,115... | collective-permute-start | bytes 3145736 | tf_op jit(solution)/shard_map/ppermute | solution.py:67
  50.5 2.0 %collective-permute-start.15 = (bf16[22,64,256]{2,1,0:T(8,128)(2,1)S(1)}, bf16[22,64,256]{2,1,0:T(8,128)(2,1)}, u32[]{:S(2)}, u32[]{:S(2)}) collective-permute-start(bf16[22,64,256]{2,1,0:T(8,128)(2,1)S(1)} %collective-permute-done.10.refs_23_.refs_7_), channel_id=1, source_target_pairs={{0,1},{16,17},{1,2},{17,18},{2,3},{18,19},{3,4},{19,20},{4,5},{20,... | collective-permute-start | bytes 2162696 | tf_op jit(solution)/shard_map/ppermute | solution.py:67
  52.5 1.9 collective-permute-start.12
  54.4 5.6 %pick_tiles.1 = bf16[8,24,128,128]{3,2,1,0:T(8,128)(2,1)} custom-call(s32[1]{0:T(128)} %bitcast.16.side, bf16[8,2,24,128,128]{4,3,2,1,0:T(8,128)(2,1)} %bitcast.42), custom_call_target="tpu_custom_call" | custom-call | bytes 12582912 | tf_op jit(solution)/shard_map/pick_tiles/pallas_call | solution.py:207
  60.1 5.0 %collective-permute-done.12 = bf16[8,128,256]{2,1,0:T(8,128)(2,1)S(1)} collective-permute-done((bf16[8,128,256]{2,1,0:T(8,128)(2,1)S(1)}, bf16[8,128,256]{2,1,0:T(8,128)(2,1)S(1)}, u32[]{:S(2)}, u32[]{:S(2)}) %collective-permute-start.12) | collective-permute-done | bytes 524320 | tf_op jit(solution)/shard_map/ppermute | solution.py:67
  69.2 3.2 %collective-permute-start.18 = (bf16[2,8,128,256]{3,2,1,0:T(8,128)(2,1)S(1)}, bf16[2,8,128,256]{3,2,1,0:T(8,128)(2,1)}, u32[]{:S(2)}, u32[]{:S(2)}) collective-permute-start(bf16[2,8,128,256]{3,2,1,0:T(8,128)(2,1)S(1)} %pad_maximum_fusion.1), channel_id=1, source_target_pairs={{0,136},{16,112},{1,137},{17,113},{2,138},{18,114},{3,139},{19,115... | collective-permute-start | bytes 3145736 | tf_op jit(solution)/shard_map/ppermute | solution.py:67
  72.4 2.0 %collective-permute-start.19 = (bf16[22,64,256]{2,1,0:T(8,128)(2,1)}, bf16[22,64,256]{2,1,0:T(8,128)(2,1)S(1)}, u32[]{:S(2)}, u32[]{:S(2)}) collective-permute-start(bf16[22,64,256]{2,1,0:T(8,128)(2,1)} %collective-permute-done.15.refs_22_.refs_6_), channel_id=1, source_target_pairs={{0,1},{16,17},{1,2},{17,18},{2,3},{18,19},{3,4},{19,20},{4,5},{20,... | collective-permute-start | bytes 2162696 | tf_op jit(solution)/shard_map/ppermute | solution.py:67
  74.6 16.0 %collective-permute-done.19.refs_21_.refs_5_ = bf16[22,64,256]{2,1,0:T(8,128)(2,1)S(1)} collective-permute-done((bf16[22,64,256]{2,1,0:T(8,128)(2,1)}, bf16[22,64,256]{2,1,0:T(8,128)(2,1)S(1)}, u32[]{:S(2)}, u32[]{:S(2)}) %collective-permute-start.19) | collective-permute-done | bytes 720928 | tf_op jit(solution)/shard_map/ppermute | solution.py:67
  90.6 2.2 %collective-permute-done.20.refs_18_.refs_3_ = bf16[22,64,256]{2,1,0:T(8,128)(2,1)S(1)} collective-permute-done((bf16[22,64,256]{2,1,0:T(8,128)(2,1)}, bf16[22,64,256]{2,1,0:T(8,128)(2,1)S(1)}, u32[]{:S(2)}, u32[]{:S(2)}) %collective-permute-start.20) | collective-permute-done | bytes 720928 | tf_op jit(solution)/shard_map/ppermute | solution.py:67
  92.8 3.3 %collective-permute-start.23 = (bf16[2,8,128,256]{3,2,1,0:T(8,128)(2,1)}, bf16[2,8,128,256]{3,2,1,0:T(8,128)(2,1)}, u32[]{:S(2)}, u32[]{:S(2)}) collective-permute-start(bf16[2,8,128,256]{3,2,1,0:T(8,128)(2,1)} %collective-permute-done.18), channel_id=1, source_target_pairs={{0,136},{16,112},{1,137},{17,113},{2,138},{18,114},{3,139},{19,115... | collective-permute-start | bytes 3145736 | tf_op jit(solution)/shard_map/ppermute | solution.py:67
  101.6 7.5 %collective-permute-done.22 = bf16[2,8,128,256]{3,2,1,0:T(8,128)(2,1)} collective-permute-done((bf16[2,8,128,256]{3,2,1,0:T(8,128)(2,1)}, bf16[2,8,128,256]{3,2,1,0:T(8,128)(2,1)}, u32[]{:S(2)}, u32[]{:S(2)}) %collective-permute-start.22) | collective-permute-done | bytes 1048608 | tf_op jit(solution)/shard_map/ppermute | solution.py:67
  110.0 20.8 %tile_products.1 = (f32[24,128,256]{2,1,0:T(8,128)}, bf16[24,128,256]{2,1,0:T(8,128)(2,1)}) custom-call(s32[16]{0:T(128)} %min.8.refs_0_, s32[384]{0:T(512)} %fusion.9.refs_1_, s32[384]{0:T(512)} %get-tuple-element.52.refs_2_, s32[384]{0:T(512)} %get-tuple-element.59.refs_3_, s32[3]{0:T(128)} %pad_add_fusion.1.refs_4_.here, ...), custom_call_target="tpu_custom_call" | custom-call | flops 3221225472 | bytes 31457280 | tf_op jit(solution)/shard_map/tile_products/pallas_call | solution.py:230
  130.9 3.2 %turn_features.1.turned = bf16[8,256,384]{2,1,0:T(8,128)(2,1)} custom-call(bf16[22,64,256]{2,1,0:T(8,128)(2,1)} %copy-done.7, bf16[22,64,256]{2,1,0:T(8,128)(2,1)} %copy-done.9, bf16[22,64,256]{2,1,0:T(8,128)(2,1)} %collective-permute-done.16.refs_17_.refs_2_, bf16[22,64,256]{2,1,0:T(8,128)(2,1)} %copy-done.3, bf16[11,64,256]{2,1,0:T(8,128)(2,1)} %copy-done.10, ...), custom_call_target="tpu_custom_call" | custom-call | bytes 4194304 | tf_op jit(solution)/shard_map/turn_features/pallas_call | solution.py:147
  136.2 6.9 %features_product.1 = f32[256,256]{1,0:T(8,128)} custom-call(s32[3]{0:T(128)} %pad_add_fusion.1.refs_4_.here, bf16[8,256,384]{2,1,0:T(8,128)(2,1)} %turn_features.1.turned, bf16[2,8,192,256]{3,2,1,0:T(8,128)(2,1)} %bitcast.45), custom_call_target="tpu_custom_call" | custom-call | flops 402653184 | bytes 4194304 | tf_op jit(solution)/shard_map/features_product/pallas_call | solution.py:174
  143.0 7.2 %all-to-all-start.1 = ((f32[16,16,256]{2,1,0:T(8,128)}), f32[16,16,256]{2,1,0:T(8,128)S(1)}, u32[]{:S(2)}, u32[]{:S(2)}) async-start(f32[16,16,256]{2,1,0:T(8,128)} %bitcast.50), calls=%async_computation.1 | async-start | bytes 524288 | tf_op jit(solution)/shard_map/all_to_all | solution.py:355
  150.2 10.1 %all-to-all-done.1 = f32[16,16,256]{2,1,0:T(8,128)S(1)} async-done(((f32[16,16,256]{2,1,0:T(8,128)}), f32[16,16,256]{2,1,0:T(8,128)S(1)}, u32[]{:S(2)}, u32[]{:S(2)}) %all-to-all-start.1) | async-done | bytes 262176 | tf_op jit(solution)/shard_map/all_to_all | solution.py:355
  160.3 2.2 %fusion = bf16[8,192,256]{2,1,0:T(8,128)(2,1)} fusion(bf16[8,192,256]{2,1,0:T(8,128)(2,1)S(1)} %collective-permute-done.27, bf16[2,8,192,256]{3,2,1,0:T(8,128)(2,1)} %bitcast.46, s32[]{:T(128)S(6)} %select_n.208), kind=kLoop, calls=%fused_computation.2 | loop fusion | flops 1572864 | bytes 2359300 | tf_op jit(solution)/shard_map/convert_element_type | solution.py:356
  162.5 4.4 %all-to-all-start.2 = ((bf16[8,192,256]{2,1,0:T(8,128)(2,1)}), bf16[8,192,256]{2,1,0:T(8,128)(2,1)S(1)}, u32[]{:S(2)}, u32[]{:S(2)}) async-start(bf16[8,192,256]{2,1,0:T(8,128)(2,1)} %fusion), calls=%async_computation.2 | async-start | bytes 1572864 | tf_op jit(solution)/shard_map/all_to_all | solution.py:358
  168.1 2.4 %collective-permute-start.29 = (f32[16,256]{1,0:T(8,128)S(1)}, f32[16,256]{1,0:T(8,128)S(1)}, u32[]{:S(2)}, u32[]{:S(2)}) collective-permute-start(f32[16,256]{1,0:T(8,128)S(1)} %add.256), channel_id=1, source_target_pairs={{0,128},{16,144},{1,129},{17,145},{2,130},{18,146},{3,131},{19,147... | collective-permute-start | bytes 49160 | tf_op jit(solution)/shard_map/ppermute | solution.py:67
  170.5 2.8 %collective-permute-done.29 = f32[16,256]{1,0:T(8,128)S(1)} collective-permute-done((f32[16,256]{1,0:T(8,128)S(1)}, f32[16,256]{1,0:T(8,128)S(1)}, u32[]{:S(2)}, u32[]{:S(2)}) %collective-permute-start.29) | collective-permute-done | bytes 16416 | tf_op jit(solution)/shard_map/ppermute | solution.py:67
  173.4 3.7 %collective-permute-done.30 = f32[16,256]{1,0:T(8,128)S(1)} collective-permute-done((f32[16,256]{1,0:T(8,128)S(1)}, f32[16,256]{1,0:T(8,128)S(1)}, u32[]{:S(2)}, u32[]{:S(2)}) %collective-permute-start.30) | collective-permute-done | bytes 16416 | tf_op jit(solution)/shard_map/ppermute | solution.py:67
  177.8 4.6 %collective-permute-done.31 = f32[16,256]{1,0:T(8,128)S(1)} collective-permute-done((f32[16,256]{1,0:T(8,128)S(1)}, f32[16,256]{1,0:T(8,128)S(1)}, u32[]{:S(2)}, u32[]{:S(2)}) %collective-permute-start.31) | collective-permute-done | bytes 16416 | tf_op jit(solution)/shard_map/ppermute | solution.py:67
  182.4 5.2 %all-to-all-done.2 = bf16[8,192,256]{2,1,0:T(8,128)(2,1)S(1)} async-done(((bf16[8,192,256]{2,1,0:T(8,128)(2,1)}), bf16[8,192,256]{2,1,0:T(8,128)(2,1)S(1)}, u32[]{:S(2)}, u32[]{:S(2)}) %all-to-all-start.2) | async-done | bytes 786464 | tf_op jit(solution)/shard_map/all_to_all | solution.py:358
  188.3 4.8 %all-to-all-start.3 = ((f32[16,16,256]{2,1,0:T(8,128)}), f32[16,16,256]{2,1,0:T(8,128)S(1)}, u32[]{:S(2)}, u32[]{:S(2)}) async-start(f32[16,16,256]{2,1,0:T(8,128)} %bitcast.32), calls=%async_computation.3 | async-start | bytes 524288 | tf_op jit(solution)/shard_map/all_to_all | solution.py:363
  194.0 8.5 %all-to-all-done.3 = f32[16,16,256]{2,1,0:T(8,128)S(1)} async-done(((f32[16,16,256]{2,1,0:T(8,128)}), f32[16,16,256]{2,1,0:T(8,128)S(1)}, u32[]{:S(2)}, u32[]{:S(2)}) %all-to-all-start.3) | async-done | bytes 262176 | tf_op jit(solution)/shard_map/all_to_all | solution.py:363
  (124 shorter events, 33.4 us)
Async XLA Ops:
  2.5 15.7 %collective-permute-start.3 = (bf16[64,256]{1,0:T(8,128)(2,1)S(1)}, bf16[64,256]{1,0:T(8,128)(2,1)S(1)}, u32[]{:S(2)}, u32[]{:S(2)}) collective-permute-start(bf16[64,256]{1,0:T(8,128)(2,1)S(1)} %get-tuple-element.51), channel_id=1, source_target_pairs={{0,136},{16,112},{1,137},{17,113},{2,138},{18,114},{3,139},{19,115... | collective-permute-start | bytes 98312 | tf_op jit(solution)/shard_map/ppermute | solution.py:67
  5.3 12.9 %collective-permute-start.4 = (bf16[64,256]{1,0:T(8,128)(2,1)S(1)}, bf16[64,256]{1,0:T(8,128)(2,1)S(1)}, u32[]{:S(2)}, u32[]{:S(2)}) collective-permute-start(bf16[64,256]{1,0:T(8,128)(2,1)S(1)} %get-tuple-element.51), channel_id=1, source_target_pairs={{0,128},{16,80},{1,129},{17,81},{2,130},{18,82},{3,131},{19,83},{4... | collective-permute-start | bytes 98312 | tf_op jit(solution)/shard_map/ppermute | solution.py:67
  6.1 12.1 %collective-permute-start.5 = (bf16[64,256]{1,0:T(8,128)(2,1)S(1)}, bf16[64,256]{1,0:T(8,128)(2,1)S(1)}, u32[]{:S(2)}, u32[]{:S(2)}) collective-permute-start(bf16[64,256]{1,0:T(8,128)(2,1)S(1)} %get-tuple-element.51), channel_id=1, source_target_pairs={{0,8},{16,48},{1,9},{17,49},{2,10},{18,50},{3,11},{19,51},{4,12},{... | collective-permute-start | bytes 98312 | tf_op jit(solution)/shard_map/ppermute | solution.py:67
  7.8 24.1 %all-to-all-start = ((bf16[8,128,256]{2,1,0:T(8,128)(2,1)}), bf16[8,128,256]{2,1,0:T(8,128)(2,1)S(1)}, u32[]{:S(2)}, u32[]{:S(2)}) async-start(bf16[8,128,256]{2,1,0:T(8,128)(2,1)} %broadcast_in_dim.42), calls=%async_computation | async-start | bytes 1048576 | tf_op jit(solution)/shard_map/all_to_all | solution.py:43
  16.4 12.8 %collective-permute-start.9 = (bf16[192,256]{1,0:T(8,128)(2,1)S(1)}, bf16[192,256]{1,0:T(8,128)(2,1)S(1)}, u32[]{:S(2)}, u32[]{:S(2)}) collective-permute-start(bf16[192,256]{1,0:T(8,128)(2,1)S(1)} %get-tuple-element.60), channel_id=1, source_target_pairs={{0,8},{16,24},{1,9},{17,25},{2,10},{18,26},{3,11},{19,27},{4,12},{... | collective-permute-start | bytes 294920 | tf_op jit(solution)/shard_map/ppermute | solution.py:67
  18.3 7.0 %collective-permute-start.6 = (bf16[4,64,256]{2,1,0:T(8,128)(2,1)S(1)}, bf16[4,64,256]{2,1,0:T(8,128)(2,1)S(1)}, u32[]{:S(2)}, u32[]{:S(2)}) collective-permute-start(bf16[4,64,256]{2,1,0:T(8,128)(2,1)S(1)} %pad_maximum_fusion.2), channel_id=1, source_target_pairs={{0,96},{16,152},{1,97},{17,153},{2,98},{18,154},{3,99},{19,155},{4... | collective-permute-start | bytes 393224 | tf_op jit(solution)/shard_map/ppermute | solution.py:67
  21.4 6.6 %collective-permute-start.7 = (bf16[4,64,256]{2,1,0:T(8,128)(2,1)S(1)}, bf16[4,64,256]{2,1,0:T(8,128)(2,1)S(1)}, u32[]{:S(2)}, u32[]{:S(2)}) collective-permute-start(bf16[4,64,256]{2,1,0:T(8,128)(2,1)S(1)} %pad_maximum_fusion.2), channel_id=1, source_target_pairs={{0,64},{16,144},{1,65},{17,145},{2,66},{18,146},{3,67},{19,147},{4... | collective-permute-start | bytes 393224 | tf_op jit(solution)/shard_map/ppermute | solution.py:67
  22.0 7.2 %collective-permute-start.8 = (bf16[4,64,256]{2,1,0:T(8,128)(2,1)S(1)}, bf16[4,64,256]{2,1,0:T(8,128)(2,1)S(1)}, u32[]{:S(2)}, u32[]{:S(2)}) collective-permute-start(bf16[4,64,256]{2,1,0:T(8,128)(2,1)S(1)} %pad_maximum_fusion.2), channel_id=1, source_target_pairs={{0,32},{16,24},{1,33},{17,25},{2,34},{18,26},{3,35},{19,27},{4,36}... | collective-permute-start | bytes 393224 | tf_op jit(solution)/shard_map/ppermute | solution.py:67
  29.3 15.1 %collective-permute-start.10 = (bf16[22,64,256]{2,1,0:T(8,128)(2,1)S(1)}, bf16[22,64,256]{2,1,0:T(8,128)(2,1)S(1)}, u32[]{:S(2)}, u32[]{:S(2)}) collective-permute-start(bf16[22,64,256]{2,1,0:T(8,128)(2,1)S(1)} %constant_dynamic-update-slice_fusion.refs_15_.refs_0_), channel_id=1, source_target_pairs={{0,1},{16,17},{1,2},{17,18},{2,3},{18,19},{3,4},{19,20},{4,5},{20,... | collective-permute-start | bytes 2162696 | tf_op jit(solution)/shard_map/ppermute | solution.py:67
  30.8 14.9 %collective-permute-start.11 = (bf16[22,64,256]{2,1,0:T(8,128)(2,1)S(1)}, bf16[22,64,256]{2,1,0:T(8,128)(2,1)S(1)}, u32[]{:S(2)}, u32[]{:S(2)}) collective-permute-start(bf16[22,64,256]{2,1,0:T(8,128)(2,1)S(1)} %constant_dynamic-update-slice_fusion.refs_15_.refs_0_), channel_id=1, source_target_pairs={{0,7},{16,23},{1,0},{17,16},{2,1},{18,17},{3,2},{19,18},{4,3},{20,... | collective-permute-start | bytes 2162696 | tf_op jit(solution)/shard_map/ppermute | solution.py:67
  31.9 13.8 %collective-permute-start.1 = (bf16[8,128,256]{2,1,0:T(8,128)(2,1)S(1)}, bf16[8,128,256]{2,1,0:T(8,128)(2,1)S(1)}, u32[]{:S(2)}, u32[]{:S(2)}) collective-permute-start(bf16[8,128,256]{2,1,0:T(8,128)(2,1)S(1)} %all-to-all-done), channel_id=1, source_target_pairs={{0,32},{16,24},{1,33},{17,25},{2,34},{18,26},{3,35},{19,27},{4,36}... | collective-permute-start | bytes 1572872 | tf_op jit(solution)/shard_map/ppermute | solution.py:67
  33.8 12.0 %collective-permute-start.2 = (bf16[8,128,256]{2,1,0:T(8,128)(2,1)S(1)}, bf16[8,128,256]{2,1,0:T(8,128)(2,1)}, u32[]{:S(2)}, u32[]{:S(2)}) collective-permute-start(bf16[8,128,256]{2,1,0:T(8,128)(2,1)S(1)} %all-to-all-done), channel_id=1, source_target_pairs={{0,96},{16,152},{1,97},{17,153},{2,98},{18,154},{3,99},{19,155},{4... | collective-permute-start | bytes 1572872 | tf_op jit(solution)/shard_map/ppermute | solution.py:67
  47.2 21.7 %collective-permute-start.13 = (bf16[2,8,128,256]{3,2,1,0:T(8,128)(2,1)S(1)}, bf16[2,8,128,256]{3,2,1,0:T(8,128)(2,1)S(1)}, u32[]{:S(2)}, u32[]{:S(2)}) collective-permute-start(bf16[2,8,128,256]{3,2,1,0:T(8,128)(2,1)S(1)} %pad_maximum_fusion), channel_id=1, source_target_pairs={{0,8},{16,48},{1,9},{17,49},{2,10},{18,50},{3,11},{19,51},{4,12},{... | collective-permute-start | bytes 3145736 | tf_op jit(solution)/shard_map/ppermute | solution.py:67
  47.8 21.1 %collective-permute-start.14 = (bf16[2,8,128,256]{3,2,1,0:T(8,128)(2,1)S(1)}, bf16[2,8,128,256]{3,2,1,0:T(8,128)(2,1)S(1)}, u32[]{:S(2)}, u32[]{:S(2)}) collective-permute-start(bf16[2,8,128,256]{3,2,1,0:T(8,128)(2,1)S(1)} %pad_maximum_fusion), channel_id=1, source_target_pairs={{0,136},{16,112},{1,137},{17,113},{2,138},{18,114},{3,139},{19,115... | collective-permute-start | bytes 3145736 | tf_op jit(solution)/shard_map/ppermute | solution.py:67
  50.5 15.3 %collective-permute-start.15 = (bf16[22,64,256]{2,1,0:T(8,128)(2,1)S(1)}, bf16[22,64,256]{2,1,0:T(8,128)(2,1)}, u32[]{:S(2)}, u32[]{:S(2)}) collective-permute-start(bf16[22,64,256]{2,1,0:T(8,128)(2,1)S(1)} %collective-permute-done.10.refs_23_.refs_7_), channel_id=1, source_target_pairs={{0,1},{16,17},{1,2},{17,18},{2,3},{18,19},{3,4},{19,20},{4,5},{20,... | collective-permute-start | bytes 2162696 | tf_op jit(solution)/shard_map/ppermute | solution.py:67
  52.5 14.9 %collective-permute-start.16 = (bf16[22,64,256]{2,1,0:T(8,128)(2,1)S(1)}, bf16[22,64,256]{2,1,0:T(8,128)(2,1)}, u32[]{:S(2)}, u32[]{:S(2)}) collective-permute-start(bf16[22,64,256]{2,1,0:T(8,128)(2,1)S(1)} %collective-permute-done.11.refs_16_.refs_1_), channel_id=1, source_target_pairs={{0,7},{16,23},{1,0},{17,16},{2,1},{18,17},{3,2},{19,18},{4,3},{20,... | collective-permute-start | bytes 2162696 | tf_op jit(solution)/shard_map/ppermute | solution.py:67
  52.5 12.5 %collective-permute-start.12 = (bf16[8,128,256]{2,1,0:T(8,128)(2,1)S(1)}, bf16[8,128,256]{2,1,0:T(8,128)(2,1)S(1)}, u32[]{:S(2)}, u32[]{:S(2)}) collective-permute-start(bf16[8,128,256]{2,1,0:T(8,128)(2,1)S(1)} %collective-permute-done.1), channel_id=1, source_target_pairs={{0,32},{16,24},{1,33},{17,25},{2,34},{18,26},{3,35},{19,27},{4,36}... | collective-permute-start | bytes 1572872 | tf_op jit(solution)/shard_map/ppermute | solution.py:67
  68.9 23.9 %collective-permute-start.21 = (bf16[8,24,128,128]{3,2,1,0:T(8,128)(2,1)}, bf16[8,24,128,128]{3,2,1,0:T(8,128)(2,1)}, u32[]{:S(2)}, u32[]{:S(2)}) collective-permute-start(bf16[8,24,128,128]{3,2,1,0:T(8,128)(2,1)} %pick_tiles.1), channel_id=1, source_target_pairs={{0,16},{16,0},{1,17},{17,1},{2,18},{18,2},{3,19},{19,3},{4,20},{20... | collective-permute-start | bytes 18874376 | tf_op jit(solution)/shard_map/ppermute | solution.py:67
  69.1 23.7 %collective-permute-start.17 = (bf16[2,8,128,256]{3,2,1,0:T(8,128)(2,1)S(1)}, bf16[2,8,128,256]{3,2,1,0:T(8,128)(2,1)}, u32[]{:S(2)}, u32[]{:S(2)}) collective-permute-start(bf16[2,8,128,256]{3,2,1,0:T(8,128)(2,1)S(1)} %pad_maximum_fusion.1), channel_id=1, source_target_pairs={{0,8},{16,48},{1,9},{17,49},{2,10},{18,50},{3,11},{19,51},{4,12},{... | collective-permute-start | bytes 3145736 | tf_op jit(solution)/shard_map/ppermute | solution.py:67
  69.2 23.6 %collective-permute-start.18 = (bf16[2,8,128,256]{3,2,1,0:T(8,128)(2,1)S(1)}, bf16[2,8,128,256]{3,2,1,0:T(8,128)(2,1)}, u32[]{:S(2)}, u32[]{:S(2)}) collective-permute-start(bf16[2,8,128,256]{3,2,1,0:T(8,128)(2,1)S(1)} %pad_maximum_fusion.1), channel_id=1, source_target_pairs={{0,136},{16,112},{1,137},{17,113},{2,138},{18,114},{3,139},{19,115... | collective-permute-start | bytes 3145736 | tf_op jit(solution)/shard_map/ppermute | solution.py:67
  72.4 18.2 %collective-permute-start.19 = (bf16[22,64,256]{2,1,0:T(8,128)(2,1)}, bf16[22,64,256]{2,1,0:T(8,128)(2,1)S(1)}, u32[]{:S(2)}, u32[]{:S(2)}) collective-permute-start(bf16[22,64,256]{2,1,0:T(8,128)(2,1)} %collective-permute-done.15.refs_22_.refs_6_), channel_id=1, source_target_pairs={{0,1},{16,17},{1,2},{17,18},{2,3},{18,19},{3,4},{19,20},{4,5},{20,... | collective-permute-start | bytes 2162696 | tf_op jit(solution)/shard_map/ppermute | solution.py:67
  74.5 18.3 %collective-permute-start.20 = (bf16[22,64,256]{2,1,0:T(8,128)(2,1)}, bf16[22,64,256]{2,1,0:T(8,128)(2,1)S(1)}, u32[]{:S(2)}, u32[]{:S(2)}) collective-permute-start(bf16[22,64,256]{2,1,0:T(8,128)(2,1)} %collective-permute-done.16.refs_17_.refs_2_), channel_id=1, source_target_pairs={{0,7},{16,23},{1,0},{17,16},{2,1},{18,17},{3,2},{19,18},{4,3},{20,... | collective-permute-start | bytes 2162696 | tf_op jit(solution)/shard_map/ppermute | solution.py:67
  90.6 6.7 %collective-permute-start = (s32[8,24]{1,0:T(8,128)S(1)}, s32[8,24]{1,0:T(8,128)S(1)}, u32[]{:S(2)}, u32[]{:S(2)}) collective-permute-start(s32[8,24]{1,0:T(8,128)S(1)} %bitcast.64), channel_id=1, source_target_pairs={{0,16},{16,0},{1,17},{17,1},{2,18},{18,2},{3,19},{19,3},{4,20},{20... | collective-permute-start | bytes 2312 | tf_op jit(solution)/shard_map/ppermute | solution.py:67
  92.8 16.3 %collective-permute-start.22 = (bf16[2,8,128,256]{3,2,1,0:T(8,128)(2,1)}, bf16[2,8,128,256]{3,2,1,0:T(8,128)(2,1)}, u32[]{:S(2)}, u32[]{:S(2)}) collective-permute-start(bf16[2,8,128,256]{3,2,1,0:T(8,128)(2,1)} %copy-done.11), channel_id=1, source_target_pairs={{0,8},{16,48},{1,9},{17,49},{2,10},{18,50},{3,11},{19,51},{4,12},{... | collective-permute-start | bytes 3145736 | tf_op jit(solution)/shard_map/ppermute | solution.py:67
  92.8 16.3 %collective-permute-start.23 = (bf16[2,8,128,256]{3,2,1,0:T(8,128)(2,1)}, bf16[2,8,128,256]{3,2,1,0:T(8,128)(2,1)}, u32[]{:S(2)}, u32[]{:S(2)}) collective-permute-start(bf16[2,8,128,256]{3,2,1,0:T(8,128)(2,1)} %collective-permute-done.18), channel_id=1, source_target_pairs={{0,136},{16,112},{1,137},{17,113},{2,138},{18,114},{3,139},{19,115... | collective-permute-start | bytes 3145736 | tf_op jit(solution)/shard_map/ppermute | solution.py:67
  98.2 10.9 %collective-permute-start.24 = (bf16[11,64,256]{2,1,0:T(8,128)(2,1)S(1)}, bf16[11,64,256]{2,1,0:T(8,128)(2,1)S(1)}, u32[]{:S(2)}, u32[]{:S(2)}) collective-permute-start(bf16[11,64,256]{2,1,0:T(8,128)(2,1)S(1)} %slice.6), channel_id=1, source_target_pairs={{0,1},{16,17},{1,2},{17,18},{2,3},{18,19},{3,4},{19,20},{4,5},{20,... | collective-permute-start | bytes 1081352 | tf_op jit(solution)/shard_map/ppermute | solution.py:67
  100.0 9.1 %collective-permute-start.25 = (bf16[11,64,256]{2,1,0:T(8,128)(2,1)S(1)}, bf16[11,64,256]{2,1,0:T(8,128)(2,1)S(1)}, u32[]{:S(2)}, u32[]{:S(2)}) collective-permute-start(bf16[11,64,256]{2,1,0:T(8,128)(2,1)S(1)} %slice.7), channel_id=1, source_target_pairs={{0,7},{16,23},{1,0},{17,16},{2,1},{18,17},{3,2},{19,18},{4,3},{20,... | collective-permute-start | bytes 1081352 | tf_op jit(solution)/shard_map/ppermute | solution.py:67
  135.1 25.2 %collective-permute-start.27 = (bf16[8,192,256]{2,1,0:T(8,128)(2,1)S(1)}, bf16[8,192,256]{2,1,0:T(8,128)(2,1)S(1)}, u32[]{:S(2)}, u32[]{:S(2)}) collective-permute-start(bf16[8,192,256]{2,1,0:T(8,128)(2,1)S(1)} %dynamic-slice_bitcast_fusion), channel_id=1, source_target_pairs={{0,8},{16,24},{1,9},{17,25},{2,10},{18,26},{3,11},{19,27},{4,12},{... | collective-permute-start | bytes 2359304 | tf_op jit(solution)/shard_map/ppermute | solution.py:67
  143.0 17.2 %all-to-all-start.1 = ((f32[16,16,256]{2,1,0:T(8,128)}), f32[16,16,256]{2,1,0:T(8,128)S(1)}, u32[]{:S(2)}, u32[]{:S(2)}) async-start(f32[16,16,256]{2,1,0:T(8,128)} %bitcast.50), calls=%async_computation.1 | async-start | bytes 524288 | tf_op jit(solution)/shard_map/all_to_all | solution.py:355
  162.5 25.0 %all-to-all-start.2 = ((bf16[8,192,256]{2,1,0:T(8,128)(2,1)}), bf16[8,192,256]{2,1,0:T(8,128)(2,1)S(1)}, u32[]{:S(2)}, u32[]{:S(2)}) async-start(bf16[8,192,256]{2,1,0:T(8,128)(2,1)} %fusion), calls=%async_computation.2 | async-start | bytes 1572864 | tf_op jit(solution)/shard_map/all_to_all | solution.py:358
  168.1 5.2 %collective-permute-start.29 = (f32[16,256]{1,0:T(8,128)S(1)}, f32[16,256]{1,0:T(8,128)S(1)}, u32[]{:S(2)}, u32[]{:S(2)}) collective-permute-start(f32[16,256]{1,0:T(8,128)S(1)} %add.256), channel_id=1, source_target_pairs={{0,128},{16,144},{1,129},{17,145},{2,130},{18,146},{3,131},{19,147... | collective-permute-start | bytes 49160 | tf_op jit(solution)/shard_map/ppermute | solution.py:67
  188.3 14.3 %all-to-all-start.3 = ((f32[16,16,256]{2,1,0:T(8,128)}), f32[16,16,256]{2,1,0:T(8,128)S(1)}, u32[]{:S(2)}, u32[]{:S(2)}) async-start(f32[16,16,256]{2,1,0:T(8,128)} %bitcast.32), calls=%async_computation.3 | async-start | bytes 524288 | tf_op jit(solution)/shard_map/all_to_all | solution.py:363
  (20 other events, 399.4 us)

commit v8 on v7

--- a/solution.py
+++ b/solution.py
@@ -161,12 +161,12 @@
 
 
 def features_kernel(here, turned, partial, gradient):
-    @pl.when(pl.program_id(0) == 0)
-    def _():
-        gradient[...] = jnp.zeros_like(gradient)
-
-    rows = jnp.concatenate([partial[here[1], 0], partial[1 - here[1], 0]], axis=0)
-    gradient[...] += jnp.dot(turned[0], rows, preferred_element_type=jnp.float32)
+    total = jnp.zeros(gradient.shape, jnp.float32)
+    for place in range(NZ):
+        ahead = lax.rem(place - here[2] + NZ, NZ)
+        rows = jnp.concatenate([partial[here[1], place], partial[1 - here[1], place]], axis=0)
+        total += jnp.dot(turned[ahead], rows, preferred_element_type=jnp.float32)
+    gradient[...] = total
 
 
 def features_product(partial, turned, here):
@@ -176,14 +176,11 @@
         out_shape=jax.ShapeDtypeStruct((width, width), jnp.float32),
         grid_spec=pltpu.PrefetchScalarGridSpec(
             num_scalar_prefetch=1,
-            grid=(NZ,),
-            in_specs=[
-                pl.BlockSpec((1, width, 384), lambda d, here: (lax.rem(d - here[2] + NZ, NZ), 0, 0)),
-                pl.BlockSpec((2, 1, 192, width), lambda d, here: (0, d, 0, 0)),
-            ],
-            out_specs=pl.BlockSpec((width, width), lambda d, here: (0, 0)),
-        ),
-        compiler_params=pltpu.CompilerParams(vmem_limit_bytes=56 << 20),
+            grid=(),
+            in_specs=[pl.BlockSpec(memory_space=pltpu.VMEM)] * 2,
+            out_specs=pl.BlockSpec(memory_space=pltpu.VMEM),
+        ),
+        compiler_params=pltpu.CompilerParams(vmem_limit_bytes=24 << 20),
         cost_estimate=pl.CostEstimate(flops=2 * 3072 * width * width, bytes_accessed=4 << 20, transcendentals=0),
         name="features_product",
     )(here, turned, partial)

time: 204 us -> 204 us (level)
  waiting for transfers between devices: 88.4 us -> 93.7 us
  Pallas kernels: 36.4 us -> 31.3 us
    pallas_call x1, Pallas kernels: 6.89 us -> 1.94 us  [features_product(): pl.pallas_call(features_kernel, out_shape=jax.ShapeDtypeStruct((width, wi...]
    all_to_all x1, waiting for transfers between devices: 10.1 us -> 12.5 us  [body(): lax.all_to_all(local_weight, 'rep', 0, 0, tiled=True).reshape(16, 16, width)]
    all_to_all x1, starting transfers between devices: 4.38 us -> 6.63 us  [body(): lax.all_to_all(line, BOTH, 0, 0, axis_index_groups=z_lines(), tiled=True)]
  transfers between devices with their start and end apart: 36 -> 36, of which waited for: 21 -> 21; matrix products, arithmetic and copies ran while one was open for 3% -> 3% of each run, Pallas kernels for 8% -> 5%
where the time goes in v8:
time: 204 us; the launch traced here: 203 us
  waiting for transfers between devices  93.7 us (46%)
  starting transfers between devices  63.3 us (31%)
  Pallas kernels  31.3 us (15%)
  other arithmetic  7.1 us (3%)
  local copies, waits for them, and re-layouts  5.8 us (3%)
    ppermute x32, waiting for transfers between devices, send(): return lax.ppermute(value, BOTH, moves)  65.4 us
    ppermute x32, starting transfers between devices, send(): return lax.ppermute(value, BOTH, moves)  36.5 us
    pallas_call x1, Pallas kernels, products(): pl.pallas_call(lambda *refs: products_kernel(places, *refs), out_shape=(j...  20.6 us
    all_to_all x1, waiting for transfers between devices, body(): lax.all_to_all(local_weight, 'rep', 0, 0, tiled=True).reshape(16, 16, width)  12.5 us
    all_to_all x1, waiting for transfers between devices, body(): weight_grad = lax.all_to_all(spread, 'rep', 0, 0, tiled=True)  9.59 us
    all_to_all x1, starting transfers between devices, spread_over(): lax.all_to_all(copies, BOTH, 0, 0, axis_index_groups=places, tiled=True)  8.57 us
    all_to_all x1, starting transfers between devices, body(): lax.all_to_all(local_weight, 'rep', 0, 0, tiled=True).reshape(16, 16, width)  6.74 us
    all_to_all x1, starting transfers between devices, body(): lax.all_to_all(line, BOTH, 0, 0, axis_index_groups=z_lines(), tiled=True)  6.63 us
  transfers between devices with their start and end apart: 36, of which 21 were waited for; matrix products, arithmetic and copies ran while one was open for 3% of the time, Pallas kernels for 5%

profile of v8, /device:TPU:32, one launch (start us, length us, event | category | flops | bytes accessed | tf_op | source)
XLA Modules:
  0.0 203.1 jit_solution(12870778277110143064)
XLA Ops:
  2.5 2.8 %collective-permute-start.3 = (bf16[64,256]{1,0:T(8,128)(2,1)S(1)}, bf16[64,256]{1,0:T(8,128)(2,1)S(1)}, u32[]{:S(2)}, u32[]{:S(2)}) collective-permute-start(bf16[64,256]{1,0:T(8,128)(2,1)S(1)} %get-tuple-element.51), channel_id=1, source_target_pairs={{0,136},{16,112},{1,137},{17,113},{2,138},{18,114},{3,139},{19,115... | collective-permute-start | bytes 98312 | tf_op jit(solution)/shard_map/ppermute | solution.py:67
  7.9 8.6 %all-to-all-start = ((bf16[8,128,256]{2,1,0:T(8,128)(2,1)}), bf16[8,128,256]{2,1,0:T(8,128)(2,1)S(1)}, u32[]{:S(2)}, u32[]{:S(2)}) async-start(bf16[8,128,256]{2,1,0:T(8,128)(2,1)} %broadcast_in_dim.42), calls=%async_computation | async-start | bytes 1048576 | tf_op jit(solution)/shard_map/all_to_all | solution.py:43
  16.4 1.8 collective-permute-start.9
  18.3 3.1 %collective-permute-start.6 = (bf16[4,64,256]{2,1,0:T(8,128)(2,1)S(1)}, bf16[4,64,256]{2,1,0:T(8,128)(2,1)S(1)}, u32[]{:S(2)}, u32[]{:S(2)}) collective-permute-start(bf16[4,64,256]{2,1,0:T(8,128)(2,1)S(1)} %pad_maximum_fusion.2), channel_id=1, source_target_pairs={{0,96},{16,152},{1,97},{17,153},{2,98},{18,154},{3,99},{19,155},{4... | collective-permute-start | bytes 393224 | tf_op jit(solution)/shard_map/ppermute | solution.py:67
  23.0 2.3 %collective-permute-done.6 = bf16[4,64,256]{2,1,0:T(8,128)(2,1)S(1)} collective-permute-done((bf16[4,64,256]{2,1,0:T(8,128)(2,1)S(1)}, bf16[4,64,256]{2,1,0:T(8,128)(2,1)S(1)}, u32[]{:S(2)}, u32[]{:S(2)}) %collective-permute-start.6) | collective-permute-done | bytes 131104 | tf_op jit(solution)/shard_map/ppermute | solution.py:67
  25.3 2.6 %collective-permute-done.7 = bf16[4,64,256]{2,1,0:T(8,128)(2,1)S(1)} collective-permute-done((bf16[4,64,256]{2,1,0:T(8,128)(2,1)S(1)}, bf16[4,64,256]{2,1,0:T(8,128)(2,1)S(1)}, u32[]{:S(2)}, u32[]{:S(2)}) %collective-permute-start.7) | collective-permute-done | bytes 131104 | tf_op jit(solution)/shard_map/ppermute | solution.py:67
  31.9 1.9 collective-permute-start.1
  35.2 9.3 %collective-permute-done.10.refs_23_.refs_7_ = bf16[22,64,256]{2,1,0:T(8,128)(2,1)S(1)} collective-permute-done((bf16[22,64,256]{2,1,0:T(8,128)(2,1)S(1)}, bf16[22,64,256]{2,1,0:T(8,128)(2,1)S(1)}, u32[]{:S(2)}, u32[]{:S(2)}) %collective-permute-start.10) | collective-permute-done | bytes 720928 | tf_op jit(solution)/shard_map/ppermute | solution.py:67
  47.8 2.7 %collective-permute-start.14 = (bf16[2,8,128,256]{3,2,1,0:T(8,128)(2,1)S(1)}, bf16[2,8,128,256]{3,2,1,0:T(8,128)(2,1)S(1)}, u32[]{:S(2)}, u32[]{:S(2)}) collective-permute-start(bf16[2,8,128,256]{3,2,1,0:T(8,128)(2,1)S(1)} %pad_maximum_fusion), channel_id=1, source_target_pairs={{0,136},{16,112},{1,137},{17,113},{2,138},{18,114},{3,139},{19,115... | collective-permute-start | bytes 3145736 | tf_op jit(solution)/shard_map/ppermute | solution.py:67
  50.5 2.0 %collective-permute-start.15 = (bf16[22,64,256]{2,1,0:T(8,128)(2,1)S(1)}, bf16[22,64,256]{2,1,0:T(8,128)(2,1)}, u32[]{:S(2)}, u32[]{:S(2)}) collective-permute-start(bf16[22,64,256]{2,1,0:T(8,128)(2,1)S(1)} %collective-permute-done.10.refs_23_.refs_7_), channel_id=1, source_target_pairs={{0,1},{16,17},{1,2},{17,18},{2,3},{18,19},{3,4},{19,20},{4,5},{20,... | collective-permute-start | bytes 2162696 | tf_op jit(solution)/shard_map/ppermute | solution.py:67
  52.6 1.9 collective-permute-start.12
  54.4 5.6 %pick_tiles.1 = bf16[8,24,128,128]{3,2,1,0:T(8,128)(2,1)} custom-call(s32[1]{0:T(128)} %bitcast.16.side, bf16[8,2,24,128,128]{4,3,2,1,0:T(8,128)(2,1)} %bitcast.45), custom_call_target="tpu_custom_call" | custom-call | bytes 12582912 | tf_op jit(solution)/shard_map/pick_tiles/pallas_call | solution.py:204
  60.1 5.0 %collective-permute-done.12 = bf16[8,128,256]{2,1,0:T(8,128)(2,1)S(1)} collective-permute-done((bf16[8,128,256]{2,1,0:T(8,128)(2,1)S(1)}, bf16[8,128,256]{2,1,0:T(8,128)(2,1)S(1)}, u32[]{:S(2)}, u32[]{:S(2)}) %collective-permute-start.12) | collective-permute-done | bytes 524320 | tf_op jit(solution)/shard_map/ppermute | solution.py:67
  69.2 3.2 %collective-permute-start.18 = (bf16[2,8,128,256]{3,2,1,0:T(8,128)(2,1)S(1)}, bf16[2,8,128,256]{3,2,1,0:T(8,128)(2,1)}, u32[]{:S(2)}, u32[]{:S(2)}) collective-permute-start(bf16[2,8,128,256]{3,2,1,0:T(8,128)(2,1)S(1)} %pad_maximum_fusion.1), channel_id=1, source_target_pairs={{0,136},{16,112},{1,137},{17,113},{2,138},{18,114},{3,139},{19,115... | collective-permute-start | bytes 3145736 | tf_op jit(solution)/shard_map/ppermute | solution.py:67
  72.4 2.0 %collective-permute-start.19 = (bf16[22,64,256]{2,1,0:T(8,128)(2,1)}, bf16[22,64,256]{2,1,0:T(8,128)(2,1)S(1)}, u32[]{:S(2)}, u32[]{:S(2)}) collective-permute-start(bf16[22,64,256]{2,1,0:T(8,128)(2,1)} %collective-permute-done.15.refs_22_.refs_6_), channel_id=1, source_target_pairs={{0,1},{16,17},{1,2},{17,18},{2,3},{18,19},{3,4},{19,20},{4,5},{20,... | collective-permute-start | bytes 2162696 | tf_op jit(solution)/shard_map/ppermute | solution.py:67
  74.6 16.0 %collective-permute-done.19.refs_21_.refs_5_ = bf16[22,64,256]{2,1,0:T(8,128)(2,1)S(1)} collective-permute-done((bf16[22,64,256]{2,1,0:T(8,128)(2,1)}, bf16[22,64,256]{2,1,0:T(8,128)(2,1)S(1)}, u32[]{:S(2)}, u32[]{:S(2)}) %collective-permute-start.19) | collective-permute-done | bytes 720928 | tf_op jit(solution)/shard_map/ppermute | solution.py:67
  90.6 2.2 %collective-permute-done.20.refs_18_.refs_3_ = bf16[22,64,256]{2,1,0:T(8,128)(2,1)S(1)} collective-permute-done((bf16[22,64,256]{2,1,0:T(8,128)(2,1)}, bf16[22,64,256]{2,1,0:T(8,128)(2,1)S(1)}, u32[]{:S(2)}, u32[]{:S(2)}) %collective-permute-start.20) | collective-permute-done | bytes 720928 | tf_op jit(solution)/shard_map/ppermute | solution.py:67
  92.8 3.3 %collective-permute-start.23 = (bf16[2,8,128,256]{3,2,1,0:T(8,128)(2,1)}, bf16[2,8,128,256]{3,2,1,0:T(8,128)(2,1)}, u32[]{:S(2)}, u32[]{:S(2)}) collective-permute-start(bf16[2,8,128,256]{3,2,1,0:T(8,128)(2,1)} %collective-permute-done.18), channel_id=1, source_target_pairs={{0,136},{16,112},{1,137},{17,113},{2,138},{18,114},{3,139},{19,115... | collective-permute-start | bytes 3145736 | tf_op jit(solution)/shard_map/ppermute | solution.py:67
  98.2 1.8 collective-permute-start.24
  101.6 7.5 %collective-permute-done.22 = bf16[2,8,128,256]{3,2,1,0:T(8,128)(2,1)} collective-permute-done((bf16[2,8,128,256]{3,2,1,0:T(8,128)(2,1)}, bf16[2,8,128,256]{3,2,1,0:T(8,128)(2,1)}, u32[]{:S(2)}, u32[]{:S(2)}) %collective-permute-start.22) | collective-permute-done | bytes 1048608 | tf_op jit(solution)/shard_map/ppermute | solution.py:67
  110.0 20.6 %tile_products.1 = (f32[24,128,256]{2,1,0:T(8,128)}, bf16[24,128,256]{2,1,0:T(8,128)(2,1)}) custom-call(s32[16]{0:T(128)} %min.8.refs_0_, s32[384]{0:T(512)} %fusion.9.refs_1_, s32[384]{0:T(512)} %get-tuple-element.52.refs_2_, s32[384]{0:T(512)} %get-tuple-element.59.refs_3_, s32[3]{0:T(128)} %pad_add_fusion.1.refs_4_.here, ...), custom_call_target="tpu_custom_call" | custom-call | flops 3221225472 | bytes 31457280 | tf_op jit(solution)/shard_map/tile_products/pallas_call | solution.py:227
  130.8 3.2 %turn_features.1.turned = bf16[8,256,384]{2,1,0:T(8,128)(2,1)} custom-call(bf16[22,64,256]{2,1,0:T(8,128)(2,1)} %copy-done.8, bf16[22,64,256]{2,1,0:T(8,128)(2,1)} %copy-done.10, bf16[22,64,256]{2,1,0:T(8,128)(2,1)} %collective-permute-done.16.refs_17_.refs_2_, bf16[22,64,256]{2,1,0:T(8,128)(2,1)} %copy-done.4, bf16[11,64,256]{2,1,0:T(8,128)(2,1)} %copy-done.11, ...), custom_call_target="tpu_custom_call" | custom-call | bytes 4194304 | tf_op jit(solution)/shard_map/turn_features/pallas_call | solution.py:147
  136.3 1.9 features_product.1
  138.2 6.7 %all-to-all-start.1 = ((f32[16,16,256]{2,1,0:T(8,128)}), f32[16,16,256]{2,1,0:T(8,128)S(1)}, u32[]{:S(2)}, u32[]{:S(2)}) async-start(f32[16,16,256]{2,1,0:T(8,128)} %bitcast.30), calls=%async_computation.1 | async-start | bytes 524288 | tf_op jit(solution)/shard_map/all_to_all | solution.py:352
  144.9 12.5 %all-to-all-done.1 = f32[16,16,256]{2,1,0:T(8,128)S(1)} async-done(((f32[16,16,256]{2,1,0:T(8,128)}), f32[16,16,256]{2,1,0:T(8,128)S(1)}, u32[]{:S(2)}, u32[]{:S(2)}) %all-to-all-start.1) | async-done | bytes 262176 | tf_op jit(solution)/shard_map/all_to_all | solution.py:352
  158.6 6.6 %all-to-all-start.2 = ((bf16[8,192,256]{2,1,0:T(8,128)(2,1)}), bf16[8,192,256]{2,1,0:T(8,128)(2,1)S(1)}, u32[]{:S(2)}, u32[]{:S(2)}) async-start(bf16[8,192,256]{2,1,0:T(8,128)(2,1)} %fusion), calls=%async_computation.2 | async-start | bytes 1572864 | tf_op jit(solution)/shard_map/all_to_all | solution.py:355
  167.8 3.8 %collective-permute-done.29 = f32[16,256]{1,0:T(8,128)S(1)} collective-permute-done((f32[16,256]{1,0:T(8,128)S(1)}, f32[16,256]{1,0:T(8,128)S(1)}, u32[]{:S(2)}, u32[]{:S(2)}) %collective-permute-start.29) | collective-permute-done | bytes 16416 | tf_op jit(solution)/shard_map/ppermute | solution.py:67
  171.6 3.7 %collective-permute-done.30 = f32[16,256]{1,0:T(8,128)S(1)} collective-permute-done((f32[16,256]{1,0:T(8,128)S(1)}, f32[16,256]{1,0:T(8,128)S(1)}, u32[]{:S(2)}, u32[]{:S(2)}) %collective-permute-start.30) | collective-permute-done | bytes 16416 | tf_op jit(solution)/shard_map/ppermute | solution.py:67
  175.7 4.9 %collective-permute-done.31 = f32[16,256]{1,0:T(8,128)S(1)} collective-permute-done((f32[16,256]{1,0:T(8,128)S(1)}, f32[16,256]{1,0:T(8,128)S(1)}, u32[]{:S(2)}, u32[]{:S(2)}) %collective-permute-start.31) | collective-permute-done | bytes 16416 | tf_op jit(solution)/shard_map/ppermute | solution.py:67
  180.6 5.7 %all-to-all-done.2 = bf16[8,192,256]{2,1,0:T(8,128)(2,1)S(1)} async-done(((bf16[8,192,256]{2,1,0:T(8,128)(2,1)}), bf16[8,192,256]{2,1,0:T(8,128)(2,1)S(1)}, u32[]{:S(2)}, u32[]{:S(2)}) %all-to-all-start.2) | async-done | bytes 786464 | tf_op jit(solution)/shard_map/all_to_all | solution.py:355
  187.1 4.8 %all-to-all-start.3 = ((f32[16,16,256]{2,1,0:T(8,128)}), f32[16,16,256]{2,1,0:T(8,128)S(1)}, u32[]{:S(2)}, u32[]{:S(2)}) async-start(f32[16,16,256]{2,1,0:T(8,128)} %bitcast.32), calls=%async_computation.3 | async-start | bytes 524288 | tf_op jit(solution)/shard_map/all_to_all | solution.py:360
  192.8 9.6 %all-to-all-done.3 = f32[16,16,256]{2,1,0:T(8,128)S(1)} async-done(((f32[16,16,256]{2,1,0:T(8,128)}), f32[16,16,256]{2,1,0:T(8,128)S(1)}, u32[]{:S(2)}, u32[]{:S(2)}) %all-to-all-start.3) | async-done | bytes 262176 | tf_op jit(solution)/shard_map/all_to_all | solution.py:360
  (130 shorter events, 32.3 us)
Async XLA Ops:
  2.5 15.7 %collective-permute-start.3 = (bf16[64,256]{1,0:T(8,128)(2,1)S(1)}, bf16[64,256]{1,0:T(8,128)(2,1)S(1)}, u32[]{:S(2)}, u32[]{:S(2)}) collective-permute-start(bf16[64,256]{1,0:T(8,128)(2,1)S(1)} %get-tuple-element.51), channel_id=1, source_target_pairs={{0,136},{16,112},{1,137},{17,113},{2,138},{18,114},{3,139},{19,115... | collective-permute-start | bytes 98312 | tf_op jit(solution)/shard_map/ppermute | solution.py:67
  5.3 12.9 %collective-permute-start.4 = (bf16[64,256]{1,0:T(8,128)(2,1)S(1)}, bf16[64,256]{1,0:T(8,128)(2,1)S(1)}, u32[]{:S(2)}, u32[]{:S(2)}) collective-permute-start(bf16[64,256]{1,0:T(8,128)(2,1)S(1)} %get-tuple-element.51), channel_id=1, source_target_pairs={{0,128},{16,80},{1,129},{17,81},{2,130},{18,82},{3,131},{19,83},{4... | collective-permute-start | bytes 98312 | tf_op jit(solution)/shard_map/ppermute | solution.py:67
  6.1 12.1 %collective-permute-start.5 = (bf16[64,256]{1,0:T(8,128)(2,1)S(1)}, bf16[64,256]{1,0:T(8,128)(2,1)S(1)}, u32[]{:S(2)}, u32[]{:S(2)}) collective-permute-start(bf16[64,256]{1,0:T(8,128)(2,1)S(1)} %get-tuple-element.51), channel_id=1, source_target_pairs={{0,8},{16,48},{1,9},{17,49},{2,10},{18,50},{3,11},{19,51},{4,12},{... | collective-permute-start | bytes 98312 | tf_op jit(solution)/shard_map/ppermute | solution.py:67
  7.9 24.1 %all-to-all-start = ((bf16[8,128,256]{2,1,0:T(8,128)(2,1)}), bf16[8,128,256]{2,1,0:T(8,128)(2,1)S(1)}, u32[]{:S(2)}, u32[]{:S(2)}) async-start(bf16[8,128,256]{2,1,0:T(8,128)(2,1)} %broadcast_in_dim.42), calls=%async_computation | async-start | bytes 1048576 | tf_op jit(solution)/shard_map/all_to_all | solution.py:43
  16.4 12.8 %collective-permute-start.9 = (bf16[192,256]{1,0:T(8,128)(2,1)S(1)}, bf16[192,256]{1,0:T(8,128)(2,1)S(1)}, u32[]{:S(2)}, u32[]{:S(2)}) collective-permute-start(bf16[192,256]{1,0:T(8,128)(2,1)S(1)} %get-tuple-element.60), channel_id=1, source_target_pairs={{0,8},{16,24},{1,9},{17,25},{2,10},{18,26},{3,11},{19,27},{4,12},{... | collective-permute-start | bytes 294920 | tf_op jit(solution)/shard_map/ppermute | solution.py:67
  18.3 7.0 %collective-permute-start.6 = (bf16[4,64,256]{2,1,0:T(8,128)(2,1)S(1)}, bf16[4,64,256]{2,1,0:T(8,128)(2,1)S(1)}, u32[]{:S(2)}, u32[]{:S(2)}) collective-permute-start(bf16[4,64,256]{2,1,0:T(8,128)(2,1)S(1)} %pad_maximum_fusion.2), channel_id=1, source_target_pairs={{0,96},{16,152},{1,97},{17,153},{2,98},{18,154},{3,99},{19,155},{4... | collective-permute-start | bytes 393224 | tf_op jit(solution)/shard_map/ppermute | solution.py:67
  21.4 6.6 %collective-permute-start.7 = (bf16[4,64,256]{2,1,0:T(8,128)(2,1)S(1)}, bf16[4,64,256]{2,1,0:T(8,128)(2,1)S(1)}, u32[]{:S(2)}, u32[]{:S(2)}) collective-permute-start(bf16[4,64,256]{2,1,0:T(8,128)(2,1)S(1)} %pad_maximum_fusion.2), channel_id=1, source_target_pairs={{0,64},{16,144},{1,65},{17,145},{2,66},{18,146},{3,67},{19,147},{4... | collective-permute-start | bytes 393224 | tf_op jit(solution)/shard_map/ppermute | solution.py:67
  22.0 7.2 %collective-permute-start.8 = (bf16[4,64,256]{2,1,0:T(8,128)(2,1)S(1)}, bf16[4,64,256]{2,1,0:T(8,128)(2,1)S(1)}, u32[]{:S(2)}, u32[]{:S(2)}) collective-permute-start(bf16[4,64,256]{2,1,0:T(8,128)(2,1)S(1)} %pad_maximum_fusion.2), channel_id=1, source_target_pairs={{0,32},{16,24},{1,33},{17,25},{2,34},{18,26},{3,35},{19,27},{4,36}... | collective-permute-start | bytes 393224 | tf_op jit(solution)/shard_map/ppermute | solution.py:67
  29.3 15.1 %collective-permute-start.10 = (bf16[22,64,256]{2,1,0:T(8,128)(2,1)S(1)}, bf16[22,64,256]{2,1,0:T(8,128)(2,1)S(1)}, u32[]{:S(2)}, u32[]{:S(2)}) collective-permute-start(bf16[22,64,256]{2,1,0:T(8,128)(2,1)S(1)} %constant_dynamic-update-slice_fusion.refs_15_.refs_0_), channel_id=1, source_target_pairs={{0,1},{16,17},{1,2},{17,18},{2,3},{18,19},{3,4},{19,20},{4,5},{20,... | collective-permute-start | bytes 2162696 | tf_op jit(solution)/shard_map/ppermute | solution.py:67
  30.9 14.9 %collective-permute-start.11 = (bf16[22,64,256]{2,1,0:T(8,128)(2,1)S(1)}, bf16[22,64,256]{2,1,0:T(8,128)(2,1)S(1)}, u32[]{:S(2)}, u32[]{:S(2)}) collective-permute-start(bf16[22,64,256]{2,1,0:T(8,128)(2,1)S(1)} %constant_dynamic-update-slice_fusion.refs_15_.refs_0_), channel_id=1, source_target_pairs={{0,7},{16,23},{1,0},{17,16},{2,1},{18,17},{3,2},{19,18},{4,3},{20,... | collective-permute-start | bytes 2162696 | tf_op jit(solution)/shard_map/ppermute | solution.py:67
  31.9 13.8 %collective-permute-start.1 = (bf16[8,128,256]{2,1,0:T(8,128)(2,1)S(1)}, bf16[8,128,256]{2,1,0:T(8,128)(2,1)S(1)}, u32[]{:S(2)}, u32[]{:S(2)}) collective-permute-start(bf16[8,128,256]{2,1,0:T(8,128)(2,1)S(1)} %all-to-all-done), channel_id=1, source_target_pairs={{0,32},{16,24},{1,33},{17,25},{2,34},{18,26},{3,35},{19,27},{4,36}... | collective-permute-start | bytes 1572872 | tf_op jit(solution)/shard_map/ppermute | solution.py:67
  33.8 12.0 %collective-permute-start.2 = (bf16[8,128,256]{2,1,0:T(8,128)(2,1)S(1)}, bf16[8,128,256]{2,1,0:T(8,128)(2,1)}, u32[]{:S(2)}, u32[]{:S(2)}) collective-permute-start(bf16[8,128,256]{2,1,0:T(8,128)(2,1)S(1)} %all-to-all-done), channel_id=1, source_target_pairs={{0,96},{16,152},{1,97},{17,153},{2,98},{18,154},{3,99},{19,155},{4... | collective-permute-start | bytes 1572872 | tf_op jit(solution)/shard_map/ppermute | solution.py:67
  47.2 21.7 %collective-permute-start.13 = (bf16[2,8,128,256]{3,2,1,0:T(8,128)(2,1)S(1)}, bf16[2,8,128,256]{3,2,1,0:T(8,128)(2,1)S(1)}, u32[]{:S(2)}, u32[]{:S(2)}) collective-permute-start(bf16[2,8,128,256]{3,2,1,0:T(8,128)(2,1)S(1)} %pad_maximum_fusion), channel_id=1, source_target_pairs={{0,8},{16,48},{1,9},{17,49},{2,10},{18,50},{3,11},{19,51},{4,12},{... | collective-permute-start | bytes 3145736 | tf_op jit(solution)/shard_map/ppermute | solution.py:67
  47.8 21.1 %collective-permute-start.14 = (bf16[2,8,128,256]{3,2,1,0:T(8,128)(2,1)S(1)}, bf16[2,8,128,256]{3,2,1,0:T(8,128)(2,1)S(1)}, u32[]{:S(2)}, u32[]{:S(2)}) collective-permute-start(bf16[2,8,128,256]{3,2,1,0:T(8,128)(2,1)S(1)} %pad_maximum_fusion), channel_id=1, source_target_pairs={{0,136},{16,112},{1,137},{17,113},{2,138},{18,114},{3,139},{19,115... | collective-permute-start | bytes 3145736 | tf_op jit(solution)/shard_map/ppermute | solution.py:67
  50.5 15.3 %collective-permute-start.15 = (bf16[22,64,256]{2,1,0:T(8,128)(2,1)S(1)}, bf16[22,64,256]{2,1,0:T(8,128)(2,1)}, u32[]{:S(2)}, u32[]{:S(2)}) collective-permute-start(bf16[22,64,256]{2,1,0:T(8,128)(2,1)S(1)} %collective-permute-done.10.refs_23_.refs_7_), channel_id=1, source_target_pairs={{0,1},{16,17},{1,2},{17,18},{2,3},{18,19},{3,4},{19,20},{4,5},{20,... | collective-permute-start | bytes 2162696 | tf_op jit(solution)/shard_map/ppermute | solution.py:67
  52.6 14.9 %collective-permute-start.16 = (bf16[22,64,256]{2,1,0:T(8,128)(2,1)S(1)}, bf16[22,64,256]{2,1,0:T(8,128)(2,1)}, u32[]{:S(2)}, u32[]{:S(2)}) collective-permute-start(bf16[22,64,256]{2,1,0:T(8,128)(2,1)S(1)} %collective-permute-done.11.refs_16_.refs_1_), channel_id=1, source_target_pairs={{0,7},{16,23},{1,0},{17,16},{2,1},{18,17},{3,2},{19,18},{4,3},{20,... | collective-permute-start | bytes 2162696 | tf_op jit(solution)/shard_map/ppermute | solution.py:67
  52.6 12.5 %collective-permute-start.12 = (bf16[8,128,256]{2,1,0:T(8,128)(2,1)S(1)}, bf16[8,128,256]{2,1,0:T(8,128)(2,1)S(1)}, u32[]{:S(2)}, u32[]{:S(2)}) collective-permute-start(bf16[8,128,256]{2,1,0:T(8,128)(2,1)S(1)} %collective-permute-done.1), channel_id=1, source_target_pairs={{0,32},{16,24},{1,33},{17,25},{2,34},{18,26},{3,35},{19,27},{4,36}... | collective-permute-start | bytes 1572872 | tf_op jit(solution)/shard_map/ppermute | solution.py:67
  68.9 23.9 %collective-permute-start.21 = (bf16[8,24,128,128]{3,2,1,0:T(8,128)(2,1)}, bf16[8,24,128,128]{3,2,1,0:T(8,128)(2,1)}, u32[]{:S(2)}, u32[]{:S(2)}) collective-permute-start(bf16[8,24,128,128]{3,2,1,0:T(8,128)(2,1)} %pick_tiles.1), channel_id=1, source_target_pairs={{0,16},{16,0},{1,17},{17,1},{2,18},{18,2},{3,19},{19,3},{4,20},{20... | collective-permute-start | bytes 18874376 | tf_op jit(solution)/shard_map/ppermute | solution.py:67
  69.1 23.7 %collective-permute-start.17 = (bf16[2,8,128,256]{3,2,1,0:T(8,128)(2,1)S(1)}, bf16[2,8,128,256]{3,2,1,0:T(8,128)(2,1)}, u32[]{:S(2)}, u32[]{:S(2)}) collective-permute-start(bf16[2,8,128,256]{3,2,1,0:T(8,128)(2,1)S(1)} %pad_maximum_fusion.1), channel_id=1, source_target_pairs={{0,8},{16,48},{1,9},{17,49},{2,10},{18,50},{3,11},{19,51},{4,12},{... | collective-permute-start | bytes 3145736 | tf_op jit(solution)/shard_map/ppermute | solution.py:67
  69.2 23.6 %collective-permute-start.18 = (bf16[2,8,128,256]{3,2,1,0:T(8,128)(2,1)S(1)}, bf16[2,8,128,256]{3,2,1,0:T(8,128)(2,1)}, u32[]{:S(2)}, u32[]{:S(2)}) collective-permute-start(bf16[2,8,128,256]{3,2,1,0:T(8,128)(2,1)S(1)} %pad_maximum_fusion.1), channel_id=1, source_target_pairs={{0,136},{16,112},{1,137},{17,113},{2,138},{18,114},{3,139},{19,115... | collective-permute-start | bytes 3145736 | tf_op jit(solution)/shard_map/ppermute | solution.py:67
  72.4 18.2 %collective-permute-start.19 = (bf16[22,64,256]{2,1,0:T(8,128)(2,1)}, bf16[22,64,256]{2,1,0:T(8,128)(2,1)S(1)}, u32[]{:S(2)}, u32[]{:S(2)}) collective-permute-start(bf16[22,64,256]{2,1,0:T(8,128)(2,1)} %collective-permute-done.15.refs_22_.refs_6_), channel_id=1, source_target_pairs={{0,1},{16,17},{1,2},{17,18},{2,3},{18,19},{3,4},{19,20},{4,5},{20,... | collective-permute-start | bytes 2162696 | tf_op jit(solution)/shard_map/ppermute | solution.py:67
  74.5 18.3 %collective-permute-start.20 = (bf16[22,64,256]{2,1,0:T(8,128)(2,1)}, bf16[22,64,256]{2,1,0:T(8,128)(2,1)S(1)}, u32[]{:S(2)}, u32[]{:S(2)}) collective-permute-start(bf16[22,64,256]{2,1,0:T(8,128)(2,1)} %collective-permute-done.16.refs_17_.refs_2_), channel_id=1, source_target_pairs={{0,7},{16,23},{1,0},{17,16},{2,1},{18,17},{3,2},{19,18},{4,3},{20,... | collective-permute-start | bytes 2162696 | tf_op jit(solution)/shard_map/ppermute | solution.py:67
  90.6 6.7 %collective-permute-start = (s32[8,24]{1,0:T(8,128)S(1)}, s32[8,24]{1,0:T(8,128)S(1)}, u32[]{:S(2)}, u32[]{:S(2)}) collective-permute-start(s32[8,24]{1,0:T(8,128)S(1)} %bitcast.63), channel_id=1, source_target_pairs={{0,16},{16,0},{1,17},{17,1},{2,18},{18,2},{3,19},{19,3},{4,20},{20... | collective-permute-start | bytes 2312 | tf_op jit(solution)/shard_map/ppermute | solution.py:67
  92.8 16.3 %collective-permute-start.22 = (bf16[2,8,128,256]{3,2,1,0:T(8,128)(2,1)}, bf16[2,8,128,256]{3,2,1,0:T(8,128)(2,1)}, u32[]{:S(2)}, u32[]{:S(2)}) collective-permute-start(bf16[2,8,128,256]{3,2,1,0:T(8,128)(2,1)} %copy-done.12), channel_id=1, source_target_pairs={{0,8},{16,48},{1,9},{17,49},{2,10},{18,50},{3,11},{19,51},{4,12},{... | collective-permute-start | bytes 3145736 | tf_op jit(solution)/shard_map/ppermute | solution.py:67
  92.8 16.3 %collective-permute-start.23 = (bf16[2,8,128,256]{3,2,1,0:T(8,128)(2,1)}, bf16[2,8,128,256]{3,2,1,0:T(8,128)(2,1)}, u32[]{:S(2)}, u32[]{:S(2)}) collective-permute-start(bf16[2,8,128,256]{3,2,1,0:T(8,128)(2,1)} %collective-permute-done.18), channel_id=1, source_target_pairs={{0,136},{16,112},{1,137},{17,113},{2,138},{18,114},{3,139},{19,115... | collective-permute-start | bytes 3145736 | tf_op jit(solution)/shard_map/ppermute | solution.py:67
  98.2 10.9 %collective-permute-start.24 = (bf16[11,64,256]{2,1,0:T(8,128)(2,1)S(1)}, bf16[11,64,256]{2,1,0:T(8,128)(2,1)S(1)}, u32[]{:S(2)}, u32[]{:S(2)}) collective-permute-start(bf16[11,64,256]{2,1,0:T(8,128)(2,1)S(1)} %slice.6), channel_id=1, source_target_pairs={{0,1},{16,17},{1,2},{17,18},{2,3},{18,19},{3,4},{19,20},{4,5},{20,... | collective-permute-start | bytes 1081352 | tf_op jit(solution)/shard_map/ppermute | solution.py:67
  100.0 9.1 %collective-permute-start.25 = (bf16[11,64,256]{2,1,0:T(8,128)(2,1)S(1)}, bf16[11,64,256]{2,1,0:T(8,128)(2,1)S(1)}, u32[]{:S(2)}, u32[]{:S(2)}) collective-permute-start(bf16[11,64,256]{2,1,0:T(8,128)(2,1)S(1)} %slice.7), channel_id=1, source_target_pairs={{0,7},{16,23},{1,0},{17,16},{2,1},{18,17},{3,2},{19,18},{4,3},{20,... | collective-permute-start | bytes 1081352 | tf_op jit(solution)/shard_map/ppermute | solution.py:67
  134.9 22.5 %collective-permute-start.27 = (bf16[8,192,256]{2,1,0:T(8,128)(2,1)S(1)}, bf16[8,192,256]{2,1,0:T(8,128)(2,1)S(1)}, u32[]{:S(2)}, u32[]{:S(2)}) collective-permute-start(bf16[8,192,256]{2,1,0:T(8,128)(2,1)S(1)} %dynamic-slice_bitcast_fusion), channel_id=1, source_target_pairs={{0,8},{16,24},{1,9},{17,25},{2,10},{18,26},{3,11},{19,27},{4,12},{... | collective-permute-start | bytes 2359304 | tf_op jit(solution)/shard_map/ppermute | solution.py:67
  138.2 19.2 %all-to-all-start.1 = ((f32[16,16,256]{2,1,0:T(8,128)}), f32[16,16,256]{2,1,0:T(8,128)S(1)}, u32[]{:S(2)}, u32[]{:S(2)}) async-start(f32[16,16,256]{2,1,0:T(8,128)} %bitcast.30), calls=%async_computation.1 | async-start | bytes 524288 | tf_op jit(solution)/shard_map/all_to_all | solution.py:352
  158.6 27.8 %all-to-all-start.2 = ((bf16[8,192,256]{2,1,0:T(8,128)(2,1)}), bf16[8,192,256]{2,1,0:T(8,128)(2,1)S(1)}, u32[]{:S(2)}, u32[]{:S(2)}) async-start(bf16[8,192,256]{2,1,0:T(8,128)(2,1)} %fusion), calls=%async_computation.2 | async-start | bytes 1572864 | tf_op jit(solution)/shard_map/all_to_all | solution.py:355
  166.4 5.2 %collective-permute-start.29 = (f32[16,256]{1,0:T(8,128)S(1)}, f32[16,256]{1,0:T(8,128)S(1)}, u32[]{:S(2)}, u32[]{:S(2)}) collective-permute-start(f32[16,256]{1,0:T(8,128)S(1)} %add.256), channel_id=1, source_target_pairs={{0,128},{16,144},{1,129},{17,145},{2,130},{18,146},{3,131},{19,147... | collective-permute-start | bytes 49160 | tf_op jit(solution)/shard_map/ppermute | solution.py:67
  187.1 15.4 %all-to-all-start.3 = ((f32[16,16,256]{2,1,0:T(8,128)}), f32[16,16,256]{2,1,0:T(8,128)S(1)}, u32[]{:S(2)}, u32[]{:S(2)}) async-start(f32[16,16,256]{2,1,0:T(8,128)} %bitcast.32), calls=%async_computation.3 | async-start | bytes 524288 | tf_op jit(solution)/shard_map/all_to_all | solution.py:360
  (23 other events, 438.8 us)
